TPU v7x, 32 devices: a whole 2x2x4 slice. The times are simulated.
32 devices in a mesh: wide: 16 (over z, x, core), narrow: 2 (over y).
Axes of the slice: x: 2, y: 2, z: 4, core: 2. Of those that a mesh axis runs over, the one named last changes fastest.
Arguments:
- tokens: bfloat16 [2, 32, 320, 1024], P(None, ('wide', 'narrow')), may hold values from -6 to 6
- cotangent: bfloat16 [2, 32, 320, 1024], P(None, ('wide', 'narrow')), may hold values from -6 to 6
- cond: bfloat16 [8, 1024], replicated, may hold values from -6 to 6
- clip_frames: int32 [8], replicated, may hold values from 2 to 9, as said below
- window_clip: int32 [2, 32], P(None, ('wide', 'narrow')), may hold values from 0 to 7
- window_half: int32 [2, 32], P(None, ('wide', 'narrow')), may hold values from 0 to 1
- ada_weight: bfloat16 [1024, 6144], P('narrow', 'wide'), may hold values from -0.1875 to 0.1875
- qkv_weight: bfloat16 [1024, 3072], P('narrow', 'wide'), may hold values from -0.1875 to 0.1875
- out_weight: bfloat16 [1024, 1024], P('narrow', 'wide'), may hold values from -1 to 1
- up_weight: bfloat16 [1024, 4096], P('narrow', 'wide'), may hold values from -0.1875 to 0.1875
- down_weight: bfloat16 [4096, 1024], P('narrow', 'wide'), may hold values from -0.09375 to 0.09375
- offset_table: bfloat16 [16, 39], replicated, may hold values from -3 to 3
Outputs:
- mixed: bfloat16 [2, 32, 320, 1024], P(None, ('wide', 'narrow'))
- grad_tokens: float32 [2, 32, 320, 1024], P(None, ('wide', 'narrow'))
- grad_ada: float32 [1024, 6144], P('narrow', 'wide')
- grad_qkv: float32 [1024, 3072], P('narrow', 'wide')
- grad_out: float32 [1024, 1024], P('narrow', 'wide')
- grad_up: float32 [1024, 4096], P('narrow', 'wide')
- grad_down: float32 [4096, 1024], P('narrow', 'wide')
- grad_table: float32 [16, 39], replicated
Inputs may be any that keep to these rules, and one draw needn't show every extreme that they name: `clip_frames`: latent frames of each clip; short clips are the most common, each longer count about half as frequent as the one below it, and some clip has the most. `window_clip`: a clip number.
All inputs are finite; a program needn't handle non-finite values.
Results may differ from a plain program's by a relative error of at most 0.017.
Values may be sent and summed in bfloat16 or wider, within the bound.
A program may use at most 256 MiB of HBM per device.

v0:
```python
import math

import jax
import jax.numpy as jnp
from jax import lax
from jax.sharding import PartitionSpec as P

HEADS = 16
WIN_FRAMES = 5
WIN_SIDE = 8


epsilon = 1e-06
masked_score = -1e30
highest = lax.Precision.HIGHEST
inv_root_two = 0.7071067811865476
inv_root_tau = 0.3989422804014327


def normalize(values):
    centre = jnp.mean(values, -1, keepdims=True)
    shifted = values - centre
    inv_std = lax.rsqrt(jnp.mean(shifted * shifted, -1, keepdims=True) + epsilon)
    return (shifted * inv_std, inv_std)


def normalize_back(grad_norm, normed, inv_std):
    return inv_std * (
        grad_norm
        - jnp.mean(grad_norm, -1, keepdims=True)
        - normed * jnp.mean(grad_norm * normed, -1, keepdims=True)
    )


def offset_maps():
    frame_pos = jnp.arange(WIN_FRAMES)
    side_pos = jnp.arange(WIN_SIDE)
    frame_off = frame_pos[:, None] - frame_pos[None, :] + WIN_FRAMES - 1
    side_off = side_pos[:, None] - side_pos[None, :] + WIN_SIDE - 1
    frame_map = (frame_off[:, :, None] == jnp.arange(2 * WIN_FRAMES - 1)[None, None, :]).astype(
        jnp.float32
    )
    side_map = (side_off[:, :, None] == jnp.arange(2 * WIN_SIDE - 1)[None, None, :]).astype(
        jnp.float32
    )
    return (frame_map, side_map)


def build_bias(table):
    frame_map, side_map = offset_maps()
    frame_span = 2 * WIN_FRAMES - 1
    side_span = 2 * WIN_SIDE - 1
    along_frame = jnp.einsum("hk,ijk->hij", table[:, :frame_span], frame_map, precision=highest)
    along_row = jnp.einsum(
        "hk,ijk->hij", table[:, frame_span : frame_span + side_span], side_map, precision=highest
    )
    along_col = jnp.einsum(
        "hk,ijk->hij", table[:, frame_span + side_span :], side_map, precision=highest
    )
    full_grid = (
        along_frame[:, :, None, None, :, None, None]
        + along_row[:, None, :, None, None, :, None]
        + along_col[:, None, None, :, None, None, :]
    )
    win_tokens = WIN_FRAMES * WIN_SIDE * WIN_SIDE
    return full_grid.reshape(table.shape[0], win_tokens, win_tokens)


def table_grad(grad_bias):
    frame_map, side_map = offset_maps()
    grid_vals = grad_bias.reshape(
        grad_bias.shape[0], WIN_FRAMES, WIN_SIDE, WIN_SIDE, WIN_FRAMES, WIN_SIDE, WIN_SIDE
    )
    by_frame = jnp.sum(grid_vals, axis=(2, 3, 5, 6))
    by_row = jnp.sum(grid_vals, axis=(1, 3, 4, 6))
    by_col = jnp.sum(grid_vals, axis=(1, 2, 4, 5))
    return jnp.concatenate(
        [
            jnp.einsum("hij,ijk->hk", by_frame, frame_map, precision=highest),
            jnp.einsum("hij,ijk->hk", by_row, side_map, precision=highest),
            jnp.einsum("hij,ijk->hk", by_col, side_map, precision=highest),
        ],
        axis=1,
    )


def live_keys(window_ids, window_halves, clip_frames):
    clip_hits = window_ids[:, None] == jnp.arange(clip_frames.shape[0])[None, :]
    frames_of = jnp.sum(jnp.where(clip_hits, clip_frames[None, :], 0), axis=1)
    live = jnp.clip(frames_of - WIN_FRAMES * window_halves, 1, WIN_FRAMES)
    frame_of_pos = jnp.arange(WIN_FRAMES * WIN_SIDE * WIN_SIDE) // (WIN_SIDE * WIN_SIDE)
    return frame_of_pos[None, :] < live[:, None]


def gelu_slope(pre_act):
    return 0.5 * (1.0 + lax.erf(pre_act * inv_root_two)) + pre_act * inv_root_tau * jnp.exp(
        -0.5 * pre_act * pre_act
    )


def window_scores(queries, keys_in, bias, valid):
    scale_factor = 1.0 / math.sqrt(queries.shape[-1])
    raw_scores = (
        jnp.einsum("wihe,wjhe->whij", queries, keys_in, preferred_element_type=jnp.float32)
        * scale_factor
    )
    return jnp.where(valid[:, None, None, :], raw_scores + bias[None], masked_score)


def gather_weights(ada_part, qkv_part, out_part, up_part, down_part):
    col_full = (
        lax.all_gather(ada_part, "wide", axis=1, tiled=True),
        lax.all_gather(qkv_part, "wide", axis=1, tiled=True),
        lax.all_gather(out_part, "wide", axis=1, tiled=True),
        lax.all_gather(up_part, "wide", axis=1, tiled=True),
        lax.all_gather(down_part, "wide", axis=1, tiled=True),
    )
    return (
        lax.all_gather(col_full[0], "narrow", axis=0, tiled=True),
        lax.all_gather(col_full[1], "narrow", axis=0, tiled=True),
        lax.all_gather(col_full[2], "narrow", axis=0, tiled=True),
        lax.all_gather(col_full[3], "narrow", axis=0, tiled=True),
        lax.all_gather(col_full[4], "narrow", axis=0, tiled=True),
    )


def scatter_grads(grad_set):
    row_owned = (
        lax.psum_scatter(
            grad_set[0].astype(jnp.bfloat16), "narrow", scatter_dimension=0, tiled=True
        ).astype(jnp.float32),
        lax.psum_scatter(
            grad_set[1].astype(jnp.bfloat16), "narrow", scatter_dimension=0, tiled=True
        ).astype(jnp.float32),
        lax.psum_scatter(
            grad_set[2].astype(jnp.bfloat16), "narrow", scatter_dimension=0, tiled=True
        ).astype(jnp.float32),
        lax.psum_scatter(
            grad_set[3].astype(jnp.bfloat16), "narrow", scatter_dimension=0, tiled=True
        ).astype(jnp.float32),
        lax.psum_scatter(
            grad_set[4].astype(jnp.bfloat16), "narrow", scatter_dimension=0, tiled=True
        ).astype(jnp.float32),
    )
    return (
        lax.psum_scatter(
            row_owned[0].astype(jnp.bfloat16), "wide", scatter_dimension=1, tiled=True
        ).astype(jnp.float32),
        lax.psum_scatter(
            row_owned[1].astype(jnp.bfloat16), "wide", scatter_dimension=1, tiled=True
        ).astype(jnp.float32),
        lax.psum_scatter(
            row_owned[2].astype(jnp.bfloat16), "wide", scatter_dimension=1, tiled=True
        ).astype(jnp.float32),
        lax.psum_scatter(
            row_owned[3].astype(jnp.bfloat16), "wide", scatter_dimension=1, tiled=True
        ).astype(jnp.float32),
        lax.psum_scatter(
            row_owned[4].astype(jnp.bfloat16), "wide", scatter_dimension=1, tiled=True
        ).astype(jnp.float32),
    )


def forward_pass(inputs, cond_rows, valid, weights, bias):
    ada_full, qkv_full, out_full, up_full, down_full = weights
    win_count, win_tokens, width = inputs.shape
    cond_act = jax.nn.silu(cond_rows.astype(jnp.float32)).astype(jnp.bfloat16)
    modulation = jnp.dot(cond_act, ada_full, preferred_element_type=jnp.float32).reshape(
        win_count, 6, 1, width
    )
    resid_in = inputs.astype(jnp.float32)
    normed_one, inv_one = normalize(resid_in)
    hidden_one = (normed_one * (1.0 + modulation[:, 1]) + modulation[:, 0]).astype(jnp.bfloat16)
    qkv_vals = jnp.einsum(
        "wtd,de->wte", hidden_one, qkv_full, preferred_element_type=jnp.float32
    ).astype(jnp.bfloat16)
    split_qkv = qkv_vals.reshape(win_count, win_tokens, 3, HEADS, width // HEADS)
    queries = split_qkv[:, :, 0]
    keys_in = split_qkv[:, :, 1]
    values_in = split_qkv[:, :, 2]
    scores = window_scores(queries, keys_in, bias, valid)
    row_peak = jnp.max(scores, -1, keepdims=True)
    exp_scores = jnp.exp(scores - row_peak)
    total_exp = jnp.sum(exp_scores, -1, keepdims=True)
    log_total = row_peak + jnp.log(total_exp)
    probs_low = (exp_scores / total_exp).astype(jnp.bfloat16)
    heads_out = jnp.einsum(
        "whij,wjhe->wihe", probs_low, values_in, preferred_element_type=jnp.float32
    )
    heads_low = heads_out.reshape(win_count, win_tokens, width).astype(jnp.bfloat16)
    attended = jnp.einsum("wtd,de->wte", heads_low, out_full, preferred_element_type=jnp.float32)
    resid_mid = resid_in + modulation[:, 2] * attended
    normed_two, inv_two = normalize(resid_mid)
    hidden_two = (normed_two * (1.0 + modulation[:, 4]) + modulation[:, 3]).astype(jnp.bfloat16)
    up_proj = jnp.einsum("wtd,df->wtf", hidden_two, up_full, preferred_element_type=jnp.float32)
    gelu_low = jax.nn.gelu(up_proj, approximate=False).astype(jnp.bfloat16)
    ffn_out = jnp.einsum("wtf,fd->wtd", gelu_low, down_full, preferred_element_type=jnp.float32)
    result = (resid_mid + modulation[:, 5] * ffn_out).astype(jnp.bfloat16)
    saved_vals = (
        cond_act,
        modulation,
        normed_one,
        inv_one,
        hidden_one,
        queries,
        keys_in,
        values_in,
        log_total,
        heads_low,
        attended,
        normed_two,
        inv_two,
        hidden_two,
        up_proj,
        gelu_low,
        ffn_out,
    )
    return (result, saved_vals)


def backward_pass(grad_out, saved_vals, weights, bias, valid):
    (
        cond_act,
        modulation,
        normed_one,
        inv_one,
        hidden_one,
        queries,
        keys_in,
        values_in,
        log_total,
        heads_low,
        attended,
        normed_two,
        inv_two,
        hidden_two,
        up_proj,
        gelu_low,
        ffn_out,
    ) = saved_vals
    ada_full, qkv_full, out_full, up_full, down_full = weights
    win_count, win_tokens, width = grad_out.shape
    grad_res = grad_out.astype(jnp.float32)
    grad_gate_two = jnp.sum(grad_res * ffn_out, 1)
    grad_ffn = (modulation[:, 5] * grad_res).astype(jnp.bfloat16)
    grad_downw = jnp.einsum("wtf,wtd->fd", gelu_low, grad_ffn, preferred_element_type=jnp.float32)
    grad_gelu = jnp.einsum("wtd,fd->wtf", grad_ffn, down_full, preferred_element_type=jnp.float32)
    grad_pre = (grad_gelu * gelu_slope(up_proj)).astype(jnp.bfloat16)
    grad_upw = jnp.einsum("wtd,wtf->df", hidden_two, grad_pre, preferred_element_type=jnp.float32)
    grad_hidden_two = jnp.einsum(
        "wtf,df->wtd", grad_pre, up_full, preferred_element_type=jnp.float32
    )
    grad_shift_two = jnp.sum(grad_hidden_two, 1)
    grad_scale_two = jnp.sum(grad_hidden_two * normed_two, 1)
    grad_mid = grad_res + normalize_back(
        grad_hidden_two * (1.0 + modulation[:, 4]), normed_two, inv_two
    )
    grad_gate_one = jnp.sum(grad_mid * attended, 1)
    grad_att = (modulation[:, 2] * grad_mid).astype(jnp.bfloat16)
    grad_outw = jnp.einsum("wtd,wte->de", heads_low, grad_att, preferred_element_type=jnp.float32)
    grad_heads = jnp.einsum(
        "wte,de->wtd", grad_att, out_full, preferred_element_type=jnp.float32
    ).astype(jnp.bfloat16)
    grad_heads = grad_heads.reshape(win_count, win_tokens, HEADS, width // HEADS)
    scores = window_scores(queries, keys_in, bias, valid)
    probs = jnp.exp(scores - log_total)
    probs_low = probs.astype(jnp.bfloat16)
    grad_values = jnp.einsum(
        "whij,wihe->wjhe", probs_low, grad_heads, preferred_element_type=jnp.float32
    )
    grad_probs = jnp.einsum(
        "wihe,wjhe->whij", grad_heads, values_in, preferred_element_type=jnp.float32
    )
    grad_scores = probs * (grad_probs - jnp.sum(probs * grad_probs, -1, keepdims=True))
    grad_bias = jnp.sum(grad_scores, 0)
    scores_low = grad_scores.astype(jnp.bfloat16)
    scale_factor = 1.0 / math.sqrt(queries.shape[-1])
    grad_queries = (
        jnp.einsum("whij,wjhe->wihe", scores_low, keys_in, preferred_element_type=jnp.float32)
        * scale_factor
    )
    grad_keys = (
        jnp.einsum("whij,wihe->wjhe", scores_low, queries, preferred_element_type=jnp.float32)
        * scale_factor
    )
    grad_qkv = (
        jnp.stack([grad_queries, grad_keys, grad_values], 2)
        .reshape(win_count, win_tokens, 3 * width)
        .astype(jnp.bfloat16)
    )
    grad_qkvw = jnp.einsum("wtd,wte->de", hidden_one, grad_qkv, preferred_element_type=jnp.float32)
    grad_hidden_one = jnp.einsum(
        "wte,de->wtd", grad_qkv, qkv_full, preferred_element_type=jnp.float32
    )
    grad_shift_one = jnp.sum(grad_hidden_one, 1)
    grad_scale_one = jnp.sum(grad_hidden_one * normed_one, 1)
    grad_input = grad_mid + normalize_back(
        grad_hidden_one * (1.0 + modulation[:, 1]), normed_one, inv_one
    )
    grad_mod = jnp.stack(
        [
            grad_shift_one,
            grad_scale_one,
            grad_gate_one,
            grad_shift_two,
            grad_scale_two,
            grad_gate_two,
        ],
        1,
    )
    grad_mod = grad_mod.reshape(win_count, 6 * width).astype(jnp.bfloat16)
    grad_adaw = jnp.einsum("wc,we->ce", cond_act, grad_mod, preferred_element_type=jnp.float32)
    return (grad_input, (grad_adaw, grad_qkvw, grad_outw, grad_upw, grad_downw), grad_bias)


def body(
    tokens,
    cotangent,
    cond,
    clip_frames,
    window_clip,
    window_half,
    ada_weight,
    qkv_weight,
    out_weight,
    up_weight,
    down_weight,
    offset_table,
):
    table = offset_table.astype(jnp.float32)
    bias = build_bias(table)
    results = []
    input_grads = []
    shard_sums = None
    bias_total = None
    for micro_idx in range(tokens.shape[0]):
        window_ids = window_clip[micro_idx]
        valid = live_keys(window_ids, window_half[micro_idx], clip_frames)
        cond_rows = cond[window_ids]
        fwd_weights = gather_weights(ada_weight, qkv_weight, out_weight, up_weight, down_weight)
        result, saved_vals = forward_pass(tokens[micro_idx], cond_rows, valid, fwd_weights, bias)
        fenced, saved_vals = lax.optimization_barrier(
            ((ada_weight, qkv_weight, out_weight, up_weight, down_weight), saved_vals)
        )
        back_weights = gather_weights(fenced[0], fenced[1], fenced[2], fenced[3], fenced[4])
        grad_input, weight_grads, grad_bias = backward_pass(
            cotangent[micro_idx], saved_vals, back_weights, bias, valid
        )
        results.append(result)
        input_grads.append(grad_input)
        bias_total = grad_bias if micro_idx == 0 else bias_total + grad_bias
        reduced = scatter_grads(weight_grads)
        shard_sums = (
            reduced
            if micro_idx == 0
            else tuple((prior_val + new_val for prior_val, new_val in zip(shard_sums, reduced)))
        )
    grad_table = lax.psum(table_grad(bias_total), ("wide", "narrow"))
    mixed = jnp.stack(results, 0)
    grad_tokens = jnp.stack(input_grads, 0)
    return (
        mixed,
        grad_tokens,
        shard_sums[0],
        shard_sums[1],
        shard_sums[2],
        shard_sums[3],
        shard_sums[4],
        grad_table,
    )


def solution(mesh):
    placed = (
        P(None, ("wide", "narrow"), None, None),
        P(None, ("wide", "narrow"), None, None),
        P(),
        P(),
        P(None, ("wide", "narrow")),
        P(None, ("wide", "narrow")),
        P("narrow", "wide"),
        P("narrow", "wide"),
        P("narrow", "wide"),
        P("narrow", "wide"),
        P("narrow", "wide"),
        P(),
    )
    return jax.shard_map(
        body,
        mesh=mesh,
        in_specs=placed,
        out_specs=(
            P(None, ("wide", "narrow"), None, None),
            P(None, ("wide", "narrow"), None, None),
            P("narrow", "wide"),
            P("narrow", "wide"),
            P("narrow", "wide"),
            P("narrow", "wide"),
            P("narrow", "wide"),
            P(),
        ),
        check_vma=False,
    )
```

profile of v0, /device:TPU:0, one launch (start us, length us, event | category | flops | bytes accessed | tf_op | source)
XLA Modules:
  0.0 3461.6 jit_solution(14667892397251496808)
XLA Ops:
  11.8 63.6 %all-gather.27.cloned.1.call-done = bf16[512,6144]{0,1:T(8,128)(2,1)} async-done(((bf16[512,384]{0,1:T(8,128)(2,1)}), bf16[512,6144]{0,1:T(8,128)(2,1)}) %all-gather.27.cloned.1.call-update) | async-done | bytes 6291472 | tf_op jit(solution)/shard_map/all_gather | solution.py:112
  75.5 46.3 %all-gather.31.cloned.1.call-done = bf16[512,3072]{0,1:T(8,128)(2,1)} async-done(((bf16[512,192]{0,1:T(8,128)(2,1)}), bf16[512,3072]{0,1:T(8,128)(2,1)}) %all-gather.31.cloned.1.call-update) | async-done | bytes 3145744 | tf_op jit(solution)/shard_map/all_gather | solution.py:113
  121.8 38.9 %all-gather.35.cloned.1.call-done = bf16[512,1024]{0,1:T(8,128)(2,1)} async-done(((bf16[512,64]{0,1:T(8,128)(2,1)}), bf16[512,1024]{0,1:T(8,128)(2,1)}) %all-gather.35.cloned.1.call-update) | async-done | bytes 1048592 | tf_op jit(solution)/shard_map/all_gather | solution.py:114
  160.8 54.1 %all-gather.39.cloned.1.call-done = bf16[512,4096]{1,0:T(8,128)(2,1)} async-done(((bf16[512,256]{1,0:T(8,128)(2,1)}), bf16[512,4096]{1,0:T(8,128)(2,1)}) %all-gather.39.cloned.1.call-update) | async-done | bytes 4194320 | tf_op jit(solution)/shard_map/all_gather | solution.py:115
  219.0 17.2 broadcast_add_fusion
  236.3 34.8 %copy.67 = f32[16,320,320]{1,2,0:T(8,128)} copy(f32[16,320,320]{0,2,1:T(8,128)} %bitcast.500) | data formatting | bytes 13107200 | tf_op jit(solution)/shard_map/add | solution.py:61
  279.4 138.9 %all-gather.29.cloned.1.call-done = bf16[1024,6144]{0,1:T(8,128)(2,1)} async-done(((bf16[512,6144]{0,1:T(8,128)(2,1)}), bf16[1024,6144]{0,1:T(8,128)(2,1)}) %all-gather.29.cloned.1.call-update) | async-done | bytes 12582928 | tf_op jit(solution)/shard_map/all_gather | solution.py:119
  418.3 8.1 fusion.171
  430.9 69.4 %all-gather.33.cloned.1.call-done = bf16[1024,3072]{0,1:T(8,128)(2,1)} async-done(((bf16[512,3072]{0,1:T(8,128)(2,1)}), bf16[1024,3072]{0,1:T(8,128)(2,1)}) %all-gather.33.cloned.1.call-update) | async-done | bytes 6291472 | tf_op jit(solution)/shard_map/all_gather | solution.py:120
  526.6 8.4 all-gather.37.cloned.1.call-done
  555.2 85.4 %all-gather.41.cloned.1.call-done = bf16[1024,4096]{1,0:T(8,128)(2,1)} async-done(((bf16[512,4096]{1,0:T(8,128)(2,1)}), bf16[1024,4096]{1,0:T(8,128)(2,1)}) %all-gather.41.cloned.1.call-update) | async-done | bytes 8388624 | tf_op jit(solution)/shard_map/all_gather | solution.py:122
  640.5 18.8 fusion.11
  659.4 86.6 %all-gather.45.cloned.1.call-done = bf16[4096,1024]{0,1:T(8,128)(2,1)} async-done(((bf16[2048,1024]{0,1:T(8,128)(2,1)}), bf16[4096,1024]{0,1:T(8,128)(2,1)}) %all-gather.45.cloned.1.call-update) | async-done | bytes 8388624 | tf_op jit(solution)/shard_map/all_gather | solution.py:123
  758.5 18.4 fusion.8
  784.4 20.7 all-gather.63.cloned.1.call-done
  805.1 53.7 %all-gather.67.cloned.1.call-done = bf16[512,4096]{1,0:T(8,128)(2,1)} async-done(((bf16[512,256]{1,0:T(8,128)(2,1)}), bf16[512,4096]{1,0:T(8,128)(2,1)}) %all-gather.67.cloned.1.call-update) | async-done | bytes 4194320 | tf_op jit(solution)/shard_map/all_gather | solution.py:115
  858.9 50.9 %all-gather.47.cloned.1.call-done = bf16[2048,1024]{0,1:T(8,128)(2,1)} async-done(((bf16[2048,64]{0,1:T(8,128)(2,1)}), bf16[2048,1024]{0,1:T(8,128)(2,1)}) %all-gather.47.cloned.1.call-update) | async-done | bytes 4194320 | tf_op jit(solution)/shard_map/all_gather | solution.py:116
  909.8 53.7 %all-gather.51.cloned.1.call-done = bf16[512,4096]{1,0:T(8,128)(2,1)} async-done(((bf16[512,256]{1,0:T(8,128)(2,1)}), bf16[512,4096]{1,0:T(8,128)(2,1)}) %all-gather.51.cloned.1.call-update) | async-done | bytes 4194320 | tf_op jit(solution)/shard_map/all_gather | solution.py:115
  963.6 38.1 %all-gather.71.cloned.1.call-done = bf16[512,1024]{0,1:T(8,128)(2,1)} async-done(((bf16[512,64]{0,1:T(8,128)(2,1)}), bf16[512,1024]{0,1:T(8,128)(2,1)}) %all-gather.71.cloned.1.call-update) | async-done | bytes 1048592 | tf_op jit(solution)/shard_map/all_gather | solution.py:114
  1001.7 38.8 %all-gather.55.cloned.1.call-done = bf16[512,1024]{0,1:T(8,128)(2,1)} async-done(((bf16[512,64]{0,1:T(8,128)(2,1)}), bf16[512,1024]{0,1:T(8,128)(2,1)}) %all-gather.55.cloned.1.call-update) | async-done | bytes 1048592 | tf_op jit(solution)/shard_map/all_gather | solution.py:114
  1040.6 46.2 %all-gather.75.cloned.1.call-done = bf16[512,3072]{0,1:T(8,128)(2,1)} async-done(((bf16[512,192]{0,1:T(8,128)(2,1)}), bf16[512,3072]{0,1:T(8,128)(2,1)}) %all-gather.75.cloned.1.call-update) | async-done | bytes 3145744 | tf_op jit(solution)/shard_map/all_gather | solution.py:113
  1086.9 46.3 %all-gather.59.cloned.1.call-done = bf16[512,3072]{0,1:T(8,128)(2,1)} async-done(((bf16[512,192]{0,1:T(8,128)(2,1)}), bf16[512,3072]{0,1:T(8,128)(2,1)}) %all-gather.59.cloned.1.call-update) | async-done | bytes 3145744 | tf_op jit(solution)/shard_map/all_gather | solution.py:113
  1133.3 104.3 %all-gather.65.cloned.1.call-done = bf16[4096,1024]{0,1:T(8,128)(2,1)} async-done(((bf16[2048,1024]{0,1:T(8,128)(2,1)}), bf16[4096,1024]{0,1:T(8,128)(2,1)}) %all-gather.65.cloned.1.call-update) | async-done | bytes 8388624 | tf_op jit(solution)/shard_map/all_gather | solution.py:123
  1237.6 8.7 fusion.33
  1246.3 96.8 %all-gather.69.cloned.1.call-done = bf16[1024,4096]{1,0:T(8,128)(2,1)} async-done(((bf16[512,4096]{1,0:T(8,128)(2,1)}), bf16[1024,4096]{1,0:T(8,128)(2,1)}) %all-gather.69.cloned.1.call-update) | async-done | bytes 8388624 | tf_op jit(solution)/shard_map/all_gather | solution.py:122
  1343.1 6.5 fusion.85
  1353.9 94.8 %all-gather.49.cloned.1.call-done = bf16[4096,1024]{0,1:T(8,128)(2,1)} async-done(((bf16[2048,1024]{0,1:T(8,128)(2,1)}), bf16[4096,1024]{0,1:T(8,128)(2,1)}) %all-gather.49.cloned.1.call-update) | async-done | bytes 8388624 | tf_op jit(solution)/shard_map/all_gather | solution.py:123
  1448.7 8.4 fusion.32
  1457.1 97.2 %all-gather.53.cloned.1.call-done = bf16[1024,4096]{1,0:T(8,128)(2,1)} async-done(((bf16[512,4096]{1,0:T(8,128)(2,1)}), bf16[1024,4096]{1,0:T(8,128)(2,1)}) %all-gather.53.cloned.1.call-update) | async-done | bytes 8388624 | tf_op jit(solution)/shard_map/all_gather | solution.py:122
  1554.2 6.5 fusion.87
  1566.1 9.7 convolution_convert_fusion
  1575.9 9.7 convolution_convert_fusion.1
  1593.7 29.8 all-gather.57.cloned.1.call-done
  1649.3 17.6 fusion.40
  1700.7 8.4 convolution_convert_fusion.2
  1710.2 8.5 convolution_convert_fusion.3
  1719.4 7.0 fusion.86
  1727.8 7.5 multiply_convert_fusion
  1736.0 51.2 %all-gather.61.cloned.1.call-done = bf16[1024,3072]{0,1:T(8,128)(2,1)} async-done(((bf16[512,3072]{0,1:T(8,128)(2,1)}), bf16[1024,3072]{0,1:T(8,128)(2,1)}) %all-gather.61.cloned.1.call-update) | async-done | bytes 6291472 | tf_op jit(solution)/shard_map/all_gather | solution.py:120
  1794.2 7.5 multiply_convert_fusion.1
  1801.8 19.4 reduce-scatter.47.cloned.1.call-done
  1823.5 31.8 reduce-scatter.45.cloned.1.call-done
  1857.7 99.3 %reduce-scatter.59.cloned.1.call-done = bf16[2048,1024]{1,0:T(8,128)(2,1)} async-done(((bf16[4096,1024]{1,0:T(8,128)(2,1)}), bf16[2048,1024]{1,0:T(8,128)(2,1)}) %reduce-scatter.59.cloned.1.call-update) | async-done | bytes 4194320 | tf_op jit(solution)/shard_map/reduce_scatter | solution.py:141
  1963.6 94.9 %reduce-scatter.57.cloned.1.call-done = bf16[2048,1024]{1,0:T(8,128)(2,1)} async-done(((bf16[4096,1024]{1,0:T(8,128)(2,1)}), bf16[2048,1024]{1,0:T(8,128)(2,1)}) %reduce-scatter.57.cloned.1.call-update) | async-done | bytes 4194320 | tf_op jit(solution)/shard_map/reduce_scatter | solution.py:141
  2065.1 72.8 %reduce-scatter.43.cloned.1.call-done = bf16[512,3072]{1,0:T(8,128)(2,1)} async-done(((bf16[1024,3072]{1,0:T(8,128)(2,1)}), bf16[512,3072]{1,0:T(8,128)(2,1)}) %reduce-scatter.43.cloned.1.call-update) | async-done | bytes 3145744 | tf_op jit(solution)/shard_map/reduce_scatter | solution.py:132
  2142.6 74.8 %reduce-scatter.41.cloned.1.call-done = bf16[512,3072]{1,0:T(8,128)(2,1)} async-done(((bf16[1024,3072]{1,0:T(8,128)(2,1)}), bf16[512,3072]{1,0:T(8,128)(2,1)}) %reduce-scatter.41.cloned.1.call-update) | async-done | bytes 3145744 | tf_op jit(solution)/shard_map/reduce_scatter | solution.py:132
  2222.1 96.7 %reduce-scatter.53.cloned.1.call-done = bf16[512,4096]{1,0:T(8,128)(2,1)} async-done(((bf16[1024,4096]{1,0:T(8,128)(2,1)}), bf16[512,4096]{1,0:T(8,128)(2,1)}) %reduce-scatter.53.cloned.1.call-update) | async-done | bytes 4194320 | tf_op jit(solution)/shard_map/reduce_scatter | solution.py:138
  2318.9 101.6 %reduce-scatter.49.cloned.1.call-done = bf16[512,4096]{1,0:T(8,128)(2,1)} async-done(((bf16[1024,4096]{1,0:T(8,128)(2,1)}), bf16[512,4096]{1,0:T(8,128)(2,1)}) %reduce-scatter.49.cloned.1.call-update) | async-done | bytes 4194320 | tf_op jit(solution)/shard_map/reduce_scatter | solution.py:138
  2420.7 146.6 %reduce-scatter.39.cloned.1.call-done = bf16[512,6144]{1,0:T(8,128)(2,1)} async-done(((bf16[1024,6144]{1,0:T(8,128)(2,1)}), bf16[512,6144]{1,0:T(8,128)(2,1)}) %reduce-scatter.39.cloned.1.call-update) | async-done | bytes 6291472 | tf_op jit(solution)/shard_map/reduce_scatter | solution.py:129
  2567.3 8.7 copy.98
  2576.0 137.9 %reduce-scatter.37.cloned.1.call-done = bf16[512,6144]{1,0:T(8,128)(2,1)} async-done(((bf16[1024,6144]{1,0:T(8,128)(2,1)}), bf16[512,6144]{1,0:T(8,128)(2,1)}) %reduce-scatter.37.cloned.1.call-update) | async-done | bytes 6291472 | tf_op jit(solution)/shard_map/reduce_scatter | solution.py:129
  2713.9 8.7 copy.96
  2725.1 32.1 copy.82
  2757.2 17.0 fusion.194
  2774.9 39.4 %psum.7 = f32[16,39]{1,0:T(8,128)} all-reduce(f32[16,39]{1,0:T(8,128)S(1)} %pad_maximum_fusion.2), channel_id=1, replica_groups=mesh['wide'=16,'narrow'=2] {'wide','narrow'}, use_global_device_ids=true, to_apply=%region_59.60 | all-reduce | flops 624 | bytes 4992 | tf_op jit(solution)/shard_map/psum | solution.py:358
  2819.9 15.6 reduce-scatter.69.cloned.1.call-done
  2837.2 73.4 %reduce-scatter.75.cloned.1.call-done = bf16[64,2048]{1,0:T(8,128)(2,1)} async-done(((bf16[1024,2048]{1,0:T(8,128)(2,1)}), bf16[64,2048]{1,0:T(8,128)(2,1)}) %reduce-scatter.75.cloned.1.call-update) | async-done | bytes 262160
  2911.8 74.7 %reduce-scatter.73.cloned.1.call-done = bf16[64,2048]{1,0:T(8,128)(2,1)} async-done(((bf16[1024,2048]{1,0:T(8,128)(2,1)}), bf16[64,2048]{1,0:T(8,128)(2,1)}) %reduce-scatter.73.cloned.1.call-update) | async-done | bytes 262160
  2989.0 66.6 %reduce-scatter.67.cloned.1.call-done = bf16[192,512]{1,0:T(8,128)(2,1)} async-done(((bf16[3072,512]{1,0:T(8,128)(2,1)}), bf16[192,512]{1,0:T(8,128)(2,1)}) %reduce-scatter.67.cloned.1.call-update) | async-done | bytes 196624
  3056.7 68.1 %reduce-scatter.65.cloned.1.call-done = bf16[192,512]{1,0:T(8,128)(2,1)} async-done(((bf16[3072,512]{1,0:T(8,128)(2,1)}), bf16[192,512]{1,0:T(8,128)(2,1)}) %reduce-scatter.65.cloned.1.call-update) | async-done | bytes 196624
  3126.8 73.2 %reduce-scatter.55.cloned.1.call-done = bf16[512,256]{1,0:T(8,128)(2,1)} async-done(((bf16[512,4096]{1,0:T(8,128)(2,1)}), bf16[512,256]{1,0:T(8,128)(2,1)}) %reduce-scatter.55.cloned.1.call-update) | async-done | bytes 262160 | tf_op jit(solution)/shard_map/reduce_scatter | solution.py:155
  3200.0 75.8 %reduce-scatter.51.cloned.1.call-done = bf16[512,256]{1,0:T(8,128)(2,1)} async-done(((bf16[512,4096]{1,0:T(8,128)(2,1)}), bf16[512,256]{1,0:T(8,128)(2,1)}) %reduce-scatter.51.cloned.1.call-update) | async-done | bytes 262160 | tf_op jit(solution)/shard_map/reduce_scatter | solution.py:155
  3277.7 86.3 %reduce-scatter.63.cloned.1.call-done = bf16[384,512]{1,0:T(8,128)(2,1)} async-done(((bf16[6144,512]{1,0:T(8,128)(2,1)}), bf16[384,512]{1,0:T(8,128)(2,1)}) %reduce-scatter.63.cloned.1.call-update) | async-done | bytes 393232
  3365.2 87.5 %reduce-scatter.61.cloned.1.call-done = bf16[384,512]{1,0:T(8,128)(2,1)} async-done(((bf16[6144,512]{1,0:T(8,128)(2,1)}), bf16[384,512]{1,0:T(8,128)(2,1)}) %reduce-scatter.61.cloned.1.call-update) | async-done | bytes 393232
  (412 shorter events, 219.1 us)
Async XLA Ops:
  7.2 68.3 %all-gather.27.cloned.1.call-start = ((), (), s32[]{:S(2)}) async-start(), calls=%async_computation.20 | async-start | bytes 6684672 | tf_op jit(solution)/shard_map/all_gather | solution.py:112
  9.2 112.6 %all-gather.31.cloned.1.call-start = ((), (), s32[]{:S(2)}) async-start(), calls=%async_computation.22 | async-start | bytes 3342336 | tf_op jit(solution)/shard_map/all_gather | solution.py:113
  9.9 150.8 %all-gather.35.cloned.1.call-start = ((), (), s32[]{:S(2)}) async-start(), calls=%async_computation.24 | async-start | bytes 1114112 | tf_op jit(solution)/shard_map/all_gather | solution.py:114
  10.6 204.3 %all-gather.39.cloned.1.call-start = ((), (), s32[]{:S(2)}) async-start(), calls=%async_computation.26 | async-start | bytes 4456448 | tf_op jit(solution)/shard_map/all_gather | solution.py:115
  11.2 268.0 %all-gather.43.cloned.1.call-start = ((), (), s32[]{:S(2)}) async-start(), calls=%async_computation.28 | async-start | bytes 4456448 | tf_op jit(solution)/shard_map/all_gather | solution.py:116
  11.8 406.5 %all-gather.29.cloned.1.call-start = ((), (), s32[]{:S(2)}) async-start(), calls=%async_computation.21 | async-start | bytes 18874368 | tf_op jit(solution)/shard_map/all_gather | solution.py:119
  75.5 424.8 %all-gather.33.cloned.1.call-start = ((), (), s32[]{:S(2)}) async-start(), calls=%async_computation.23 | async-start | bytes 9437184 | tf_op jit(solution)/shard_map/all_gather | solution.py:120
  121.8 93.2 %copy-start.74 = (s32[2,1]{0,1:T(1,128)S(1)}, s32[2,1]{0,1:T(1,128)}, u32[]{:S(2)}) copy-start(s32[2,1]{0,1:T(1,128)} %param.16) | copy-start | bytes 28
  121.8 96.4 %copy-start.77 = (bf16[16,39]{1,0:T(8,128)(2,1)S(1)}, bf16[16,39]{1,0:T(8,128)(2,1)}, u32[]{:S(2)}) copy-start(bf16[16,39]{1,0:T(8,128)(2,1)} %param.23) | copy-start | bytes 3748
  121.8 413.2 %all-gather.37.cloned.1.call-start = ((), (), s32[]{:S(2)}) async-start(), calls=%async_computation.25 | async-start | bytes 3145728 | tf_op jit(solution)/shard_map/all_gather | solution.py:121
  160.7 479.8 %all-gather.41.cloned.1.call-start = ((), (), s32[]{:S(2)}) async-start(), calls=%async_computation.27 | async-start | bytes 12582912 | tf_op jit(solution)/shard_map/all_gather | solution.py:122
  214.9 531.1 %all-gather.45.cloned.1.call-start = ((), (), s32[]{:S(2)}) async-start(), calls=%async_computation.29 | async-start | bytes 12582912 | tf_op jit(solution)/shard_map/all_gather | solution.py:123
  236.3 34.9 %copy-start.75 = (s32[2,1]{0,1:T(1,128)S(1)}, s32[2,1]{0,1:T(1,128)}, u32[]{:S(2)}) copy-start(s32[2,1]{0,1:T(1,128)} %param.17) | copy-start | bytes 28
  236.3 36.8 %copy-start.76 = (s32[8]{0:T(128)S(1)}, s32[8]{0:T(128)}, u32[]{:S(2)}) copy-start(s32[8]{0:T(128)} %param.15) | copy-start | bytes 100
  236.3 40.0 %copy-start.7 = (bf16[2,1,320,1024]{3,2,1,0:T(8,128)(2,1)S(1)}, bf16[2,1,320,1024]{3,2,1,0:T(8,128)(2,1)}, u32[]{:S(2)}) copy-start(bf16[2,1,320,1024]{3,2,1,0:T(8,128)(2,1)} %param.12) | copy-start | bytes 3932164
  236.3 42.8 %copy-start.65 = (bf16[8,1024]{1,0:T(8,128)(2,1)S(1)}, bf16[8,1024]{1,0:T(8,128)(2,1)}, u32[]{:S(2)}) copy-start(bf16[8,1024]{1,0:T(8,128)(2,1)} %param.14) | copy-start | bytes 49156
  279.0 230.8 %copy-start.72 = (pred[320]{0:T(512)(128)(4,1)}, pred[320]{0:T(512)(128)(4,1)S(1)}, u32[]{:S(2)}) copy-start(pred[320]{0:T(512)(128)(4,1)S(1)} %fusion.185) | copy-start | bytes 964
  279.1 258.7 %copy-start.70 = (pred[320]{0:T(512)(128)(4,1)}, pred[320]{0:T(512)(128)(4,1)S(1)}, u32[]{:S(2)}) copy-start(pred[320]{0:T(512)(128)(4,1)S(1)} %fusion.186) | copy-start | bytes 964
  279.1 147.3 %copy-start.61 = (bf16[1,1024]{1,0:T(2,128)(2,1)}, bf16[1,1024]{1,0:T(2,128)(2,1)S(1)}, u32[]{:S(2)}) copy-start(bf16[1,1024]{1,0:T(2,128)(2,1)S(1)} %get-tuple-element.81) | copy-start | bytes 6148
  279.1 147.3 %copy-start.59 = (bf16[1,1024]{1,0:T(2,128)(2,1)}, bf16[1,1024]{1,0:T(2,128)(2,1)S(1)}, u32[]{:S(2)}) copy-start(bf16[1,1024]{1,0:T(2,128)(2,1)S(1)} %get-tuple-element.78) | copy-start | bytes 6148
  279.2 525.8 %all-gather.63.cloned.1.call-start = ((), (), s32[]{:S(2)}) async-start(), calls=%async_computation.38 | async-start | bytes 4456448 | tf_op jit(solution)/shard_map/all_gather | solution.py:116
  754.2 104.6 %all-gather.67.cloned.1.call-start = ((), (), s32[]{:S(2)}) async-start(), calls=%async_computation.40 | async-start | bytes 4456448 | tf_op jit(solution)/shard_map/all_gather | solution.py:115
  754.7 155.0 %all-gather.47.cloned.1.call-start = ((), (), s32[]{:S(2)}) async-start(), calls=%async_computation.30 | async-start | bytes 4456448 | tf_op jit(solution)/shard_map/all_gather | solution.py:116
  781.4 772.8 %copy-start.35 = (f32[1,320,1024]{2,1,0:T(8,128)}, f32[1,320,1024]{2,1,0:T(8,128)S(1)}, u32[]{:S(2)}) copy-start(f32[1,320,1024]{2,1,0:T(8,128)S(1)} %get-tuple-element.55) | copy-start | bytes 3932164
  781.4 182.1 %all-gather.51.cloned.1.call-start = ((), (), s32[]{:S(2)}) async-start(), calls=%async_computation.32 | async-start | bytes 4456448 | tf_op jit(solution)/shard_map/all_gather | solution.py:115
  782.0 219.6 %all-gather.71.cloned.1.call-start = ((), (), s32[]{:S(2)}) async-start(), calls=%async_computation.42 | async-start | bytes 1114112 | tf_op jit(solution)/shard_map/all_gather | solution.py:114
  782.6 258.0 %all-gather.55.cloned.1.call-start = ((), (), s32[]{:S(2)}) async-start(), calls=%async_computation.34 | async-start | bytes 1114112 | tf_op jit(solution)/shard_map/all_gather | solution.py:114
  783.2 303.7 %all-gather.75.cloned.1.call-start = ((), (), s32[]{:S(2)}) async-start(), calls=%async_computation.44 | async-start | bytes 3342336 | tf_op jit(solution)/shard_map/all_gather | solution.py:113
  783.7 349.5 %all-gather.59.cloned.1.call-start = ((), (), s32[]{:S(2)}) async-start(), calls=%async_computation.36 | async-start | bytes 3342336 | tf_op jit(solution)/shard_map/all_gather | solution.py:113
  784.3 453.3 %all-gather.65.cloned.1.call-start = ((), (), s32[]{:S(2)}) async-start(), calls=%async_computation.39 | async-start | bytes 12582912 | tf_op jit(solution)/shard_map/all_gather | solution.py:123
  805.1 538.0 %all-gather.69.cloned.1.call-start = ((), (), s32[]{:S(2)}) async-start(), calls=%async_computation.41 | async-start | bytes 12582912 | tf_op jit(solution)/shard_map/all_gather | solution.py:122
  858.8 589.9 %all-gather.49.cloned.1.call-start = ((), (), s32[]{:S(2)}) async-start(), calls=%async_computation.31 | async-start | bytes 12582912 | tf_op jit(solution)/shard_map/all_gather | solution.py:123
  909.8 644.5 %all-gather.53.cloned.1.call-start = ((), (), s32[]{:S(2)}) async-start(), calls=%async_computation.33 | async-start | bytes 12582912 | tf_op jit(solution)/shard_map/all_gather | solution.py:122
  963.5 625.4 %all-gather.73.cloned.1.call-start = ((), (), s32[]{:S(2)}) async-start(), calls=%async_computation.43 | async-start | bytes 3145728 | tf_op jit(solution)/shard_map/all_gather | solution.py:121
  1001.7 131.6 %copy-start.57 = (f32[1,6,1024]{2,1,0:T(8,128)S(1)}, f32[1,6,1024]{2,1,0:T(8,128)}, u32[]{:S(2)}) copy-start(f32[1,6,1024]{2,1,0:T(8,128)} %copy-done.56) | copy-start | bytes 73732
  1001.7 621.8 %all-gather.57.cloned.1.call-start = ((), (), s32[]{:S(2)}) async-start(), calls=%async_computation.35 | async-start | bytes 3145728 | tf_op jit(solution)/shard_map/all_gather | solution.py:121
  1040.6 678.8 %all-gather.77.cloned.1.call-start = ((), (), s32[]{:S(2)}) async-start(), calls=%async_computation.45 | async-start | bytes 9437184 | tf_op jit(solution)/shard_map/all_gather | solution.py:120
  1086.8 700.4 %all-gather.61.cloned.1.call-start = ((), (), s32[]{:S(2)}) async-start(), calls=%async_computation.37 | async-start | bytes 9437184 | tf_op jit(solution)/shard_map/all_gather | solution.py:120
  1133.2 687.9 %reduce-scatter.47.cloned.1.call-start = ((), (), s32[]{:S(2)}) async-start(), calls=%async_computation.51 | async-start | bytes 3145728 | tf_op jit(solution)/shard_map/reduce_scatter | solution.py:135
  1237.6 105.4 %copy-start.38 = (f32[1,320,1024]{2,1,0:T(8,128)S(1)}, f32[1,320,1024]{2,1,0:T(8,128)}, u32[]{:S(2)}) copy-start(f32[1,320,1024]{2,1,0:T(8,128)} %get-tuple-element.69) | copy-start | bytes 3932164
  1350.7 238.2 %copy-start.19 = (f32[1,320,1024]{2,1,0:T(8,128)}, f32[1,320,1024]{2,1,0:T(8,128)S(1)}, u32[]{:S(2)}) copy-start(f32[1,320,1024]{2,1,0:T(8,128)S(1)} %get-tuple-element.191) | copy-start | bytes 3932164
  1353.8 501.6 %reduce-scatter.45.cloned.1.call-start = ((), (), s32[]{:S(2)}) async-start(), calls=%async_computation.50 | async-start | bytes 3145728 | tf_op jit(solution)/shard_map/reduce_scatter | solution.py:135
  1562.9 60.5 %copy-start.20 = (f32[1,320,1024]{2,1,0:T(8,128)}, f32[1,320,1024]{2,1,0:T(8,128)S(1)}, u32[]{:S(2)}) copy-start(f32[1,320,1024]{2,1,0:T(8,128)S(1)} %get-tuple-element.166) | copy-start | bytes 3932164
  1565.6 391.4 %reduce-scatter.59.cloned.1.call-start = ((), (), s32[]{:S(2)}) async-start(), calls=%async_computation.57 | async-start | bytes 12582912 | tf_op jit(solution)/shard_map/reduce_scatter | solution.py:141
  1575.8 482.7 %reduce-scatter.57.cloned.1.call-start = ((), (), s32[]{:S(2)}) async-start(), calls=%async_computation.56 | async-start | bytes 12582912 | tf_op jit(solution)/shard_map/reduce_scatter | solution.py:141
  1585.6 552.3 %reduce-scatter.43.cloned.1.call-start = ((), (), s32[]{:S(2)}) async-start(), calls=%async_computation.49 | async-start | bytes 9437184 | tf_op jit(solution)/shard_map/reduce_scatter | solution.py:132
  1593.7 34.6 copy-start.30
  1682.2 535.1 %reduce-scatter.41.cloned.1.call-start = ((), (), s32[]{:S(2)}) async-start(), calls=%async_computation.48 | async-start | bytes 9437184 | tf_op jit(solution)/shard_map/reduce_scatter | solution.py:132
  1699.6 619.2 %reduce-scatter.53.cloned.1.call-start = ((), (), s32[]{:S(2)}) async-start(), calls=%async_computation.54 | async-start | bytes 12582912 | tf_op jit(solution)/shard_map/reduce_scatter | solution.py:138
  1709.1 711.3 %reduce-scatter.49.cloned.1.call-start = ((), (), s32[]{:S(2)}) async-start(), calls=%async_computation.52 | async-start | bytes 12582912 | tf_op jit(solution)/shard_map/reduce_scatter | solution.py:138
  1718.7 848.6 %reduce-scatter.39.cloned.1.call-start = ((), (), s32[]{:S(2)}) async-start(), calls=%async_computation.47 | async-start | bytes 18874368 | tf_op jit(solution)/shard_map/reduce_scatter | solution.py:129
  1735.4 978.5 %reduce-scatter.37.cloned.1.call-start = ((), (), s32[]{:S(2)}) async-start(), calls=%async_computation.46 | async-start | bytes 18874368 | tf_op jit(solution)/shard_map/reduce_scatter | solution.py:129
  1801.8 1017.1 %reduce-scatter.71.cloned.1.call-start = ((), (), s32[]{:S(2)}) async-start(), calls=%async_computation.63 | async-start | bytes 1114112
  1823.5 1012.0 %reduce-scatter.69.cloned.1.call-start = ((), (), s32[]{:S(2)}) async-start(), calls=%async_computation.62 | async-start | bytes 1114112
  1857.7 1053.0 %reduce-scatter.75.cloned.1.call-start = ((), (), s32[]{:S(2)}) async-start(), calls=%async_computation.65 | async-start | bytes 4456448
  1963.5 1023.0 %reduce-scatter.73.cloned.1.call-start = ((), (), s32[]{:S(2)}) async-start(), calls=%async_computation.64 | async-start | bytes 4456448
  2065.0 990.6 %reduce-scatter.67.cloned.1.call-start = ((), (), s32[]{:S(2)}) async-start(), calls=%async_computation.61 | async-start | bytes 3342336
  2142.5 982.2 %reduce-scatter.65.cloned.1.call-start = ((), (), s32[]{:S(2)}) async-start(), calls=%async_computation.60 | async-start | bytes 3342336
  2222.0 978.0 %reduce-scatter.55.cloned.1.call-start = ((), (), s32[]{:S(2)}) async-start(), calls=%async_computation.55 | async-start | bytes 4456448 | tf_op jit(solution)/shard_map/reduce_scatter | solution.py:155
  2318.8 957.0 %reduce-scatter.51.cloned.1.call-start = ((), (), s32[]{:S(2)}) async-start(), calls=%async_computation.53 | async-start | bytes 4456448 | tf_op jit(solution)/shard_map/reduce_scatter | solution.py:155
  2420.5 943.5 %reduce-scatter.63.cloned.1.call-start = ((), (), s32[]{:S(2)}) async-start(), calls=%async_computation.59 | async-start | bytes 6684672
  2576.0 876.8 %reduce-scatter.61.cloned.1.call-start = ((), (), s32[]{:S(2)}) async-start(), calls=%async_computation.58 | async-start | bytes 6684672
  2757.2 57.2 %copy-start.12 = (f32[1,320,1024]{2,1,0:T(8,128)S(1)}, f32[1,320,1024]{2,1,0:T(8,128)}, u32[]{:S(2)}) copy-start(f32[1,320,1024]{2,1,0:T(8,128)} %get-tuple-element.77) | copy-start | bytes 3932164
  2774.1 42.5 %copy-start.11 = (f32[1,320,1024]{2,1,0:T(8,128)S(1)}, f32[1,320,1024]{2,1,0:T(8,128)}, u32[]{:S(2)}) copy-start(f32[1,320,1024]{2,1,0:T(8,128)} %get-tuple-element.63) | copy-start | bytes 3932164
  (67 other events, 340.3 us)
Sparse Core Ops, SparseCore 0:
  10.9 64.5 all-gather.26
  77.7 44.0 all-gather.30
  123.9 36.7 all-gather.34
  162.7 52.1 all-gather.38
  216.9 48.8 all-gather.42
  267.2 151.0 all-gather.28
  419.8 80.3 all-gather.32
  501.8 33.1 all-gather.36
  536.5 104.0 all-gather.40
  641.9 103.9 all-gather.44
  754.3 50.7 all-gather.62
  807.0 51.7 all-gather.66
  861.0 48.7 all-gather.46
  911.7 51.7 all-gather.50
  965.5 36.1 all-gather.70
  1003.7 36.8 all-gather.54
  1042.7 44.0 all-gather.74
  1089.0 44.2 all-gather.58
  1134.8 102.8 all-gather.64
  1239.0 104.0 all-gather.68
  1344.6 104.0 all-gather.48
  1450.2 103.9 all-gather.52
  1555.8 33.1 all-gather.72
  1590.3 33.1 all-gather.56
  1625.0 80.3 all-gather.76
  1706.8 80.3 all-gather.60
  1789.3 31.8 reduce-scatter.46
  1823.5 31.8 reduce-scatter.44
  1857.7 99.2 reduce-scatter.58
  1959.2 99.2 reduce-scatter.56
  2060.8 77.0 reduce-scatter.42
  2140.3 77.0 reduce-scatter.40
  2219.5 99.2 reduce-scatter.52
  2321.2 99.2 reduce-scatter.48
  2422.8 144.4 reduce-scatter.38
  2569.4 144.4 reduce-scatter.36
  2717.4 57.3 reduce-scatter.70
  2778.8 56.5 reduce-scatter.68
  2839.2 71.3 reduce-scatter.74
  2915.0 71.5 reduce-scatter.72
  2990.3 65.2 reduce-scatter.66
  3059.4 65.2 reduce-scatter.64
  3128.4 71.5 reduce-scatter.54
  3204.4 71.4 reduce-scatter.50
  3279.7 84.3 reduce-scatter.62
  3368.3 84.3 reduce-scatter.60
where the time goes:
time: 3470 us; the launch traced here: 3460 us
  waiting for transfers between devices  2920 us (84%)
  matrix products  227 us (7%)
  local copies, waits for them, and re-layouts  155 us (4%)
  other arithmetic  93.9 us (3%)
  blocking collectives  39.4 us (1%)
    unnamed x54, waiting for transfers between devices  478 us
    all_gather x3, waiting for transfers between devices, gather_weights(): lax.all_gather(col_full[4], 'narrow', axis=0, tiled=True)  286 us
    reduce_scatter x2, waiting for transfers between devices, scatter_grads(): lax.psum_scatter(grad_set[0].astype(jnp.bfloat16), 'narrow', scatter_dime...  284 us
    all_gather x3, waiting for transfers between devices, gather_weights(): lax.all_gather(col_full[3], 'narrow', axis=0, tiled=True)  279 us
    reduce_scatter x2, waiting for transfers between devices, scatter_grads(): lax.psum_scatter(grad_set[3].astype(jnp.bfloat16), 'narrow', scatter_dime...  198 us
    reduce_scatter x2, waiting for transfers between devices, scatter_grads(): lax.psum_scatter(grad_set[4].astype(jnp.bfloat16), 'narrow', scatter_dime...  194 us
    all_gather x3, waiting for transfers between devices, gather_weights(): lax.all_gather(up_part, 'wide', axis=1, tiled=True)  161 us
    reduce_scatter x2, waiting for transfers between devices, scatter_grads(): lax.psum_scatter(row_owned[3].astype(jnp.bfloat16), 'wide', scatter_dimen...  149 us
  transfers between devices with their start and end apart: 46, of which 43 were waited for; matrix products, arithmetic and copies ran while one was open for 13% of the time, Pallas kernels for 0%

commit v1 on v0

v1 whole, which is shorter than its diff:
```python
import functools
import math

import jax
import jax.numpy as jnp
import numpy as np
from jax import lax
from jax.experimental import pallas as pl
from jax.experimental.pallas import tpu as pltpu
from jax.sharding import PartitionSpec as P

HEADS = 16
WIN_FRAMES = 5
WIN_SIDE = 8
TOK = WIN_FRAMES * WIN_SIDE * WIN_SIDE
F_SPAN = 2 * WIN_FRAMES - 1
S_SPAN = 2 * WIN_SIDE - 1
epsilon = 1e-06
inv_root_two = 0.7071067811865476
inv_root_tau = 0.3989422804014327
highest = lax.Precision.HIGHEST
MESH = pl.DeviceIdType.MESH
bf16 = jnp.bfloat16
f32 = jnp.float32


def position_features():
    p = np.arange(TOK)
    feats = np.zeros((TOK, WIN_FRAMES + 2 * WIN_SIDE), np.float32)
    feats[p, p // 64] = 1
    feats[p, WIN_FRAMES + (p // 8) % 8] = 1
    feats[p, WIN_FRAMES + WIN_SIDE + p % 8] = 1
    return feats


def offset_selector():
    sel = np.zeros((21, 21, F_SPAN + 2 * S_SPAN), np.float32)
    for i in range(WIN_FRAMES):
        for j in range(WIN_FRAMES):
            sel[i, j, i - j + WIN_FRAMES - 1] = 1
    for i in range(WIN_SIDE):
        for j in range(WIN_SIDE):
            sel[5 + i, 5 + j, F_SPAN + i - j + WIN_SIDE - 1] = 1
            sel[13 + i, 13 + j, F_SPAN + S_SPAN + i - j + WIN_SIDE - 1] = 1
    return sel


def both_halves(features):
    pad = [(0, 0)] * (features.ndim - 1) + [(0, 64 - features.shape[-1])]
    half = jnp.pad(features, pad)
    return jnp.concatenate([half, half], -1)


class Place:
    def __init__(self, dims):
        self.A, self.B, self.C = dims
        w = lax.axis_index("wide")
        self.c = lax.axis_index("narrow")
        self.k = lax.rem(w, 2)
        self.b = lax.rem(w // 2, self.B)
        self.a = w // (2 * self.B)

    def dev(self, a=None, b=None, k=None, c=None):
        a = self.a if a is None else a
        b = self.b if b is None else b
        k = self.k if k is None else k
        c = self.c if c is None else c
        return ((a * self.B + b) * 2 + k, c)

    def a_peer(self, d):
        return lax.rem(self.a + d, self.A)

    def b_peer(self, d):
        return lax.rem(self.b + d, self.B)

    def c_peer(self, d):
        return lax.rem(self.c + d, self.C)

    def barrier(self):
        peers = [self.dev(a=self.a_peer(d)) for d in range(1, self.A)]
        peers += [self.dev(b=self.b_peer(d)) for d in range(1, self.B)]
        peers += [self.dev(c=self.c_peer(d)) for d in range(1, self.C)]
        peers += [self.dev(k=1 - self.k)]
        sem = pltpu.get_barrier_semaphore()
        for peer in peers:
            pl.semaphore_signal(sem, inc=1, device_id=peer, device_id_type=MESH)
        pl.semaphore_wait(sem, len(peers))


def send(src, dst, ssem, rsem, dev):
    copy = pltpu.make_async_remote_copy(
        src_ref=src, dst_ref=dst, send_sem=ssem, recv_sem=rsem, device_id=dev, device_id_type=MESH
    )
    copy.start()
    return copy


def cols(c, K):
    return pl.ds(pl.multiple_of(c * K, K), K)


def n_sems(dims):
    A, B, C = dims
    return (A - 1) + (B - 1) + (C - 1) + 1


class Gather:
    def __init__(self, place, block, own, part_a, part_b, part_c, order, ssem, rsem):
        self.p = place
        self.block, self.own = block, own
        self.part_a, self.part_b, self.part_c = part_a, part_b, part_c
        self.order = order
        self.ssem, self.rsem = ssem, rsem
        self.sent = []
        self.phases = []

    def start(self, phase):
        p = self.p
        out = []
        if phase == 0:
            for d in range(1, p.A):
                out.append(send(self.block, self.own, self.ssem.at[d - 1], self.rsem.at[d - 1], p.dev(a=p.a_peer(d))))
        elif phase < 3:
            first = phase == 1
            if self.order[phase - 1] == "b":
                ref = self.part_a if first else self.part_b
                base = p.A - 1
                for d in range(1, p.B):
                    s = base + d - 1
                    out.append(send(ref, ref, self.ssem.at[s], self.rsem.at[s], p.dev(b=p.b_peer(d))))
            else:
                ref = self.part_a if first else self.part_b
                base = p.A - 1 + p.B - 1
                for d in range(1, p.C):
                    s = base + d - 1
                    out.append(send(ref, ref, self.ssem.at[s], self.rsem.at[s], p.dev(c=p.c_peer(d))))
        else:
            s = p.A - 1 + p.B - 1 + p.C - 1
            out.append(send(self.part_c, self.part_c, self.ssem.at[s], self.rsem.at[s], p.dev(k=1 - p.k)))
        self.phases.append(out)

    def landed(self, phase):
        for copy in self.phases[phase]:
            copy.wait_recv()

    def drain(self):
        for out in self.phases:
            for copy in out:
                copy.wait_send()


def pieces_of_weight(place, block, full, K, rows_list, ssem, rsem, base):
    p = place
    mine = cols(p.c, K)
    made = []
    for i, (rows, order) in enumerate(rows_list):
        part_a = full.at[:, p.b, p.k, rows, mine]
        if order == "bc":
            part_b = full.at[:, :, p.k, rows, mine]
        else:
            part_b = full.at[:, p.b, p.k, rows, :]
        made.append(
            Gather(
                p,
                block.at[rows, :],
                full.at[p.a, p.b, p.k, rows, mine],
                part_a,
                part_b,
                full.at[:, :, p.k, rows, :],
                order,
                ssem.at[base + i],
                rsem.at[base + i],
            )
        )
    return made


def piece_of_small(place, block, full, ssem, rsem, base):
    p = place
    return Gather(
        p,
        block,
        full.at[p.a, p.b, p.k, p.c],
        full.at[:, p.b, p.k, p.c],
        full.at[:, :, p.k, p.c],
        full.at[:, :, p.k],
        "bc",
        ssem.at[base],
        rsem.at[base],
    )


def run_gathers(groups, owned):
    for copy in owned:
        copy.start()
    count = len(groups)
    for t in range(count + 4):
        if t < count:
            for g in groups[t]:
                g.start(0)
        if t == 0:
            for copy in owned:
                copy.wait()
        for phase in (1, 2, 3, 4):
            i = t - phase
            if 0 <= i < count:
                for g in groups[i]:
                    g.landed(phase - 1)
                    if phase < 4:
                        g.start(phase)
    for group in groups:
        for g in group:
            g.drain()


def gather_kernel(dims, widths, halves, mod_blk, qkv_b, out_b, up_b, down_b, mod_f, qkv_f, out_f, up_f, down_f, ssem, rsem, lsem):
    p = Place(dims)
    p.barrier()
    blocks = [qkv_b, out_b, up_b, down_b]
    fulls = [qkv_f, out_f, up_f, down_f]
    owned = [pltpu.make_async_copy(mod_blk, mod_f.at[p.a, p.b, p.k, p.c], lsem.at[4])]
    groups = [[piece_of_small(p, mod_blk, mod_f, ssem, rsem, 0)]]
    base = 1
    for i, (block, full) in enumerate(zip(blocks, fulls)):
        K = widths[i]
        owned.append(pltpu.make_async_copy(block, full.at[p.a, p.b, p.k, :, cols(p.c, K)], lsem.at[i]))
        groups.append(pieces_of_weight(p, block, full, K, halves[i], ssem, rsem, base))
        base += len(halves[i])
    run_gathers(groups, owned)


def gather_all(dims, mod_blk, blocks):
    A, B, C = dims
    widths = [blk.shape[1] for blk in blocks]
    halves = []
    for blk in blocks:
        R = blk.shape[0]
        halves.append([(pl.ds(0, R // 2), "bc"), (pl.ds(R // 2, R // 2), "cb")])
    out_shape = [jax.ShapeDtypeStruct((A, B, 2, C) + mod_blk.shape, mod_blk.dtype)]
    out_shape += [jax.ShapeDtypeStruct((A, B, 2, blk.shape[0], C * blk.shape[1]), blk.dtype) for blk in blocks]
    count = 1 + sum(len(h) for h in halves)
    hbm = pl.BlockSpec(memory_space=pltpu.HBM)
    return pl.pallas_call(
        functools.partial(gather_kernel, dims, widths, halves),
        out_shape=out_shape,
        in_specs=[hbm] * 5,
        out_specs=[hbm] * 5,
        scratch_shapes=[
            pltpu.SemaphoreType.DMA((count, n_sems(dims))),
            pltpu.SemaphoreType.DMA((count, n_sems(dims))),
            pltpu.SemaphoreType.DMA((5,)),
        ],
        compiler_params=pltpu.CompilerParams(collective_id=0, has_side_effects=True),
        name="gather_weights",
    )(mod_blk, *blocks)


class Scatter:
    def __init__(self, place, grad, held, sib, rx, rl, out, K, ssem, rsem, lsem):
        self.p, self.grad, self.held, self.sib, self.rx, self.rl = place, grad, held, sib, rx, rl
        self.out, self.K = out, K
        self.ssem, self.rsem, self.lsem = ssem, rsem, lsem
        self.R = grad.shape[3]
        self.sent = []

    def _send(self, src, dst, s, dev):
        copy = send(src, dst, self.ssem.at[s], self.rsem.at[s], dev)
        self.sent.append(copy)
        return copy

    def start_sibling(self):
        p = self.p
        self.local = pltpu.make_async_copy(self.grad.at[:, :, p.k], self.held, self.lsem)
        self.local.start()
        self.first = self._send(self.grad.at[:, :, 1 - p.k], self.sib, 0, p.dev(k=1 - p.k))

    def add_sibling(self):
        self.local.wait()
        self.first.wait_recv()
        p = self.p

        def step(i, _):
            a, b = i // p.B, lax.rem(i, p.B)
            self.held[a, b] = self.held[a, b] + self.sib[a, b]
            return 0

        lax.fori_loop(0, p.A * p.B, step, 0)

    def halves(self):
        h = self.R // 2
        return pl.ds(0, h), pl.ds(h, h)

    def start_two(self):
        p, K = self.p, self.K
        r0, r1 = self.halves()
        self.second = []
        for d in range(1, p.C):
            self.second.append(
                self._send(self.held.at[:, :, r0, cols(p.c_peer(d), K)], self.rx["c0"].at[d - 1], d, p.dev(c=p.c_peer(d)))
            )
        for d in range(1, p.B):
            self.second.append(
                self._send(self.held.at[:, p.b_peer(d), r1, :], self.rx["b1"].at[d - 1], p.C - 1 + d, p.dev(b=p.b_peer(d)))
            )

    def add_two(self):
        p, K = self.p, self.K
        r0, r1 = self.halves()
        for copy in self.second:
            copy.wait_recv()
        mine = cols(p.c, K)

        def step(i, _):
            a, b = i // p.B, lax.rem(i, p.B)
            total = self.held[a, b, r0, mine]
            for d in range(1, p.C):
                total = total + self.rx["c0"][d - 1, a, b]
            self.held[a, b, r0, mine] = total
            return 0

        lax.fori_loop(0, p.A * p.B, step, 0)

        def step1(a, _):
            total = self.held[a, p.b, r1, :]
            for d in range(1, p.B):
                total = total + self.rx["b1"][d - 1, a]
            self.held[a, p.b, r1, :] = total
            return 0

        lax.fori_loop(0, p.A, step1, 0)

    def start_three(self):
        p, K = self.p, self.K
        r0, r1 = self.halves()
        mine = cols(p.c, K)
        base = p.C - 1 + p.B - 1
        self.third = []
        for d in range(1, p.B):
            self.third.append(
                self._send(self.held.at[:, p.b_peer(d), r0, mine], self.rx["b0"].at[d - 1], base + d, p.dev(b=p.b_peer(d)))
            )
        base += p.B - 1
        for d in range(1, p.C):
            self.third.append(
                self._send(self.held.at[:, p.b, r1, cols(p.c_peer(d), K)], self.rx["c1"].at[d - 1], base + d, p.dev(c=p.c_peer(d)))
            )

    def add_three(self):
        p, K = self.p, self.K
        r0, r1 = self.halves()
        for copy in self.third:
            copy.wait_recv()
        mine = cols(p.c, K)

        def step(a, _):
            total = self.held[a, p.b, r0, mine]
            for d in range(1, p.B):
                total = total + self.rx["b0"][d - 1, a]
            self.held[a, p.b, r0, mine] = total
            other = self.held[a, p.b, r1, mine]
            for d in range(1, p.C):
                other = other + self.rx["c1"][d - 1, a]
            self.held[a, p.b, r1, mine] = other
            return 0

        lax.fori_loop(0, p.A, step, 0)

    def start_four(self):
        p, K = self.p, self.K
        mine = cols(p.c, K)
        base = 2 * (p.C - 1 + p.B - 1)
        self.fourth = []
        for d in range(1, p.A):
            self.fourth.append(
                self._send(self.held.at[p.a_peer(d), p.b, :, mine], self.rl.at[d - 1], base + d, p.dev(a=p.a_peer(d)))
            )

    def finish(self):
        p, K = self.p, self.K
        for copy in self.fourth:
            copy.wait_recv()
        total = self.held[p.a, p.b, :, cols(p.c, K)].astype(f32)
        for d in range(1, p.A):
            total = total + self.rl[d - 1].astype(f32)
        self.out[...] = total

    def drain(self):
        for copy in self.sent:
            copy.wait_send()


def scatter_kernel(dims, widths, n_grads, *refs):
    A, B, C = dims
    grads = refs[:n_grads]
    smalls = refs[n_grads : n_grads + 2]
    outs = refs[n_grads + 2 : 2 * n_grads + 2]
    small_fulls = refs[2 * n_grads + 2 : 2 * n_grads + 4]
    scratch = refs[2 * n_grads + 4 :]
    per = 7
    ssem, rsem, lsem, gssem, grsem, glsem = scratch[per * n_grads :]
    p = Place(dims)
    p.barrier()
    items = []
    for i in range(n_grads):
        held, sib, c0, b1, b0, c1, rl = scratch[per * i : per * (i + 1)]
        rx = {"c0": c0, "b1": b1, "b0": b0, "c1": c1}
        items.append(
            Scatter(p, grads[i], held, sib, rx, rl, outs[i], widths[i], ssem.at[i], rsem.at[i], lsem.at[i])
        )
    owned = [
        pltpu.make_async_copy(smalls[i], small_fulls[i].at[p.a, p.b, p.k, p.c], glsem.at[i]) for i in range(2)
    ]
    small = [piece_of_small(p, smalls[i], small_fulls[i], gssem, grsem, i) for i in range(2)]
    for copy in owned:
        copy.start()
    for g in small:
        g.start(0)
    for copy in owned:
        copy.wait()
    stages = [
        (None, "start_sibling"),
        ("add_sibling", "start_two"),
        ("add_two", "start_three"),
        ("add_three", "start_four"),
        ("finish", None),
    ]
    for t in range(n_grads + 4):
        for phase in range(5):
            i = t - phase
            if 0 <= i < n_grads:
                before, after = stages[phase]
                if before:
                    getattr(items[i], before)()
                if after:
                    getattr(items[i], after)()
        if 1 <= t <= 4:
            for g in small:
                g.landed(t - 1)
                if t < 4:
                    g.start(t)
    for item in items:
        item.drain()
    for g in small:
        g.drain()


def scatter_all(dims, grads, smalls):
    A, B, C = dims
    widths = [g.shape[4] // C for g in grads]
    scratch = []
    for g in grads:
        R, full = g.shape[3], g.shape[4]
        K, h = full // C, g.shape[3] // 2
        scratch += [
            pltpu.VMEM((A, B, R, full), bf16),
            pltpu.VMEM((A, B, R, full), bf16),
            pltpu.VMEM((C - 1, A, B, h, K), bf16),
            pltpu.VMEM((B - 1, A, h, full), bf16),
            pltpu.VMEM((B - 1, A, h, K), bf16),
            pltpu.VMEM((C - 1, A, h, K), bf16),
            pltpu.VMEM((A - 1, R, K), bf16),
        ]
    n = len(grads)
    count = 1 + 2 * (C - 1 + B - 1) + (A - 1)
    scratch += [
        pltpu.SemaphoreType.DMA((n, count)),
        pltpu.SemaphoreType.DMA((n, count)),
        pltpu.SemaphoreType.DMA((n,)),
        pltpu.SemaphoreType.DMA((2, n_sems(dims))),
        pltpu.SemaphoreType.DMA((2, n_sems(dims))),
        pltpu.SemaphoreType.DMA((2,)),
    ]
    hbm = pl.BlockSpec(memory_space=pltpu.HBM)
    vmem = pl.BlockSpec(memory_space=pltpu.VMEM)
    out_shape = [jax.ShapeDtypeStruct((g.shape[3], g.shape[4] // C), f32) for g in grads]
    out_shape += [jax.ShapeDtypeStruct((A, B, 2, C) + s.shape, s.dtype) for s in smalls]
    return pl.pallas_call(
        functools.partial(scatter_kernel, dims, widths, n),
        out_shape=out_shape,
        in_specs=[hbm] * (n + 2),
        out_specs=[vmem] * n + [hbm] * 2,
        scratch_shapes=scratch,
        compiler_params=pltpu.CompilerParams(
            collective_id=1, has_side_effects=True, vmem_limit_bytes=62 * 2**20
        ),
        name="scatter_grads",
    )(*grads, *smalls)


def nt(lhs, rhs):
    return lax.dot_general(lhs, rhs, (((1,), (1,)), ((), ())), preferred_element_type=f32)


def nn(lhs, rhs):
    return lax.dot_general(lhs, rhs, (((1,), (0,)), ((), ())), preferred_element_type=f32)


def tn(lhs, rhs):
    return lax.dot_general(lhs, rhs, (((0,), (0,)), ((), ())), preferred_element_type=f32)


def attend_fwd_kernel(q_ref, k_ref, v_ref, u_ref, g_ref, m_ref, o_ref, lse_ref):
    low_half = lax.broadcasted_iota(jnp.int32, (TOK, 128), 1) < 64
    q = q_ref[...] * jnp.asarray(0.125, bf16)
    k, v, u = k_ref[...], v_ref[...], u_ref[...]
    mask = m_ref[0]
    results = []
    for h in range(2):
        own = low_half if h == 0 else jnp.logical_not(low_half)
        q_ext = jnp.where(own, q, u)
        k_ext = jnp.where(own, k, g_ref[h] + mask)
        s = nt(q_ext, k_ext)
        peak = jnp.max(s, -1, keepdims=True)
        e = jnp.exp(s - peak)
        total = jnp.sum(e, -1, keepdims=True)
        probs = (e / total).astype(bf16)
        lse_ref[0, h] = peak + jnp.log(total)
        results.append(nn(probs, v))
    o_ref[...] = jnp.where(low_half, results[0], results[1]).astype(bf16)


def attend_fwd(qkv, u, g, mask):
    wins = mask.shape[0]
    width = qkv.shape[1] // 3
    pairs = width // 128
    return pl.pallas_call(
        attend_fwd_kernel,
        grid=(wins, pairs),
        in_specs=[
            pl.BlockSpec((TOK, 128), lambda w, h: (w, h)),
            pl.BlockSpec((TOK, 128), lambda w, h: (w, pairs + h)),
            pl.BlockSpec((TOK, 128), lambda w, h: (w, 2 * pairs + h)),
            pl.BlockSpec((TOK, 128), lambda w, h: (0, 0)),
            pl.BlockSpec((2, TOK, 128), lambda w, h: (h, 0, 0)),
            pl.BlockSpec((1, TOK, 128), lambda w, h: (w, 0, 0)),
        ],
        out_specs=[
            pl.BlockSpec((TOK, 128), lambda w, h: (w, h)),
            pl.BlockSpec((1, 2, TOK, 1), lambda w, h: (w, h, 0, 0)),
        ],
        out_shape=[
            jax.ShapeDtypeStruct((wins * TOK, width), bf16),
            jax.ShapeDtypeStruct((wins, 2 * pairs, TOK, 1), f32),
        ],
        name="attend_fwd",
    )(qkv, qkv, qkv, u, g, mask)


def attend_bwd_kernel(q_ref, k_ref, v_ref, do_ref, lse_ref, u_ref, g_ref, m_ref, dq_ref, dk_ref, dv_ref, z_ref):
    low_half = lax.broadcasted_iota(jnp.int32, (TOK, 128), 1) < 64
    zero = jnp.zeros((TOK, 128), bf16)
    q = q_ref[...] * jnp.asarray(0.125, bf16)
    k, v, u, do = k_ref[...], v_ref[...], u_ref[...], do_ref[...]
    mask = m_ref[0]
    dqs, dks, dvs = [], [], []
    for h in range(2):
        own = low_half if h == 0 else jnp.logical_not(low_half)
        q_ext = jnp.where(own, q, u)
        k_ext = jnp.where(own, k, g_ref[h] + mask)
        s = nt(q_ext, k_ext)
        probs = jnp.exp(s - lse_ref[0, h])
        do_h = jnp.where(own, do, zero)
        dvs.append(tn(probs.astype(bf16), do))
        dp = nt(do_h, v)
        ds = probs * (dp - jnp.sum(probs * dp, -1, keepdims=True))
        ds_low = ds.astype(bf16)
        dqs.append(nn(ds_low, k))
        dk_ext = tn(ds_low, q_ext)
        dks.append(dk_ext)
        z_ref[0, h] = lax.dot_general(
            dk_ext, u.astype(f32), (((0,), (0,)), ((), ())), precision=highest, preferred_element_type=f32
        )
    dq_ref[...] = (jnp.where(low_half, dqs[0], dqs[1]) * 0.125).astype(bf16)
    dk_ref[...] = jnp.where(low_half, dks[0], dks[1]).astype(bf16)
    dv_ref[...] = jnp.where(low_half, dvs[0], dvs[1]).astype(bf16)


def attend_bwd(qkv, do, lse, u, g, mask):
    wins = mask.shape[0]
    width = qkv.shape[1] // 3
    pairs = width // 128
    tile = jax.ShapeDtypeStruct((wins * TOK, width), bf16)
    spec = pl.BlockSpec((TOK, 128), lambda w, h: (w, h))
    return pl.pallas_call(
        attend_bwd_kernel,
        grid=(wins, pairs),
        in_specs=[
            pl.BlockSpec((TOK, 128), lambda w, h: (w, h)),
            pl.BlockSpec((TOK, 128), lambda w, h: (w, pairs + h)),
            pl.BlockSpec((TOK, 128), lambda w, h: (w, 2 * pairs + h)),
            spec,
            pl.BlockSpec((1, 2, TOK, 1), lambda w, h: (w, h, 0, 0)),
            pl.BlockSpec((TOK, 128), lambda w, h: (0, 0)),
            pl.BlockSpec((2, TOK, 128), lambda w, h: (h, 0, 0)),
            pl.BlockSpec((1, TOK, 128), lambda w, h: (w, 0, 0)),
        ],
        out_specs=[spec, spec, spec, pl.BlockSpec((1, 2, 128, 128), lambda w, h: (w, h, 0, 0))],
        out_shape=[tile, tile, tile, jax.ShapeDtypeStruct((wins, 2 * pairs, 128, 128), f32)],
        name="attend_bwd",
    )(qkv, qkv, qkv, do, lse, u, g, mask)


def normalize(values):
    centre = jnp.mean(values, -1, keepdims=True)
    shifted = values - centre
    inv_std = lax.rsqrt(jnp.mean(shifted * shifted, -1, keepdims=True) + epsilon)
    return shifted * inv_std, inv_std


def normalize_back(grad_norm, normed, inv_std):
    return inv_std * (
        grad_norm
        - jnp.mean(grad_norm, -1, keepdims=True)
        - normed * jnp.mean(grad_norm * normed, -1, keepdims=True)
    )


def gelu_parts(pre):
    gate = 0.5 * (1.0 + lax.erf(pre * inv_root_two))
    return pre * gate, gate + pre * inv_root_tau * jnp.exp(-0.5 * pre * pre)


def body(dims, tokens, cotangent, cond, clip_frames, window_clip, window_half, ada, qkv_w, out_w, up_w, down_w, table):
    A, B, C = dims
    devices = A * B * 2 * C
    micro, wl, toks, width = tokens.shape
    wins = micro * wl
    clips = cond.shape[0]
    n = lax.axis_index("narrow")
    x = tokens.reshape(wins, toks, width).astype(f32)
    dy = cotangent.reshape(wins, toks, width).astype(f32)
    ids = window_clip.reshape(wins)
    half = window_half.reshape(wins)

    cond_act = jax.nn.silu(cond.astype(f32)).astype(bf16)
    act_rows = lax.dynamic_slice_in_dim(cond_act, n * ada.shape[0], ada.shape[0], 1)
    mod_part = jnp.dot(act_rows, ada, preferred_element_type=f32)
    mod_blk = mod_part.reshape(-1, 128)
    blocks = [m.T for m in (qkv_w, out_w, up_w, down_w)]
    mod_full, *fulls = gather_all(dims, mod_blk, blocks)
    qkv_t, out_t, up_t, down_t = [f.reshape(-1, f.shape[-1]) for f in fulls]

    mod_all = mod_full.reshape(A * B * 2, C, clips, ada.shape[1]).sum(1)
    mod_all = mod_all.transpose(1, 0, 2).reshape(clips, -1)
    pick = (ids[:, None] == jnp.arange(clips)[None, :]).astype(f32)
    modulation = jnp.einsum("wc,ce->we", pick, mod_all, precision=highest).reshape(wins, 6, 1, width)

    live = jnp.clip(jnp.sum(pick.astype(jnp.int32) * clip_frames[None, :], 1) - WIN_FRAMES * half, 1, WIN_FRAMES)
    feats = jnp.asarray(position_features())
    sel = jnp.asarray(offset_selector())
    u = jnp.pad(feats, ((0, 0), (0, 11)))
    u = both_halves(u.at[:, 21].set(1.0)).astype(bf16)
    key_bias = jnp.einsum("iq,hqj->hji", jnp.eye(21, dtype=f32), jnp.einsum("qke,he,jk->hqj", sel, table.astype(f32), feats, precision=highest), precision=highest)
    g = both_halves(key_bias).astype(bf16)
    invalid = (jnp.arange(toks)[None, :] // (WIN_SIDE * WIN_SIDE)) >= live[:, None]
    lane = jnp.arange(128)
    mask = jnp.where(invalid[:, :, None] & (lane % 64 == 21)[None, None, :], -1e30, 0.0).astype(bf16)

    def flat(v):
        return v.reshape(wins * toks, v.shape[-1])

    def windows(v):
        return v.reshape(wins, toks, v.shape[-1])

    norm1, inv1 = normalize(x)
    hidden1 = flat((norm1 * (1.0 + modulation[:, 1]) + modulation[:, 0]).astype(bf16))
    qkv = nt(hidden1, qkv_t).astype(bf16)
    heads, lse = attend_fwd(qkv, u, g, mask)
    attended = windows(nt(heads, out_t))
    mid = x + modulation[:, 2] * attended
    norm2, inv2 = normalize(mid)
    hidden2 = flat((norm2 * (1.0 + modulation[:, 4]) + modulation[:, 3]).astype(bf16))
    pre = nt(hidden2, up_t)
    act, slope = gelu_parts(pre)
    act = act.astype(bf16)
    ffn = windows(nt(act, down_t))
    mixed = (mid + modulation[:, 5] * ffn).astype(bf16)

    d_gate2 = jnp.sum(dy * ffn, 1)
    d_ffn = flat((modulation[:, 5] * dy).astype(bf16))
    g_down = tn(d_ffn, act).astype(bf16)
    d_pre = (nn(d_ffn, down_t) * slope).astype(bf16)
    g_up = tn(d_pre, hidden2).astype(bf16)
    d_hidden2 = windows(nn(d_pre, up_t))
    d_shift2 = jnp.sum(d_hidden2, 1)
    d_scale2 = jnp.sum(d_hidden2 * norm2, 1)
    d_mid = dy + normalize_back(d_hidden2 * (1.0 + modulation[:, 4]), norm2, inv2)
    d_gate1 = jnp.sum(d_mid * attended, 1)
    d_att = flat((modulation[:, 2] * d_mid).astype(bf16))
    g_out = tn(d_att, heads).astype(bf16)
    d_heads = nn(d_att, out_t).astype(bf16)
    dq, dk, dv, z = attend_bwd(qkv, d_heads, lse, u, g, mask)
    d_qkv = jnp.concatenate([dq, dk, dv], 1)
    g_qkv = tn(d_qkv, hidden1).astype(bf16)
    d_hidden1 = windows(nn(d_qkv, qkv_t))
    d_shift1 = jnp.sum(d_hidden1, 1)
    d_scale1 = jnp.sum(d_hidden1 * norm1, 1)
    grad_x = d_mid + normalize_back(d_hidden1 * (1.0 + modulation[:, 1]), norm1, inv1)

    d_mod = jnp.concatenate([d_shift1, d_scale1, d_gate1, d_shift2, d_scale2, d_gate2], 1).astype(bf16)
    zsum = jnp.sum(z, 0)
    pairs_z = jnp.stack([zsum[0::2, 64:85, :21], zsum[1::2, 0:21, :21]], 1).reshape(HEADS, 21, 21)
    table_part = jnp.einsum("hqk,qke->he", pairs_z, sel, precision=highest)
    table_blk = jnp.pad(table_part, ((0, 0), (0, 128 - table_part.shape[1])))
    table_blk = table_blk.at[0, 128 - wins :].set(ids.astype(f32))

    shaped = [
        full.reshape(f.shape) for full, f in zip((g_down, g_up, g_out, g_qkv), (fulls[3], fulls[2], fulls[1], fulls[0]))
    ]
    r_down, r_up, r_out, r_qkv, mod_grads, table_parts = scatter_all(
        dims, shaped, [d_mod.reshape(-1, 128), table_blk]
    )
    table_parts = table_parts.reshape(devices, HEADS, 128)
    grad_table = table_parts.sum(0)[:, : table.shape[1]]
    all_ids = table_parts[:, 0, 128 - wins :].reshape(devices, micro, wl).transpose(1, 0, 2).reshape(-1)

    w = lax.axis_index("wide")
    ncol = ada.shape[1]
    dm = mod_grads.reshape(devices, micro, wl, 6 * width)
    dm = lax.dynamic_slice_in_dim(dm, w * ncol, ncol, 3)
    dm = dm.transpose(1, 0, 2, 3).reshape(-1, ncol)
    picked = (all_ids[:, None] == jnp.arange(clips, dtype=f32)[None, :]).astype(f32)
    by_clip = jnp.einsum("wc,we->ce", picked, dm.astype(f32), precision=highest)
    grad_ada = jnp.einsum("cr,ce->re", act_rows.astype(f32), by_clip, precision=highest)
    return (
        mixed.reshape(tokens.shape),
        grad_x.reshape(tokens.shape),
        grad_ada,
        r_qkv.T,
        r_out.T,
        r_up.T,
        r_down.T,
        grad_table,
    )


def solution(mesh):
    W, C = mesh.shape["wide"], mesh.shape["narrow"]
    A = min(4, W // 2)
    dims = (A, W // 2 // A, C)
    sh = ("wide", "narrow")
    weight = P("narrow", "wide")
    return jax.shard_map(
        functools.partial(body, dims),
        mesh=mesh,
        in_specs=(P(None, sh), P(None, sh), P(), P(), P(None, sh), P(None, sh)) + (weight,) * 5 + (P(),),
        out_specs=(P(None, sh), P(None, sh)) + (weight,) * 5 + (P(),),
        check_vma=False,
    )
```

time: 3470 us -> 526 us (0.15)
  waiting for transfers between devices: 2920 us -> 0 us
  Pallas kernels: 0 us -> 372 us
  local copies, waits for them, and re-layouts: 155 us -> 19.8 us
  matrix products: 227 us -> 106 us
  other arithmetic: 93.9 us -> 17.4 us
  blocking collectives: 39.4 us -> 0 us
    all_gather x26 -> x0, waiting for transfers between devices: 1420 us -> none  [the longest x3 286 us: gather_weights(): lax.all_gather(col_full[4], 'narrow', axis=0, tiled=True)]
    reduce_scatter x12 -> x0, waiting for transfers between devices: 1020 us -> none  [the longest x2 284 us: scatter_grads(): lax.psum_scatter(grad_set[0].astype(jnp.bfloat16), 'narrow', scatter_dime...]
    unnamed x54 -> x0, waiting for transfers between devices: 478 us -> none
    pallas_call x0 -> x4, Pallas kernels: none -> 372 us  [the longest x1 164 us: gather_all(): pl.pallas_call(functools.partial(gather_kernel, dims, widths, halves), ou...]
    dot_general x46 -> x20, matrix products: 227 us -> 106 us  [the longest x4 34.7 us: nt(): lax.dot_general(lhs, rhs, (((1,), (1,)), ((), ())), preferred_element_typ...]
    add x2 -> x0, local copies, waits for them, and re-layouts: 66.9 us -> none  [the longest x1 34.8 us: build_bias(): along_frame[:, :, None, None, :, None, None]]
    unnamed x190 -> x90, local copies, waits for them, and re-layouts: 73.4 us -> 11.6 us
    psum x1 -> x0, blocking collectives: 39.4 us -> none  [body(): grad_table = lax.psum(table_grad(bias_total), ('wide', 'narrow'))]
  transfers between devices with their start and end apart: 46 -> 0, of which waited for: 43 -> 0; matrix products, arithmetic and copies ran while one was open for 13% -> 0% of each run, Pallas kernels for 0% -> 0%
where the time goes in v1:
time: 526 us; the launch traced here: 517 us
  Pallas kernels  372 us (71%)
  matrix products  106 us (20%)
  local copies, waits for them, and re-layouts  19.8 us (4%)
  other arithmetic  17.4 us (3%)
    pallas_call x1, Pallas kernels, gather_all(): pl.pallas_call(functools.partial(gather_kernel, dims, widths, halves), ou...  164 us
    pallas_call x1, Pallas kernels, scatter_all(): pl.pallas_call(functools.partial(scatter_kernel, dims, widths, n), out_sh...  147 us
    pallas_call x1, Pallas kernels, attend_bwd(): pl.pallas_call(attend_bwd_kernel, grid=(wins, pairs), in_specs=[pl.BlockS...  40 us
    dot_general x4, matrix products, nt(): lax.dot_general(lhs, rhs, (((1,), (1,)), ((), ())), preferred_element_typ...  34.7 us
    dot_general x4, matrix products, nn(): lax.dot_general(lhs, rhs, (((1,), (0,)), ((), ())), preferred_element_typ...  33.7 us
    dot_general x4, matrix products, tn(): lax.dot_general(lhs, rhs, (((0,), (0,)), ((), ())), preferred_element_typ...  31.1 us
    pallas_call x1, Pallas kernels, attend_fwd(): pl.pallas_call(attend_fwd_kernel, grid=(wins, pairs), in_specs=[pl.BlockS...  19.7 us
    unnamed x90, local copies, waits for them, and re-layouts  11.6 us

profile of v1, /device:TPU:0, one launch (start us, length us, event | category | flops | bytes accessed | tf_op | source)
XLA Modules:
  0.0 516.7 jit_solution(4065621320742767498)
XLA Ops:
  0.7 0.8 convert_element_type.149
  1.5 0.1 copy-done
  1.6 0.2 fusion.44
  1.8 0.6 reshape.400.mod_blk
  2.4 1.9 copy.42
  4.3 164.4 %gather_weights.1 = (f32[4,2,2,2,24,128]{5,4,3,2,1,0:T(8,128)}, bf16[4,2,2,192,1024]{4,3,2,1,0:T(8,128)(2,1)}, bf16[4,2,2,64,1024]{4,3,2,1,0:T(8,128)(2,1)}, bf1...) custom-call(f32[24,128]{1,0:T(8,128)} %reshape.400.mod_blk, bf16[192,512]{1,0:T(8,128)(2,1)} %bitcast.241, ...), custom_call_target="tpu_custom_call" | custom-call | tf_op jit(solution)/shard_map/gather_weights/pallas_call | solution.py:243
  168.8 1.0 reduce_sum.166
  169.9 0.3 convolution_bitcast_fusion.1
  170.2 0.2 convert_reduce_fusion
  170.5 0.5 fusion.24
  171.0 1.9 fusion.8
  172.9 0.8 copy-done.30
  173.7 5.8 %convolution_convert_fusion.3.q_ref.k_ref.v_ref = bf16[640,3072]{1,0:T(8,128)(2,1)} fusion(bf16[640,1024]{1,0:T(8,128)(2,1)S(1)} %bitcast.230, bf16[3072,1024]{1,0:T(8,128)(2,1)S(1)} %bitcast.256), kind=kOutput, calls=%fused_computation.11 | convolution fusion | flops 4028497920 | bytes 11534336 | tf_op jit(solution)/shard_map/dot_general | solution.py:491
  179.6 0.6 compare_reduce_fusion
  180.9 0.3 scatter.6
  181.2 0.7 pad_maximum_fusion.2.u_ref
  182.0 0.7 convolution_bitcast_fusion
  182.7 0.6 fusion.26
  183.3 2.3 fusion.31
  185.7 0.3 pad_convert_fusion
  186.0 1.9 pad_maximum_fusion.g_ref
  187.9 0.2 multiply_reduce_fusion.6
  188.2 0.8 select_convert_fusion.m_ref
  189.0 19.7 %attend_fwd.1 = (bf16[640,1024]{1,0:T(8,128)(2,1)}, f32[2,16,320,1]{3,2,1,0:T(8,128)}) custom-call(bf16[640,3072]{1,0:T(8,128)(2,1)} %convolution_convert_fusion.3.q_ref.k_ref.v_ref, bf16[640,3072]{1,0:T(8,128)(2,1)} %convolution_convert_fusion.3.q_ref.k_ref.v_ref, bf16[640,3072]{1,0:T(8,128)(2,1)} %convolution_convert_fusion.3.q_ref.k_ref.v_ref, ...), custom_call_target="tpu_custom_call" | custom-call | tf_op jit(solution)/shard_map/attend_fwd/pallas_call | solution.py:526
  208.7 3.7 fusion.46
  212.4 0.4 multiply_reduce_fusion.3
  212.8 0.5 add_convert_fusion.1
  213.4 12.6 %multiply_convert_fusion = (bf16[640,4096]{1,0:T(8,128)(2,1)}, f32[640,4096]{1,0:T(8,128)}) fusion(bf16[640,1024]{1,0:T(8,128)(2,1)S(1)} %bitcast.225, bf16[4096,1024]{1,0:T(8,128)(2,1)} %bitcast.253), kind=kOutput, calls=%fused_computation.6 | convolution fusion | flops 5381816320 | bytes 25427968 | tf_op jit(solution)/shard_map/dot_general | solution.py:491
  226.0 11.5 %fusion.4 = bf16[640,4096]{1,0:T(8,128)(2,1)} fusion(f32[640,4096]{1,0:T(8,128)} %get-tuple-element.118, bf16[640,1024]{1,0:T(8,128)(2,1)S(1)} %bitcast.227, bf16[1024,4096]{1,0:T(8,128)(2,1)S(1)} %bitcast.252), kind=kOutput, calls=%fused_computation.5 | convolution fusion | flops 5394923520 | bytes 25427968 | tf_op jit(solution)/shard_map/dot_general | solution.py:495
  237.5 11.1 %multiply_reduce_fusion = (bf16[2,1024]{1,0:T(2,128)(2,1)S(1)}, f32[2,320]{1,0:T(2,128)S(1)}, f32[2,320]{1,0:T(2,128)S(1)}, bf16[2,1024]{1,0:T(2,128)(2,1)S(1)}, f32[2,320,1024]{2,1,0:T(8,128)}) fusion(f32[2,320,1024]{2,1,0:T(8,128)S(1)} %get-tuple-element.101, f32[2,320]{1,0:T(2,128)S(1)} %add_rsqrt_fusion, f32[2,320]{1,0:T(2,128)S(1)} %broadcast_multiply_fusion.4, ...), kind=kOutput, calls=%fused_computation.42 | convolution fusion | flops 5374602240 | bytes 18900992 | tf_op jit(solution)/shard_map/dot_general | solution.py:495
  248.6 12.5 %fusion.9 = (bf16[2,1024]{1,0:T(2,128)(2,1)S(1)}, bf16[2,1,320,1024]{3,2,1,0:T(8,128)(2,1)}, bf16[2,1024]{1,0:T(2,128)(2,1)S(1)}, f32[2,320,1024]{2,1,0:T(8,128)S(1)}) fusion(bf16[2,1,320,1024]{3,2,1,0:T(8,128)(2,1)S(1)} %copy-done.5, f32[2,320,1024]{2,1,0:T(8,128)S(1)} %get-tuple-element.101, f32[2,1024]{1,0:T(2,128)S(1)} %get-tuple-element.108, ...), kind=kOutput, calls=%fused_computation.23 | convolution fusion | flops 5379190784 | bytes 26773504 | tf_op jit(solution)/shard_map/dot_general | solution.py:491
  261.2 0.3 multiply_convert_fusion.1
  261.5 2.6 copy-done.7
  264.2 2.7 convolution_convert_fusion.5.do_ref
  266.8 40.0 %attend_bwd.1 = (bf16[640,1024]{1,0:T(8,128)(2,1)}, bf16[640,1024]{1,0:T(8,128)(2,1)}, bf16[640,1024]{1,0:T(8,128)(2,1)}, f32[2,16,128,128]{3,2,1,0:T(8,128)}) custom-call(bf16[640,3072]{1,0:T(8,128)(2,1)} %convolution_convert_fusion.3.q_ref.k_ref.v_ref, bf16[640,3072]{1,0:T(8,128)(2,1)} %convolution_convert_fusion.3.q_ref.k_ref.v_ref, ...), custom_call_target="tpu_custom_call" | custom-call | tf_op jit(solution)/shard_map/attend_bwd/pallas_call | solution.py:584
  306.8 1.6 constant_dynamic-update-slice_fusion.2
  308.4 0.1 copy-done.11
  308.6 0.3 copy-done.10
  309.1 8.5 %fusion.23 = (bf16[2,1024]{1,0:T(2,128)(2,1)S(1)}, f32[2,320]{1,0:T(2,128)S(1)}, f32[2,320]{1,0:T(2,128)S(1)}, bf16[2,1024]{1,0:T(2,128)(2,1)S(1)}, f32[2,320,1024]{2,1,0:T(8,128)S(1)}) fusion(bf16[2,1,320,1024]{3,2,1,0:T(8,128)(2,1)S(1)} %copy-done.2, f32[2,320]{1,0:T(2,128)S(1)} %add_rsqrt_fusion.1, f32[2,320]{1,0:T(2,128)S(1)} %broadcast_multiply_fusion.5, ...), kind=kOutput, calls=%fused_computation.40 | convolution fusion | flops 4033080320 | bytes 14182400 | tf_op jit(solution)/shard_map/dot_general | solution.py:495
  317.6 2.4 fusion.22
  320.2 1.2 fusion.5
  321.4 11.8 %convolution_convert_fusion = bf16[1024,4096]{1,0:T(8,128)(2,1)} fusion(bf16[640,1024]{1,0:T(8,128)(2,1)S(1)} %get-tuple-element.122, bf16[640,4096]{1,0:T(8,128)(2,1)} %get-tuple-element.117), kind=kOutput, calls=%fused_computation.8 | convolution fusion | flops 5372903424 | bytes 14942208 | tf_op jit(solution)/shard_map/dot_general | solution.py:499
  333.2 9.0 %convolution_convert_fusion.1 = bf16[4096,1024]{1,0:T(8,128)(2,1)} fusion(bf16[640,4096]{1,0:T(8,128)(2,1)S(1)} %bitcast.259, bf16[640,1024]{1,0:T(8,128)(2,1)S(1)} %bitcast.226), kind=kOutput, calls=%fused_computation.9 | convolution fusion | flops 5372903424 | bytes 14942208 | tf_op jit(solution)/shard_map/dot_general | solution.py:499
  342.2 3.2 convolution_convert_fusion.4
  345.5 7.1 %convolution_convert_fusion.2 = bf16[3072,1024]{1,0:T(8,128)(2,1)} fusion(bf16[640,3072]{1,0:T(8,128)(2,1)S(1)} %copy-done.19, bf16[640,1024]{1,0:T(8,128)(2,1)S(1)} %get-tuple-element.121), kind=kOutput, calls=%fused_computation.10 | convolution fusion | flops 4029677568 | bytes 11534336 | tf_op jit(solution)/shard_map/dot_general | solution.py:499
  352.6 0.6 convert_element_type.177.refs_4_
  353.3 0.2 reduce_sum.184
  353.5 0.2 copy.46
  353.8 0.5 convolution_bitcast_fusion.2
  354.3 0.6 and_reduce_fusion
  355.0 0.6 fusion.47
  355.6 2.0 broadcast_select_fusion
  357.6 1.8 scatter.9.refs_5_
  359.4 0.6 copy-done.27
  360.0 147.5 %scatter_grads.1 = (f32[64,2048]{1,0:T(8,128)}, f32[256,512]{1,0:T(8,128)}, f32[64,512]{1,0:T(8,128)}, f32[192,512]{1,0:T(8,128)}, bf16[4,2,2,2,96,128]{5,4,3,2,...) custom-call(bf16[4,2,2,64,4096]{4,3,2,1,0:T(8,128)(2,1)} %bitcast.219, bf16[4,2,2,256,1024]{4,3,2,1,0:T(8,128)(2,1)} %bitcast.220, ...), custom_call_target="tpu_custom_call" | custom-call | tf_op jit(solution)/shard_map/scatter_grads/pallas_call | solution.py:477
  507.5 2.2 reshape.419
  509.8 1.0 slice.89
  511.0 0.3 fusion.28
  511.3 1.4 fusion.45
  512.7 1.0 copy.52
  513.7 0.6 reduce_sum.185
  514.3 0.7 copy.72
  515.1 0.7 copy.73
  515.7 0.8 copy.74
  (106 shorter events, 1.1 us)
Async XLA Ops:
  0.6 1.0 copy-start
  0.7 169.2 %copy-start.29 = (s32[2,1]{0,1:T(1,128)S(1)}, s32[2,1]{0,1:T(1,128)}, u32[]{:S(2)}) copy-start(s32[2,1]{0,1:T(1,128)} %param.22) | copy-start | bytes 28
  0.7 169.5 %copy-start.2 = (bf16[2,1,320,1024]{3,2,1,0:T(8,128)(2,1)S(1)}, bf16[2,1,320,1024]{3,2,1,0:T(8,128)(2,1)}, u32[]{:S(2)}) copy-start(bf16[2,1,320,1024]{3,2,1,0:T(8,128)(2,1)} %param.18) | copy-start | bytes 3932164
  2.4 168.6 %copy-start.5 = (bf16[2,1,320,1024]{3,2,1,0:T(8,128)(2,1)S(1)}, bf16[2,1,320,1024]{3,2,1,0:T(8,128)(2,1)}, u32[]{:S(2)}) copy-start(bf16[2,1,320,1024]{3,2,1,0:T(8,128)(2,1)} %param.19) | copy-start | bytes 3932164
  170.5 3.3 copy-start.30
  173.7 7.2 %copy-start.21 = (bf16[320,32]{1,0:T(8,128)(2,1)S(1)}, bf16[320,32]{1,0:T(8,128)(2,1)}, u32[]{:S(2)}) copy-start(bf16[320,32]{1,0:T(8,128)(2,1)} %constant.236) | copy-start | bytes 61444
  173.7 8.2 %copy-start.24 = (f32[21,21,39]{2,1,0:T(8,128)S(1)}, f32[21,21,39]{2,1,0:T(8,128)}, u32[]{:S(2)}) copy-start(f32[21,21,39]{2,1,0:T(8,128)} %constant.141.clone) | copy-start | bytes 206392
  173.7 8.2 %copy-start.28 = (bf16[16,39]{1,0:T(8,128)(2,1)S(1)}, bf16[16,39]{1,0:T(8,128)(2,1)}, u32[]{:S(2)}) copy-start(bf16[16,39]{1,0:T(8,128)(2,1)} %param.29) | copy-start | bytes 3748
  173.7 9.0 %copy-start.26 = (f32[320,21,1]{0,1,2:T(8,128)S(1)}, f32[320,21,1]{0,1,2:T(8,128)}, u32[]{:S(2)}) copy-start(f32[320,21,1]{0,1,2:T(8,128)} %constant.155) | copy-start | bytes 80644
  185.6 2.2 copy-start.31
  185.6 2.4 copy-start.32
  212.8 13.1 %slice-start = ((s8[8388608]{0:T(1024)(128)(4,1)}), s8[4194304]{0:T(1024)(128)(4,1)S(1)}, s32[]{:S(2)}) async-start(s8[8388608]{0:T(1024)(128)(4,1)} %bitcast.250), calls=%async_computation | async-start | bytes 8388608
  213.3 12.6 %copy-start.8 = (bf16[2,320,1024]{2,1,0:T(8,128)(2,1)}, bf16[2,320,1024]{2,1,0:T(8,128)(2,1)S(1)}, u32[]{:S(2)}) copy-start(bf16[2,320,1024]{2,1,0:T(8,128)(2,1)S(1)} %add_convert_fusion.1) | copy-start | bytes 3932164
  213.4 12.6 %copy-start.12 = (bf16[2,320,1024]{2,1,0:T(8,128)(2,1)S(1)}, bf16[2,320,1024]{2,1,0:T(8,128)(2,1)}, u32[]{:S(2)}) copy-start(bf16[2,320,1024]{2,1,0:T(8,128)(2,1)} %get-tuple-element.123) | copy-start | bytes 3932164
  213.4 12.6 %slice-start.1 = ((s8[8388608]{0:T(1024)(128)(4,1)}), s8[4194304]{0:T(1024)(128)(4,1)S(1)}, s32[]{:S(2)}) async-start(s8[8388608]{0:T(1024)(128)(4,1)} %bitcast.250), calls=%async_computation.1 | async-start | bytes 8388608
  261.1 5.7 %copy-start.3 = (f32[2,320,1024]{2,1,0:T(8,128)}, f32[2,320,1024]{2,1,0:T(8,128)S(1)}, u32[]{:S(2)}) copy-start(f32[2,320,1024]{2,1,0:T(8,128)S(1)} %get-tuple-element.105) | copy-start | bytes 7864324
  261.1 3.0 copy-start.7
  261.5 5.3 %copy-start.13 = (bf16[2,320,1024]{2,1,0:T(8,128)(2,1)}, bf16[2,320,1024]{2,1,0:T(8,128)(2,1)S(1)}, u32[]{:S(2)}) copy-start(bf16[2,320,1024]{2,1,0:T(8,128)(2,1)S(1)} %multiply_convert_fusion.1) | copy-start | bytes 3932164
  306.8 1.7 copy-start.11
  306.8 2.1 copy-start.10
  309.0 8.5 %copy-start.18 = (bf16[640,3072]{1,0:T(8,128)(2,1)}, bf16[640,3072]{1,0:T(8,128)(2,1)S(1)}, u32[]{:S(2)}) copy-start(bf16[640,3072]{1,0:T(8,128)(2,1)S(1)} %constant_dynamic-update-slice_fusion) | copy-start | bytes 11796484
  309.0 8.6 %copy-start.4 = (f32[2,320,1024]{2,1,0:T(8,128)S(1)}, f32[2,320,1024]{2,1,0:T(8,128)}, u32[]{:S(2)}) copy-start(f32[2,320,1024]{2,1,0:T(8,128)} %copy-done.3) | copy-start | bytes 7864324
  320.1 13.0 %slice-start.2 = ((s8[5242880]{0:T(1024)(128)(4,1)}), s8[4194304]{0:T(1024)(128)(4,1)S(1)}, s32[]{:S(2)}) async-start(s8[5242880]{0:T(1024)(128)(4,1)} %bitcast.258), calls=%async_computation.2 | async-start | bytes 8388608
  321.4 11.8 %copy-start.9 = (bf16[2,320,1024]{2,1,0:T(8,128)(2,1)S(1)}, bf16[2,320,1024]{2,1,0:T(8,128)(2,1)}, u32[]{:S(2)}) copy-start(bf16[2,320,1024]{2,1,0:T(8,128)(2,1)} %copy-done.8) | copy-start | bytes 3932164
  321.4 11.8 %slice-start.3 = ((s8[5242880]{0:T(1024)(128)(4,1)}), s8[1048576]{0:T(1024)(128)(4,1)S(1)}, s32[]{:S(2)}) async-start(s8[5242880]{0:T(1024)(128)(4,1)} %bitcast.258), calls=%async_computation.3 | async-start | bytes 2097152
  333.2 9.0 %copy-start.14 = (bf16[2,320,1024]{2,1,0:T(8,128)(2,1)S(1)}, bf16[2,320,1024]{2,1,0:T(8,128)(2,1)}, u32[]{:S(2)}) copy-start(bf16[2,320,1024]{2,1,0:T(8,128)(2,1)} %copy-done.13) | copy-start | bytes 3932164
  333.2 9.0 %copy-start.15 = (bf16[640,1024]{1,0:T(8,128)(2,1)S(1)}, bf16[640,1024]{1,0:T(8,128)(2,1)}, u32[]{:S(2)}) copy-start(bf16[640,1024]{1,0:T(8,128)(2,1)} %get-tuple-element.51) | copy-start | bytes 3932164
  342.2 3.2 copy-start.19
  345.5 7.8 %copy-start.6 = (f32[2,16,128,128]{3,2,1,0:T(8,128)S(1)}, f32[2,16,128,128]{3,2,1,0:T(8,128)}, u32[]{:S(2)}) copy-start(f32[2,16,128,128]{3,2,1,0:T(8,128)} %get-tuple-element.59) | copy-start | bytes 6291460
  352.5 1.3 copy-start.23
  352.5 1.8 copy-start.33
  359.4 0.6 copy-start.27
  507.5 5.2 %copy-start.17 = (f32[256,512]{1,0:T(8,128)S(1)}, f32[256,512]{1,0:T(8,128)}, u32[]{:S(2)}) copy-start(f32[256,512]{1,0:T(8,128)} %get-tuple-element.64) | copy-start | bytes 1572868
  507.5 6.2 %copy-start.22 = (f32[4,2,2,2,16,128]{5,4,3,2,1,0:T(8,128)S(1)}, f32[4,2,2,2,16,128]{5,4,3,2,1,0:T(8,128)}, u32[]{:S(2)}) copy-start(f32[4,2,2,2,16,128]{5,4,3,2,1,0:T(8,128)} %get-tuple-element.60) | copy-start | bytes 786436
  507.5 6.8 %copy-start.20 = (f32[192,512]{1,0:T(8,128)S(1)}, f32[192,512]{1,0:T(8,128)}, u32[]{:S(2)}) copy-start(f32[192,512]{1,0:T(8,128)} %get-tuple-element.62) | copy-start | bytes 1179652
  507.5 7.6 %copy-start.25 = (f32[64,512]{1,0:T(8,128)S(1)}, f32[64,512]{1,0:T(8,128)}, u32[]{:S(2)}) copy-start(f32[64,512]{1,0:T(8,128)} %get-tuple-element.63) | copy-start | bytes 393220
  507.5 8.2 %copy-start.16 = (f32[64,2048]{1,0:T(8,128)S(1)}, f32[64,2048]{1,0:T(8,128)}, u32[]{:S(2)}) copy-start(f32[64,2048]{1,0:T(8,128)} %get-tuple-element.65) | copy-start | bytes 1572868
  507.5 9.0 %copy-start.1 = (bf16[512,384]{1,0:T(8,128)(2,1)S(1)}, bf16[512,384]{1,0:T(8,128)(2,1)}, u32[]{:S(2)}) copy-start(bf16[512,384]{1,0:T(8,128)(2,1)} %param.24) | copy-start | bytes 1179652

commit v2 on v0

v2 whole, which is shorter than its diff:
```python
import functools
import math

import jax
import jax.numpy as jnp
import numpy as np
from jax import lax
from jax.experimental import pallas as pl
from jax.experimental.pallas import tpu as pltpu
from jax.sharding import PartitionSpec as P

HEADS = 16
WIN_FRAMES = 5
WIN_SIDE = 8
TOK = WIN_FRAMES * WIN_SIDE * WIN_SIDE
F_SPAN = 2 * WIN_FRAMES - 1
S_SPAN = 2 * WIN_SIDE - 1
epsilon = 1e-06
inv_root_two = 0.7071067811865476
inv_root_tau = 0.3989422804014327
highest = lax.Precision.HIGHEST
MESH = pl.DeviceIdType.MESH
bf16 = jnp.bfloat16
f32 = jnp.float32


def position_features():
    p = np.arange(TOK)
    feats = np.zeros((TOK, WIN_FRAMES + 2 * WIN_SIDE), np.float32)
    feats[p, p // 64] = 1
    feats[p, WIN_FRAMES + (p // 8) % 8] = 1
    feats[p, WIN_FRAMES + WIN_SIDE + p % 8] = 1
    return feats


def offset_selector():
    sel = np.zeros((21, 21, F_SPAN + 2 * S_SPAN), np.float32)
    for i in range(WIN_FRAMES):
        for j in range(WIN_FRAMES):
            sel[i, j, i - j + WIN_FRAMES - 1] = 1
    for i in range(WIN_SIDE):
        for j in range(WIN_SIDE):
            sel[5 + i, 5 + j, F_SPAN + i - j + WIN_SIDE - 1] = 1
            sel[13 + i, 13 + j, F_SPAN + S_SPAN + i - j + WIN_SIDE - 1] = 1
    return sel


def nt(lhs, rhs):
    return lax.dot_general(lhs, rhs, (((1,), (1,)), ((), ())), preferred_element_type=f32)


def nn(lhs, rhs):
    return lax.dot_general(lhs, rhs, (((1,), (0,)), ((), ())), preferred_element_type=f32)


def tn(lhs, rhs):
    return lax.dot_general(lhs, rhs, (((0,), (0,)), ((), ())), preferred_element_type=f32)


def normalize(values):
    centre = jnp.mean(values, -1, keepdims=True)
    shifted = values - centre
    inv_std = lax.rsqrt(jnp.mean(shifted * shifted, -1, keepdims=True) + epsilon)
    return shifted * inv_std, inv_std


def normalize_back(grad_norm, normed, inv_std):
    return inv_std * (
        grad_norm
        - jnp.mean(grad_norm, -1, keepdims=True)
        - normed * jnp.mean(grad_norm * normed, -1, keepdims=True)
    )


def gelu_parts(pre):
    gate = 0.5 * (1.0 + lax.erf(pre * inv_root_two))
    return pre * gate, gate + pre * inv_root_tau * jnp.exp(-0.5 * pre * pre)


def guard(cond, fn):
    if isinstance(cond, bool):
        if cond:
            fn()
    else:
        pl.when(cond)(fn)


def both(*conds):
    total = True
    for cond in conds:
        if isinstance(cond, bool):
            if not cond:
                return False
        elif total is True:
            total = cond
        else:
            total = jnp.logical_and(total, cond)
    return total


def loop(count, fn):
    def step(i, carry):
        fn(i)
        return carry

    lax.fori_loop(0, count, step, 0)


def cols(c, K):
    return pl.ds(pl.multiple_of(c * K, K), K)


class Place:
    def __init__(self, dims):
        self.A, self.B, self.C = dims
        w = lax.axis_index("wide")
        self.c = lax.axis_index("narrow")
        self.k = lax.rem(w, 2)
        self.b = lax.rem(w // 2, self.B)
        self.a = w // (2 * self.B)

    def dev(self, a=None, b=None, k=None, c=None):
        a = self.a if a is None else a
        b = self.b if b is None else b
        k = self.k if k is None else k
        c = self.c if c is None else c
        return ((a * self.B + b) * 2 + k, c)

    def a_peer(self, d):
        return lax.rem(self.a + d, self.A)

    def b_peer(self, d):
        return lax.rem(self.b + d, self.B)

    def c_peer(self, d):
        return lax.rem(self.c + d, self.C)

    def barrier(self):
        peers = [self.dev(a=self.a_peer(d)) for d in range(1, self.A)]
        peers += [self.dev(b=self.b_peer(d)) for d in range(1, self.B)]
        peers += [self.dev(c=self.c_peer(d)) for d in range(1, self.C)]
        peers += [self.dev(k=1 - self.k)]
        sem = pltpu.get_barrier_semaphore()
        for peer in peers:
            pl.semaphore_signal(sem, inc=1, device_id=peer, device_id_type=MESH)
        pl.semaphore_wait(sem, len(peers))


def remote(src, dst, ssem, rsem, dev):
    return pltpu.make_async_remote_copy(
        src_ref=src, dst_ref=dst, send_sem=ssem, recv_sem=rsem, device_id=dev, device_id_type=MESH
    )


class Gather:
    def __init__(self, place, blocks, full, ssem, rsem):
        self.p, self.blocks, self.full, self.ssem, self.rsem = place, blocks, full, ssem, rsem
        self.Rp, self.K = blocks.shape[1], blocks.shape[2]
        self.count = blocks.shape[0]

    @staticmethod
    def sems(dims):
        A, B, C = dims
        return 2 * (A - 1) + 2 * (B - 1 + C - 1) + 1

    def along(self, t, ref, axis, base):
        p = self.p
        made = []
        for d in range(1, p.B if axis == "b" else p.C):
            dev = p.dev(b=p.b_peer(d)) if axis == "b" else p.dev(c=p.c_peer(d))
            made.append(remote(ref, ref, self.ssem.at[t, base + d - 1], self.rsem.at[t, base + d - 1], dev))
        return made

    def copies(self, t, phase, half=0):
        p, full = self.p, self.full
        h = self.Rp // 2
        rows = pl.ds(half * h, h)
        mine = cols(p.c, self.K)
        nA, nB, nC = p.A - 1, p.B - 1, p.C - 1
        if phase == 0:
            made = []
            for d in range(1, p.A):
                s = half * nA + d - 1
                made.append(
                    remote(
                        self.blocks.at[t, rows, :],
                        full.at[t, p.a, p.b, p.k, rows, mine],
                        self.ssem.at[t, s],
                        self.rsem.at[t, s],
                        p.dev(a=p.a_peer(d)),
                    )
                )
            return made
        if phase == 1:
            ref = full.at[t, :, p.b, p.k, rows, mine]
            return self.along(t, ref, "b", 2 * nA) if half == 0 else self.along(t, ref, "c", 2 * nA + nB)
        base = 2 * nA + nB + nC
        if phase == 2:
            if half == 0:
                return self.along(t, full.at[t, :, :, p.k, rows, mine], "c", base)
            return self.along(t, full.at[t, :, p.b, p.k, rows, :], "b", base + nC)
        s = base + nB + nC
        ref = full.at[t, :, :, p.k]
        return [remote(ref, ref, self.ssem.at[t, s], self.rsem.at[t, s], p.dev(k=1 - p.k))]

    def start(self, t, phase, half=0):
        for copy in self.copies(t, phase, half):
            copy.start()

    def landed(self, t, phase, half=0):
        for copy in self.copies(t, phase, half):
            copy.wait_recv()

    def first(self, t):
        for half in (0, 1):
            self.start(t, 0, half)

    def slot(self, s, ahead):
        n = self.count

        def advance(t, phase):
            def run():
                for half in (0, 1):
                    self.landed(t, phase - 1, half)
                    if phase < 3:
                        self.start(t, phase, half)
                if phase == 3:
                    self.start(t, 3)

            guard(both(t >= 0, t < n), run)

        guard(s + ahead < n, lambda: self.first(s + ahead))
        for phase in (1, 2, 3):
            advance(s - phase + 1, phase)
        guard(both(s - 3 >= 0, s - 3 < n), lambda: self.landed(s - 3, 3))

    def drain(self):
        def one(t):
            for phase in range(4):
                for half in (0, 1) if phase < 3 else (0,):
                    for copy in self.copies(t, phase, half):
                        copy.wait_send()

        loop(self.count, one)


class Scatter:
    def __init__(self, place, st, held, c0, b1, b0, c1, ra, fin, out, ssem, rsem, fsem):
        self.p, self.st, self.held = place, st, held
        self.c0, self.b1, self.b0, self.c1, self.ra, self.fin, self.out = c0, b1, b0, c1, ra, fin, out
        self.ssem, self.rsem, self.fsem = ssem, rsem, fsem
        self.Rp, self.K = ra.shape[2], ra.shape[3]
        self.count = held.shape[0]

    @staticmethod
    def sems(dims):
        A, B, C = dims
        return 1 + 2 * (B - 1 + C - 1) + (A - 1)

    def one(self, r, s, src, dst, dev):
        return remote(src, dst, self.ssem.at[r, s], self.rsem.at[r, s], dev)

    def sibling(self, r, slot):
        p = self.p
        return self.one(r, 0, self.st[slot].at[:, :, 1 - p.k], self.held.at[r], p.dev(k=1 - p.k))

    def copies(self, r, phase):
        p, K, held = self.p, self.K, self.held
        h = self.Rp // 2
        r0, r1 = pl.ds(0, h), pl.ds(h, h)
        mine = cols(p.c, K)
        nB, nC = p.B - 1, p.C - 1
        made = []
        if phase == 1:
            for d in range(1, p.C):
                made.append(
                    self.one(r, d, held.at[r, :, :, r0, cols(p.c_peer(d), K)], self.c0.at[r, d - 1], p.dev(c=p.c_peer(d)))
                )
            for d in range(1, p.B):
                made.append(
                    self.one(r, nC + d, held.at[r, :, p.b_peer(d), r1, :], self.b1.at[r, d - 1], p.dev(b=p.b_peer(d)))
                )
        elif phase == 2:
            base = nB + nC
            for d in range(1, p.B):
                made.append(
                    self.one(r, base + d, held.at[r, :, p.b_peer(d), r0, mine], self.b0.at[r, d - 1], p.dev(b=p.b_peer(d)))
                )
            base += nB
            for d in range(1, p.C):
                made.append(
                    self.one(
                        r, base + d, held.at[r, :, p.b, r1, cols(p.c_peer(d), K)], self.c1.at[r, d - 1], p.dev(c=p.c_peer(d))
                    )
                )
        else:
            base = 2 * (nB + nC)
            for d in range(1, p.A):
                made.append(
                    self.one(r, base + d, held.at[r, p.a_peer(d), p.b, :, mine], self.ra.at[r, d - 1], p.dev(a=p.a_peer(d)))
                )
        return made

    def start(self, r, phase):
        for copy in self.copies(r, phase):
            copy.start()

    def landed(self, r, phase):
        for copy in self.copies(r, phase):
            copy.wait_recv()

    def flush(self, r, slot):
        p = self.p
        copy = self.sibling(r, slot)
        copy.wait_recv()

        def add(i):
            a, b = i // p.B, lax.rem(i, p.B)
            self.held[r, a, b] = self.held[r, a, b] + self.st[slot][a, b, p.k]

        loop(p.A * p.B, add)
        copy.wait_send()
        self.start(r, 1)

    def mid(self, r):
        p, held = self.p, self.held
        h = self.Rp // 2
        r0, r1 = pl.ds(0, h), pl.ds(h, h)
        mine = cols(p.c, self.K)
        self.landed(r, 1)

        def add0(i):
            a, b = i // p.B, lax.rem(i, p.B)
            total = held[r, a, b, r0, mine]
            for d in range(p.C - 1):
                total = total + self.c0[r, d, a, b]
            held[r, a, b, r0, mine] = total

        loop(p.A * p.B, add0)

        def add1(a):
            total = held[r, a, p.b, r1, :]
            for d in range(p.B - 1):
                total = total + self.b1[r, d, a]
            held[r, a, p.b, r1, :] = total

        loop(p.A, add1)
        self.start(r, 2)

    def late(self, r):
        p, held = self.p, self.held
        h = self.Rp // 2
        r0, r1 = pl.ds(0, h), pl.ds(h, h)
        mine = cols(p.c, self.K)
        self.landed(r, 2)

        def add(a):
            total = held[r, a, p.b, r0, mine]
            for d in range(p.B - 1):
                total = total + self.b0[r, d, a]
            held[r, a, p.b, r0, mine] = total
            other = held[r, a, p.b, r1, mine]
            for d in range(p.C - 1):
                other = other + self.c1[r, d, a]
            held[r, a, p.b, r1, mine] = other

        loop(p.A, add)
        self.start(r, 3)

    def result(self, r):
        s = lax.rem(r, 2)
        return pltpu.make_async_copy(self.fin.at[s], self.out.at[r], self.fsem.at[s])

    def last(self, r):
        p = self.p
        self.landed(r, 3)
        total = self.held[r, p.a, p.b, :, cols(p.c, self.K)].astype(f32)
        for d in range(p.A - 1):
            total = total + self.ra[r, d].astype(f32)
        guard(r >= 2, lambda: self.result(r - 2).wait())
        self.fin[lax.rem(r, 2)] = total
        self.result(r).start()

    def slot(self, u, top):
        guard(both(u >= 0, u < top), lambda: self.mid(u))
        guard(both(u >= 1, u - 1 < top), lambda: self.late(u - 1))
        guard(both(u >= 2, u - 2 < top), lambda: self.last(u - 2))

    def drain(self):
        def one(r):
            for phase in (1, 2, 3):
                for copy in self.copies(r, phase):
                    copy.wait_send()

        loop(self.count, one)
        for r in (self.count - 2, self.count - 1):
            self.result(r).wait()


class Spread:
    def __init__(self, place, block, full, axes, ssem, rsem, base):
        p = place
        self.p, self.block, self.full, self.axes = p, block, full, axes
        self.ssem, self.rsem, self.base = ssem, rsem, base

    def copies(self, phase):
        p = self.p
        with_c = "c" in self.axes
        tail = (p.c,) if with_c else ()
        axis = self.axes[phase]
        base = self.base
        for done in self.axes[:phase]:
            base += {"a": p.A - 1, "b": p.B - 1, "c": p.C - 1, "k": 1}[done]
        every = slice(None)
        done = self.axes[:phase]
        index = (
            every if "a" in done else p.a,
            every if "b" in done else p.b,
            every if "k" in done else p.k,
        )
        if with_c:
            index += (every if "c" in done else p.c,)
        dst = self.full.at[index]
        src = self.block if phase == 0 else dst
        made = []
        count = {"a": p.A, "b": p.B, "c": p.C, "k": 2}[axis]
        for d in range(1, count):
            dev = {
                "a": lambda: p.dev(a=p.a_peer(d)),
                "b": lambda: p.dev(b=p.b_peer(d)),
                "c": lambda: p.dev(c=p.c_peer(d)),
                "k": lambda: p.dev(k=1 - p.k),
            }[axis]()
            s = base + d - 1
            made.append(remote(src, dst, self.ssem.at[s], self.rsem.at[s], dev))
        return made

    def start(self, phase):
        for copy in self.copies(phase):
            copy.start()

    def landed(self, phase):
        for copy in self.copies(phase):
            copy.wait_recv()

    def drain(self):
        for phase in range(len(self.axes)):
            for copy in self.copies(phase):
                copy.wait_send()


LOOKAHEAD = 2
ROWS = 32
NAMES_IN = (
    "mod_blk", "blocks", "x_in", "dy_in", "pick", "uq", "uk", "ut", "tmat", "selv", "ids_row",
)
NAMES_OUT = (
    "full", "mixed", "gx", "rout", "dmf", "tf",
)
NAMES_SCRATCH = (
    "x", "dy", "hid", "dff", "qkv", "heads", "mid", "ffn", "dh2", "wbuf", "mod", "dmod", "modx", "modf", "ms",
    "zacc", "tb", "dmb", "st", "held", "c0", "b1", "b0", "c1", "ra", "fin", "in_sem", "w_sem", "own_sem",
    "o_sem", "g_s", "g_r", "r_s", "r_r", "f_sem", "m_s", "m_r", "s_s", "s_r",
)


def step_kernel(dims, wins, *refs):
    names = NAMES_IN + NAMES_OUT + NAMES_SCRATCH
    R = dict(zip(names, refs))
    p = Place(dims)
    A, B, C = dims
    T = wins * TOK
    D = 1024
    Rp = R["blocks"].shape[1]
    K = R["blocks"].shape[2]
    clips, ncol = R["mod_blk"].shape
    x, dy, hid, dff, qkv, heads = (R[n] for n in ("x", "dy", "hid", "dff", "qkv", "heads"))
    mid, ffn, dh2, wbuf, mod, dmod = (R[n] for n in ("mid", "ffn", "dh2", "wbuf", "mod", "dmod"))
    full = R["full"]
    rows_per_win = TOK // ROWS

    loads = [
        pltpu.make_async_copy(R["x_in"], x, R["in_sem"].at[0]),
        pltpu.make_async_copy(R["dy_in"], dy, R["in_sem"].at[1]),
        pltpu.make_async_copy(R["mod_blk"], R["modx"].at[C - 1], R["in_sem"].at[2]),
    ]
    for copy in loads:
        copy.start()
    p.barrier()
    gather = Gather(p, R["blocks"], full, R["g_s"], R["g_r"])
    scatter = Scatter(
        p, [R["st"].at[0], R["st"].at[1], wbuf.at[0]], R["held"], R["c0"], R["b1"], R["b0"], R["c1"], R["ra"], R["fin"], R["rout"], R["r_s"], R["r_r"], R["f_sem"]
    )

    def mod_c():
        return [
            remote(R["mod_blk"], R["modx"].at[d - 1], R["m_s"].at[d - 1], R["m_r"].at[d - 1], p.dev(c=p.c_peer(d)))
            for d in range(1, C)
        ]

    for copy in mod_c():
        copy.start()
    own = pltpu.make_async_copy(R["blocks"], full.at[:, p.a, p.b, p.k, :, cols(p.c, K)], R["own_sem"].at[0])
    own.start()
    for t in range(LOOKAHEAD):
        gather.first(t)
    spread = Spread(p, R["ms"], R["modf"], "abk", R["m_s"], R["m_r"], C - 1)
    loads[2].wait()
    for copy in mod_c():
        copy.wait_recv()
    total = R["modx"][C - 1]
    for d in range(C - 1):
        total = total + R["modx"][d]
    R["ms"][...] = total
    own_ms = pltpu.make_async_copy(R["ms"], R["modf"].at[p.a, p.b, p.k], R["own_sem"].at[1])
    own_ms.start()
    spread.start(0)
    own.wait()
    gather.slot(0, LOOKAHEAD)
    own_ms.wait()
    spread.landed(0)
    spread.start(1)
    gather.slot(1, LOOKAHEAD)
    spread.landed(1)
    spread.start(2)
    gather.slot(2, LOOKAHEAD)
    spread.landed(2)

    piece = math.gcd(ncol, 128)
    for w in range(2 * A * B):
        blk = R["modf"][w // (2 * B), (w // 2) % B, w % 2]
        for win in range(wins):
            row = jnp.sum(R["pick"][win] * blk, 0, keepdims=True)
            for i in range(ncol // piece):
                col = w * ncol + i * piece
                mod[win * 6 + col // D, :, col % D : col % D + piece] = row[:, i * piece : (i + 1) * piece]
    for copy in loads[:2]:
        copy.wait()

    def rows_loop(fn):
        def run(i):
            win = i // rows_per_win
            fn(pl.ds(pl.multiple_of(i * ROWS, ROWS), ROWS), win * 6)

        loop(T // ROWS, run)

    def make_hidden1():
        def run(rows, m):
            norm, _ = normalize(x[rows, :].astype(f32))
            hid[rows, :] = (norm * (1.0 + mod[m + 1]) + mod[m]).astype(bf16)

        rows_loop(run)

    make_hidden1()
    for i in range(wins * 6):
        dmod[i] = jnp.zeros((1, D), f32)
    loop(HEADS, lambda h: R["zacc"].__setitem__(h, jnp.zeros((32, 128), f32)))

    def weight(t, slot):
        return pltpu.make_async_copy(full.at[t], wbuf.at[slot], R["w_sem"].at[slot])

    for s in (3, 4, 5):
        gather.slot(s, LOOKAHEAD)
        weight(s - 3, s - 3).start()
    for t in range(3):
        weight(t, t).wait()

    def qkv_rows(a, first):
        parts = []
        for b in range(B):
            for k in range(2):
                for t in range(3):
                    parts.append(wbuf[first + t, a, b, k])
        return jnp.concatenate(parts, 0)

    def qkv_cols(a):
        return pl.ds(pl.multiple_of(a * (3 * D // A), 128), 3 * D // A)

    def qkv_step(a):
        qkv[:, qkv_cols(a)] = nt(hid[...], qkv_rows(a, 0)).astype(bf16)

    loop(A, qkv_step)
    gather.slot(6, LOOKAHEAD)
    weight(3, 3).start()

    pairs = D // 128
    low_half = lax.broadcasted_iota(jnp.int32, (TOK, 128), 1) < 64

    def head_refs(i):
        win, pair = i // pairs, lax.rem(i, pairs)
        rows = pl.ds(pl.multiple_of(win * TOK, TOK), TOK)
        spots = [pl.ds(pl.multiple_of(j * D + pair * 128, 128), 128) for j in range(3)]
        return win, pair, rows, spots

    def extended(win, pair, q, k, h):
        own_lanes = low_half if h == 0 else jnp.logical_not(low_half)
        bias = nn(R["uk"][win], R["tmat"][pair * 2 + h]).astype(bf16)
        return own_lanes, jnp.where(own_lanes, q, R["uq"][...]), jnp.where(own_lanes, k, bias)

    def attend(i):
        win, pair, rows, spots = head_refs(i)
        q = qkv[rows, spots[0]] * jnp.asarray(0.125, bf16)
        k, v = qkv[rows, spots[1]], qkv[rows, spots[2]]
        got = []
        for h in range(2):
            _, q_ext, k_ext = extended(win, pair, q, k, h)
            s = nt(q_ext, k_ext)
            e = jnp.exp(s - jnp.max(s, -1, keepdims=True))
            probs = e * (1.0 / jnp.sum(e, -1, keepdims=True))
            got.append(nn(probs.astype(bf16), v))
        heads[rows, spots[0]] = jnp.where(low_half, got[0], got[1]).astype(bf16)
        guard(i == 4, lambda: gather.slot(7, LOOKAHEAD))
        guard(i == 12, lambda: gather.slot(8, LOOKAHEAD))

    loop(wins * pairs, attend)
    weight(4, 0).start()
    weight(5, 1).start()
    weight(3, 3).wait()
    quarter = D // A

    def quarter_cols(a):
        return pl.ds(pl.multiple_of(a * quarter, 128), quarter)

    def out_step(a):
        got = nt(heads[...], wbuf[3, a].reshape(quarter, D))
        at = quarter_cols(a)
        for win in range(wins):
            rows = slice(win * TOK, (win + 1) * TOK)
            mid[rows, at] = x[rows, at].astype(f32) + mod[win * 6 + 2, :, at] * got[rows]

    loop(A, out_step)

    def second_norm(rows, m):
        norm, _ = normalize(mid[rows, :])
        hid[rows, :] = (norm * (1.0 + mod[m + 4]) + mod[m + 3]).astype(bf16)
        dff[rows, :] = (mod[m + 5] * dy[rows, :].astype(f32)).astype(bf16)
        ffn[rows, :] = jnp.zeros((ROWS, D), f32)
        dh2[rows, :] = jnp.zeros((ROWS, D), f32)

    rows_loop(second_norm)

    st = R["st"]
    F = 512

    def ffn_step(s):
        q, hf = s // 2, lax.rem(s, 2)
        su = 2 * lax.rem(q, 2)

        @pl.when(hf == 0)
        def _():
            weight(4 + 2 * q, su).wait()
            weight(5 + 2 * q, su + 1).wait()

        up = wbuf[su, pl.ds(hf * (A // 2), A // 2)].reshape(F, D)
        at = pl.ds(pl.multiple_of(hf * F, F), F)
        down = wbuf[su + 1, :, :, :, :, at].reshape(D, F)
        act, slope = gelu_parts(nt(hid[...], up))
        act = act.astype(bf16)
        ffn[...] += nt(act, down)
        d_pre = (nn(dff[...], down) * slope).astype(bf16)
        dh2[...] += nn(d_pre, up)

        @pl.when(jnp.logical_and(hf == 0, q > 0))
        def _():
            scatter.flush(2 * q - 2, 0)
            scatter.flush(2 * q - 1, 1)

        st[0, pl.ds(hf * (A // 2), A // 2)] = tn(d_pre, hid[...]).astype(bf16).reshape(A // 2, B, 2, Rp, D)
        st[1, :, :, :, :, at] = tn(dff[...], act).astype(bf16).reshape(A, B, 2, Rp, F)

        @pl.when(hf == 1)
        def _():
            scatter.sibling(2 * q, 0).start()
            scatter.sibling(2 * q + 1, 1).start()

        gather.slot(9 + s, LOOKAHEAD)
        scatter.slot(s - 3, 12)

        @pl.when(jnp.logical_and(hf == 1, q < 3))
        def _():
            weight(6 + 2 * q, 2 - su).start()
            weight(7 + 2 * q, 3 - su).start()

    loop(8, ffn_step)
    weight(3, 0).start()
    scatter.flush(6, 0)
    scatter.flush(7, 1)
    weight(0, 1).start()
    weight(1, 2).start()
    weight(2, 3).start()

    def second_back(rows, m):
        norm, inv = normalize(mid[rows, :])
        dyr = dy[rows, :].astype(f32)
        fo = ffn[rows, :]
        dh = dh2[rows, :]
        dmod[m + 5] += jnp.sum(dyr * fo, 0, keepdims=True)
        dmod[m + 3] += jnp.sum(dh, 0, keepdims=True)
        dmod[m + 4] += jnp.sum(dh * norm, 0, keepdims=True)
        dy[rows, :] = (mid[rows, :] + mod[m + 5] * fo).astype(bf16)
        ffn[rows, :] = jnp.zeros((ROWS, D), f32)
        d_mid = dyr + normalize_back(dh * (1.0 + mod[m + 4]), norm, inv)
        dh2[rows, :] = d_mid
        dff[rows, :] = (mod[m + 2] * d_mid).astype(bf16)

    rows_loop(second_back)
    mixed_out = pltpu.make_async_copy(dy, R["mixed"], R["o_sem"].at[0])
    mixed_out.start()
    scatter.slot(5, 12)
    weight(3, 0).wait()

    def out_back(a):
        at = quarter_cols(a)
        wide = wbuf[0, a].reshape(quarter, D)
        attended = nt(heads[...], wide)
        for win in range(wins):
            rows = slice(win * TOK, (win + 1) * TOK)
            dmod[win * 6 + 2, :, at] = jnp.sum(dh2[rows, at] * attended[rows], 0, keepdims=True)
        st[0, a] = tn(dff[:, at], heads[...]).astype(bf16).reshape(B, 2, Rp, D)
        hid[:, at] = nn(dff[...], wbuf[0, :, :, :, :, at].reshape(D, quarter)).astype(bf16)

    loop(A, out_back)
    scatter.sibling(8, 0).start()
    scatter.slot(6, 12)

    def attend_back(i):
        win, pair, rows, spots = head_refs(i)
        q = qkv[rows, spots[0]] * jnp.asarray(0.125, bf16)
        k, v = qkv[rows, spots[1]], qkv[rows, spots[2]]
        do = hid[rows, spots[0]]
        zero = jnp.zeros((TOK, 128), bf16)
        dqs, dks, dvs = [], [], []
        for h in range(2):
            own_lanes, q_ext, k_ext = extended(win, pair, q, k, h)
            s = nt(k_ext, q_ext)
            e = jnp.exp(s - jnp.max(s, 0, keepdims=True))
            probs = e * (1.0 / jnp.sum(e, 0, keepdims=True))
            dvs.append(nn(probs.astype(bf16), do))
            dp = nt(v, jnp.where(own_lanes, do, zero))
            ds = (probs * (dp - jnp.sum(probs * dp, 0, keepdims=True))).astype(bf16)
            dqs.append(tn(ds, k))
            dk = nn(ds, q_ext)
            dks.append(dk)
            bias_part = jnp.where(own_lanes, 0.0, dk)
            top = bias_part.astype(bf16)
            rest = (bias_part - top.astype(f32)).astype(bf16)
            R["zacc"][pair * 2 + h] += nn(R["ut"][...], top) + nn(R["ut"][...], rest)
        qkv[rows, spots[0]] = (jnp.where(low_half, dqs[0], dqs[1]) * 0.125).astype(bf16)
        qkv[rows, spots[1]] = jnp.where(low_half, dks[0], dks[1]).astype(bf16)
        qkv[rows, spots[2]] = jnp.where(low_half, dvs[0], dvs[1]).astype(bf16)
        guard(i == 1, lambda: scatter.flush(8, 0))
        guard(i == 4, lambda: scatter.slot(7, 9))
        guard(i == 7, lambda: scatter.slot(8, 9))
        guard(i == 10, lambda: scatter.slot(9, 9))
        guard(i == 13, lambda: scatter.slot(10, 9))

    loop(wins * pairs, attend_back)
    make_hidden1()
    for t in range(3):
        weight(t, t + 1).wait()

    def qkv_grad(a):
        got = tn(qkv[:, qkv_cols(a)], hid[...]).astype(bf16)
        i = 0
        for b in range(B):
            for k in range(2):
                for t in range(3):
                    scatter.st[t][a, b, k] = got[i * Rp : (i + 1) * Rp]
                    i += 1

    loop(A, qkv_grad)
    for t in range(3):
        scatter.sibling(9 + t, t).start()

    def qkv_back(a):
        ffn[...] += nn(qkv[:, qkv_cols(a)], qkv_rows(a, 1))
        guard(a == 0, lambda: scatter.flush(9, 0))
        guard(a == 1, lambda: scatter.flush(10, 1))
        guard(a == 2, lambda: scatter.flush(11, 2))

    loop(A, qkv_back)
    scatter.mid(9)

    def first_back(rows, m):
        norm, inv = normalize(x[rows, :].astype(f32))
        dh = ffn[rows, :]
        dmod[m] += jnp.sum(dh, 0, keepdims=True)
        dmod[m + 1] += jnp.sum(dh * norm, 0, keepdims=True)
        mid[rows, :] = dh2[rows, :] + normalize_back(dh * (1.0 + mod[m + 1]), norm, inv)

    rows_loop(first_back)
    gx_out = pltpu.make_async_copy(mid, R["gx"], R["o_sem"].at[1])
    gx_out.start()
    filler = (-wins * 6) % 16
    stack = [dmod[i] for i in range(wins * 6)] + [jnp.zeros((1, D), f32)] * filler
    R["dmb"][...] = jnp.concatenate(stack, 0).astype(bf16)
    mods = Spread(p, R["dmb"], R["dmf"], "abck", R["s_s"].at[0], R["s_r"].at[0], 0)
    own_dm = pltpu.make_async_copy(R["dmb"], R["dmf"].at[p.a, p.b, p.k, p.c], R["own_sem"].at[2])
    own_dm.start()
    mods.start(0)
    scatter.mid(10)
    scatter.late(9)

    table = R["ids_row"][...]
    for v in range(21):
        zv = R["zacc"][:, v, :]
        top = zv.astype(bf16)
        rest = (zv - top.astype(f32)).astype(bf16)
        table = table + nn(top, R["selv"][v]) + nn(rest, R["selv"][v])
    R["tb"][...] = table
    tabs = Spread(p, R["tb"], R["tf"], "abck", R["s_s"].at[1], R["s_r"].at[1], 0)
    own_tb = pltpu.make_async_copy(R["tb"], R["tf"].at[p.a, p.b, p.k, p.c], R["own_sem"].at[3])
    own_tb.start()
    tabs.start(0)
    own_dm.wait()
    own_tb.wait()
    for phase in (1, 2, 3):
        for small in (mods, tabs):
            small.landed(phase - 1)
            small.start(phase)
        if phase == 1:
            scatter.mid(11)
            scatter.late(10)
            scatter.last(9)
        if phase == 2:
            scatter.late(11)
            scatter.last(10)
    for small in (mods, tabs):
        small.landed(3)
    scatter.last(11)
    mixed_out.wait()
    gx_out.wait()
    gather.drain()
    scatter.drain()
    for copy in mod_c():
        copy.wait_send()
    for small in (spread, mods, tabs):
        small.drain()


def run_step(dims, wins, ins):
    A, B, C = dims
    blocks = ins[1]
    n, Rp, K = blocks.shape
    clips, ncol = ins[0].shape
    T = wins * TOK
    D = 1024
    h = Rp // 2
    hbm = pl.BlockSpec(memory_space=pltpu.HBM)
    vmem = pl.BlockSpec(memory_space=pltpu.VMEM)
    dm_rows = -(-wins * 6 // 16) * 16
    out_shape = [
        jax.ShapeDtypeStruct((n, A, B, 2, Rp, D), bf16),
        jax.ShapeDtypeStruct((T, D), bf16),
        jax.ShapeDtypeStruct((T, D), f32),
        jax.ShapeDtypeStruct((n, Rp, K), f32),
        jax.ShapeDtypeStruct((A, B, 2, C, dm_rows, D), bf16),
        jax.ShapeDtypeStruct((A, B, 2, C, HEADS, 128), f32),
    ]
    small = A - 1 + B - 1 + C - 1 + 1
    dma = pltpu.SemaphoreType.DMA
    scratch = [
        pltpu.VMEM((T, D), bf16),
        pltpu.VMEM((T, D), bf16),
        pltpu.VMEM((T, D), bf16),
        pltpu.VMEM((T, D), bf16),
        pltpu.VMEM((T, 3 * D), bf16),
        pltpu.VMEM((T, D), bf16),
        pltpu.VMEM((T, D), f32),
        pltpu.VMEM((T, D), f32),
        pltpu.VMEM((T, D), f32),
        pltpu.VMEM((4, A, B, 2, Rp, D), bf16),
        pltpu.VMEM((wins * 6, 1, D), f32),
        pltpu.VMEM((wins * 6, 1, D), f32),
        pltpu.VMEM((C, clips, ncol), f32),
        pltpu.VMEM((A, B, 2, clips, ncol), f32),
        pltpu.VMEM((clips, ncol), f32),
        pltpu.VMEM((HEADS, 32, 128), f32),
        pltpu.VMEM((HEADS, 128), f32),
        pltpu.VMEM((dm_rows, D), bf16),
        pltpu.VMEM((2, A, B, 2, Rp, D), bf16),
        pltpu.VMEM((n, A, B, Rp, D), bf16),
        pltpu.VMEM((n, C - 1, A, B, h, K), bf16),
        pltpu.VMEM((n, B - 1, A, h, D), bf16),
        pltpu.VMEM((n, B - 1, A, h, K), bf16),
        pltpu.VMEM((n, C - 1, A, h, K), bf16),
        pltpu.VMEM((n, A - 1, Rp, K), bf16),
        pltpu.VMEM((2, Rp, K), f32),
        dma((3,)),
        dma((4,)),
        dma((4,)),
        dma((2,)),
        dma((n, Gather.sems(dims))),
        dma((n, Gather.sems(dims))),
        dma((n, Scatter.sems(dims))),
        dma((n, Scatter.sems(dims))),
        dma((2,)),
        dma((C - 1 + small,)),
        dma((C - 1 + small,)),
        dma((2, small)),
        dma((2, small)),
    ]
    return pl.pallas_call(
        functools.partial(step_kernel, dims, wins),
        out_shape=out_shape,
        in_specs=[hbm] * 4 + [vmem] * 7,
        out_specs=[hbm] * 6,
        scratch_shapes=scratch,
        compiler_params=pltpu.CompilerParams(
            collective_id=0, has_side_effects=True, vmem_limit_bytes=63 * 2**20
        ),
        name="block_step",
    )(*ins)


def body(dims, tokens, cotangent, cond, clip_frames, window_clip, window_half, ada, qkv_w, out_w, up_w, down_w, table):
    A, B, C = dims
    W = 2 * A * B
    devices = W * C
    micro, wl, toks, width = tokens.shape
    wins = micro * wl
    clips = cond.shape[0]
    n = lax.axis_index("narrow")
    w = lax.axis_index("wide")
    ids = window_clip.reshape(wins)
    half = window_half.reshape(wins)

    cond_act = jax.nn.silu(cond.astype(f32)).astype(bf16)
    act_rows = lax.dynamic_slice_in_dim(cond_act, n * ada.shape[0], ada.shape[0], 1)
    mod_blk = jnp.dot(act_rows, ada, preferred_element_type=f32)

    Rp = out_w.shape[1]
    K = out_w.shape[0]
    pieces = up_w.shape[1] // Rp
    up_t = up_w.T.reshape(pieces, Rp, K)
    down_t = down_w.reshape(-1, pieces, Rp, Rp).transpose(1, 3, 0, 2).reshape(pieces, Rp, K)
    ffn_t = jnp.stack([up_t, down_t], 1).reshape(2 * pieces, Rp, K)
    blocks = jnp.concatenate([qkv_w.T.reshape(3, Rp, K), out_w.T[None], ffn_t], 0)

    pick = (ids[:, None] == jnp.arange(clips)[None, :]).astype(f32)
    live = jnp.clip(jnp.sum(pick.astype(jnp.int32) * clip_frames[None, :], 1) - WIN_FRAMES * half, 1, WIN_FRAMES)
    feats = position_features()
    uq_const = np.zeros((toks, 128), np.float32)
    for first in (0, 64):
        uq_const[:, first : first + 21] = feats
        uq_const[:, first + 21] = 1
    uk_const = np.zeros((toks, 32), np.float32)
    uk_const[:, :21] = feats
    invalid = (jnp.arange(toks)[None, :] // (WIN_SIDE * WIN_SIDE)) >= live[:, None]
    spot = np.zeros((32,), np.float32)
    spot[21] = 1
    uk = (jnp.asarray(uk_const)[None] + invalid[:, :, None] * jnp.asarray(spot)).astype(bf16)
    sel = offset_selector()
    entries = sel.shape[2]
    spread = np.zeros((entries + 1, 32, 128), np.float32)
    for first in (0, 64):
        spread[:entries, :21, first : first + 21] = sel.transpose(2, 1, 0)
        spread[entries, 21, first + 21] = 1
    rows = jnp.concatenate([table, jnp.full((HEADS, 1), -1e30, bf16)], 1)
    tmat = jnp.dot(rows, jnp.asarray(spread.reshape(entries + 1, -1), bf16), preferred_element_type=f32)
    tmat = tmat.astype(bf16).reshape(HEADS, 32, 128)
    selv = np.zeros((21, 128, 128), np.float32)
    for first in (0, 64):
        selv[:, first : first + 21, :entries] = sel.transpose(1, 0, 2)
    ids_row = jnp.zeros((HEADS, 128), f32).at[0, 128 - wins :].set(ids.astype(f32))

    ins = (
        mod_blk,
        blocks,
        tokens.reshape(wins * toks, width),
        cotangent.reshape(wins * toks, width),
        pick[:, :, None],
        jnp.asarray(uq_const, bf16),
        uk,
        jnp.asarray(uk_const.T, bf16),
        tmat,
        jnp.asarray(selv, bf16),
        ids_row,
    )
    _, mixed, grad_x, rout, mod_grads, table_parts = run_step(dims, wins, ins)

    table_parts = table_parts.reshape(devices, HEADS, 128)
    grad_table = table_parts.sum(0)[:, : table.shape[1]]
    all_ids = table_parts[:, 0, 128 - wins :].reshape(devices, micro, wl).transpose(1, 0, 2).reshape(-1)
    ncol = ada.shape[1]
    dm = mod_grads.reshape(devices, -1, width)[:, : wins * 6].reshape(devices, micro, wl, 6 * width)
    dm = lax.dynamic_slice_in_dim(dm, w * ncol, ncol, 3)
    dm = dm.transpose(1, 0, 2, 3).reshape(-1, ncol)
    picked = (all_ids[:, None] == jnp.arange(clips, dtype=f32)[None, :]).astype(f32)
    by_clip = jnp.einsum("wc,we->ce", picked, dm.astype(f32), precision=highest)
    grad_ada = jnp.einsum("cr,ce->re", act_rows.astype(f32), by_clip, precision=highest)

    ffn_r = rout[: 2 * pieces].reshape(pieces, 2, Rp, K)
    g_up = ffn_r[:, 0].reshape(pieces * Rp, K).T
    g_down = ffn_r[:, 1].reshape(pieces, Rp, -1, Rp).transpose(2, 0, 3, 1).reshape(-1, Rp)
    g_out = rout[2 * pieces].T
    g_qkv = rout[2 * pieces + 1 :].reshape(3 * Rp, K).T
    return (
        mixed.reshape(tokens.shape),
        grad_x.reshape(tokens.shape),
        grad_ada,
        g_qkv,
        g_out,
        g_up,
        g_down,
        grad_table,
    )


def solution(mesh):
    W, C = mesh.shape["wide"], mesh.shape["narrow"]
    A = min(4, W // 2)
    dims = (A, W // 2 // A, C)
    sh = ("wide", "narrow")
    weight = P("narrow", "wide")
    return jax.shard_map(
        functools.partial(body, dims),
        mesh=mesh,
        in_specs=(P(None, sh), P(None, sh), P(), P(), P(None, sh), P(None, sh)) + (weight,) * 5 + (P(),),
        out_specs=(P(None, sh), P(None, sh)) + (weight,) * 5 + (P(),),
        check_vma=False,
    )
```

time: 3470 us -> 339 us (0.10)
  waiting for transfers between devices: 2920 us -> 0 us
  Pallas kernels: 0 us -> 304 us
  matrix products: 227 us -> 5.2 us
  local copies, waits for them, and re-layouts: 155 us -> 17.1 us
  other arithmetic: 93.9 us -> 11.3 us
  blocking collectives: 39.4 us -> 0 us
    all_gather x26 -> x0, waiting for transfers between devices: 1420 us -> none  [the longest x3 286 us: gather_weights(): lax.all_gather(col_full[4], 'narrow', axis=0, tiled=True)]
    reduce_scatter x12 -> x0, waiting for transfers between devices: 1020 us -> none  [the longest x2 284 us: scatter_grads(): lax.psum_scatter(grad_set[0].astype(jnp.bfloat16), 'narrow', scatter_dime...]
    unnamed x54 -> x0, waiting for transfers between devices: 478 us -> none
    pallas_call x0 -> x1, Pallas kernels: none -> 304 us  [run_step(): pl.pallas_call(functools.partial(step_kernel, dims, wins), out_shape=out_...]
    dot_general x46 -> x4, matrix products: 227 us -> 5.2 us  [the longest x1 2.28 us: body(): jnp.einsum('cr,ce->re', act_rows.astype(f32), by_clip, precision=highest)]
    unnamed x190 -> x24, local copies, waits for them, and re-layouts: 73.4 us -> 4.96 us
    add x2 -> x0, local copies, waits for them, and re-layouts: 66.9 us -> none  [the longest x1 34.8 us: build_bias(): along_frame[:, :, None, None, :, None, None]]
    psum x1 -> x0, blocking collectives: 39.4 us -> none  [body(): grad_table = lax.psum(table_grad(bias_total), ('wide', 'narrow'))]
  transfers between devices with their start and end apart: 46 -> 0, of which waited for: 43 -> 0; matrix products, arithmetic and copies ran while one was open for 13% -> 0% of each run, Pallas kernels for 0% -> 0%
where the time goes in v2:
time: 339 us; the launch traced here: 338 us
  Pallas kernels  304 us (90%)
  local copies, waits for them, and re-layouts  17.1 us (5%)
  other arithmetic  11.3 us (3%)
  matrix products  5.2 us (2%)
    pallas_call x1, Pallas kernels, run_step(): pl.pallas_call(functools.partial(step_kernel, dims, wins), out_shape=out_...  304 us

profile of v2, /device:TPU:0, one launch (start us, length us, event | category | flops | bytes accessed | tf_op | source)
XLA Modules:
  0.0 338.0 jit_solution(11649096931030949061)
XLA Ops:
  0.6 0.0 copy-start
  0.6 0.0 copy-start.4
  0.7 0.0 copy-start.5
  0.7 1.4 and_reduce_fusion
  2.0 1.3 fusion.11
  3.4 0.9 fusion.10
  4.2 0.7 fusion.13
  4.9 0.6 fusion.18
  5.5 0.1 compare_convert_fusion
  5.5 1.3 fusion.3.refs_4_
  6.9 1.6 scatter.4.refs_10_
  8.4 0.0 copy-start.8
  8.5 1.3 convert_element_type.47
  9.8 0.0 copy-done
  9.8 1.5 fusion.15.refs_0_
  11.3 1.2 fusion
  12.5 0.7 copy.55
  13.1 1.8 add_convert_fusion.refs_6_
  14.9 0.0 copy-done.5
  14.9 0.1 copy.43
  15.0 0.0 copy-done.4
  15.1 0.5 reshape.222
  15.6 0.1 copy.59
  15.7 0.0 copy-done.8
  15.7 0.0 copy-start.6
  15.7 0.0 copy-start.7
  15.7 0.3 stack_reshape.7
  16.0 0.1 pad_maximum_fusion.1
  16.1 0.5 copy-done.6
  16.6 0.0 copy-done.7
  16.6 0.9 pad_maximum_fusion.refs_1_
  17.6 303.6 %block_step.1 = (bf16[12,4,2,2,64,1024]{5,4,3,2,1,0:T(8,128)(2,1)}, bf16[640,1024]{1,0:T(8,128)(2,1)}, f32[640,1024]{1,0:T(8,128)}, f32[12,64,512]{2,1,0:T(8,128...) custom-call(f32[8,384]{1,0:T(8,128)} %fusion.15.refs_0_, ...), custom_call_target="tpu_custom_call" | custom-call | tf_op jit(solution)/shard_map/block_step/pallas_call | solution.py:903
  321.2 1.6 reduce_sum.22
  322.7 1.0 slice.56
  323.7 0.1 copy.53
  323.8 0.1 eq.50
  323.9 1.6 slice_bitcast_fusion
  325.5 1.8 slice.50
  327.3 1.3 slice.52
  328.6 0.1 fusion.17
  328.7 1.0 copy.52
  329.7 0.2 reshape_squeeze.11
  329.9 0.0 copy-start.3
  329.9 0.7 copy.58
  330.6 1.6 reshape.238
  332.1 0.0 copy-done.3
  332.1 0.0 copy-start.2
  332.1 0.7 reshape.234
  332.9 0.2 fusion.1
  333.1 0.0 copy-start.1
  333.1 2.3 fusion.16
  335.4 0.0 copy-done.2
  335.4 1.1 copy.63
  336.5 0.0 copy-done.1
  336.5 1.5 copy.64
  (6 shorter events, 0.1 us)
Async XLA Ops:
  0.6 9.2 %copy-start = (bf16[512,384]{1,0:T(8,128)(2,1)S(1)}, bf16[512,384]{1,0:T(8,128)(2,1)}, u32[]{:S(2)}) copy-start(bf16[512,384]{1,0:T(8,128)(2,1)} %param.26) | copy-start | bytes 1179652
  0.6 14.4 %copy-start.4 = (bf16[2048,64]{0,1:T(8,128)(2,1)S(1)}, bf16[2048,64]{0,1:T(8,128)(2,1)}, u32[]{:S(2)}) copy-start(bf16[2048,64]{0,1:T(8,128)(2,1)} %param.30) | copy-start | bytes 786436
  0.7 14.2 %copy-start.5 = (bf16[512,256]{1,0:T(8,128)(2,1)S(1)}, bf16[512,256]{1,0:T(8,128)(2,1)}, u32[]{:S(2)}) copy-start(bf16[512,256]{1,0:T(8,128)(2,1)} %param.29) | copy-start | bytes 786436
  8.4 7.2 %copy-start.8 = (f32[16,128]{1,0:T(8,128)}, f32[16,128]{1,0:T(8,128)S(1)}, u32[]{:S(2)}) copy-start(f32[16,128]{1,0:T(8,128)S(1)} %scatter.4.refs_10_) | copy-start | bytes 24580
  15.7 0.9 copy-start.6
  15.7 0.9 copy-start.7
  329.9 2.3 copy-start.3
  332.1 3.3 copy-start.2
  333.1 3.3 copy-start.1

commit v3 on v2

v3 whole, which is shorter than its diff:
```python
import functools
import math

import jax
import jax.numpy as jnp
import numpy as np
from jax import lax
from jax.experimental import pallas as pl
from jax.experimental.pallas import tpu as pltpu
from jax.sharding import PartitionSpec as P

HEADS = 16
WIN_FRAMES = 5
WIN_SIDE = 8
TOK = WIN_FRAMES * WIN_SIDE * WIN_SIDE
F_SPAN = 2 * WIN_FRAMES - 1
S_SPAN = 2 * WIN_SIDE - 1
epsilon = 1e-06
inv_root_two = 0.7071067811865476
inv_root_tau = 0.3989422804014327
highest = lax.Precision.HIGHEST
MESH = pl.DeviceIdType.MESH
bf16 = jnp.bfloat16
f32 = jnp.float32


def position_features():
    p = np.arange(TOK)
    feats = np.zeros((TOK, WIN_FRAMES + 2 * WIN_SIDE), np.float32)
    feats[p, p // 64] = 1
    feats[p, WIN_FRAMES + (p // 8) % 8] = 1
    feats[p, WIN_FRAMES + WIN_SIDE + p % 8] = 1
    return feats


def offset_selector():
    sel = np.zeros((21, 21, F_SPAN + 2 * S_SPAN), np.float32)
    for i in range(WIN_FRAMES):
        for j in range(WIN_FRAMES):
            sel[i, j, i - j + WIN_FRAMES - 1] = 1
    for i in range(WIN_SIDE):
        for j in range(WIN_SIDE):
            sel[5 + i, 5 + j, F_SPAN + i - j + WIN_SIDE - 1] = 1
            sel[13 + i, 13 + j, F_SPAN + S_SPAN + i - j + WIN_SIDE - 1] = 1
    return sel


def nt(lhs, rhs):
    return lax.dot_general(lhs, rhs, (((1,), (1,)), ((), ())), preferred_element_type=f32)


def nn(lhs, rhs):
    return lax.dot_general(lhs, rhs, (((1,), (0,)), ((), ())), preferred_element_type=f32)


def tn(lhs, rhs):
    return lax.dot_general(lhs, rhs, (((0,), (0,)), ((), ())), preferred_element_type=f32)


def normalize(values):
    centre = jnp.mean(values, -1, keepdims=True)
    shifted = values - centre
    inv_std = lax.rsqrt(jnp.mean(shifted * shifted, -1, keepdims=True) + epsilon)
    return shifted * inv_std, inv_std


def normalize_back(grad_norm, normed, inv_std):
    return inv_std * (
        grad_norm
        - jnp.mean(grad_norm, -1, keepdims=True)
        - normed * jnp.mean(grad_norm * normed, -1, keepdims=True)
    )


def gelu_parts(pre):
    gate = 0.5 * (1.0 + lax.erf(pre * inv_root_two))
    return pre * gate, gate + pre * inv_root_tau * jnp.exp(-0.5 * pre * pre)


def guard(cond, fn):
    if isinstance(cond, bool):
        if cond:
            fn()
    else:
        pl.when(cond)(fn)


def both(*conds):
    total = True
    for cond in conds:
        if isinstance(cond, bool):
            if not cond:
                return False
        elif total is True:
            total = cond
        else:
            total = jnp.logical_and(total, cond)
    return total


def loop(count, fn):
    def step(i, carry):
        fn(i)
        return carry

    lax.fori_loop(0, count, step, 0)


def cols(c, K):
    return pl.ds(pl.multiple_of(c * K, K), K)


class Place:
    def __init__(self, dims):
        self.A, self.B, self.C = dims
        w = lax.axis_index("wide")
        self.c = lax.axis_index("narrow")
        self.k = lax.rem(w, 2)
        self.b = lax.rem(w // 2, self.B)
        self.a = w // (2 * self.B)

    def dev(self, a=None, b=None, k=None, c=None):
        a = self.a if a is None else a
        b = self.b if b is None else b
        k = self.k if k is None else k
        c = self.c if c is None else c
        return ((a * self.B + b) * 2 + k, c)

    def a_peer(self, d):
        return lax.rem(self.a + d, self.A)

    def b_peer(self, d):
        return lax.rem(self.b + d, self.B)

    def c_peer(self, d):
        return lax.rem(self.c + d, self.C)

    def barrier(self):
        peers = [self.dev(a=self.a_peer(d)) for d in range(1, self.A)]
        peers += [self.dev(b=self.b_peer(d)) for d in range(1, self.B)]
        peers += [self.dev(c=self.c_peer(d)) for d in range(1, self.C)]
        peers += [self.dev(k=1 - self.k)]
        sem = pltpu.get_barrier_semaphore()
        for peer in peers:
            pl.semaphore_signal(sem, inc=1, device_id=peer, device_id_type=MESH)
        pl.semaphore_wait(sem, len(peers))


def remote(src, dst, ssem, rsem, dev):
    return pltpu.make_async_remote_copy(
        src_ref=src, dst_ref=dst, send_sem=ssem, recv_sem=rsem, device_id=dev, device_id_type=MESH
    )


def peers_along(p, axis):
    if axis == "a":
        return [(p.a_peer(d), p.dev(a=p.a_peer(d))) for d in range(1, p.A)]
    if axis == "b":
        return [(p.b_peer(d), p.dev(b=p.b_peer(d))) for d in range(1, p.B)]
    return [(p.c_peer(d), p.dev(c=p.c_peer(d))) for d in range(1, p.C)]


def every_nth(t, n, spot):
    return t % n == spot if isinstance(t, int) else lax.rem(t, n) == spot


def by_kind(kind, fn):
    if isinstance(kind, bool):
        fn(kind)
    else:
        pl.when(kind)(lambda: fn(True))
        pl.when(jnp.logical_not(kind))(lambda: fn(False))


class Gather:
    ORDERS = {False: ("abc", "acb"), True: ("bac", "cab")}

    def __init__(self, place, blocks, full, ssem, rsem):
        self.p, self.blocks, self.full, self.ssem, self.rsem = place, blocks, full, ssem, rsem
        self.Rp, self.K = blocks.shape[1], blocks.shape[2]
        self.count = blocks.shape[0]
        self.size = {"a": place.A - 1, "b": place.B - 1, "c": place.C - 1}

    @staticmethod
    def kind(t):
        return every_nth(t, 2, 1)

    @staticmethod
    def sems(dims):
        A, B, C = dims
        return 2 * (A - 1 + B - 1 + C - 1) + 1 + 2

    def region(self, t, order, phase, half, a):
        p = self.p
        done = order[:phase]
        every = slice(None)
        return self.full.at[
            t,
            every if "a" in done else a,
            every if "b" in done else p.b,
            p.k,
            pl.ds(half * (self.Rp // 2), self.Rp // 2),
            every if "c" in done else cols(p.c, self.K),
        ]

    def copies(self, t, mixed, phase, half=0):
        p = self.p
        if phase == 3:
            s = 2 * sum(self.size.values())
            ref = self.full.at[t, :, :, p.k]
            return [(True, remote(ref, ref, self.ssem.at[t, s], self.rsem.at[t, s], p.dev(k=1 - p.k)))]
        order = self.ORDERS[mixed][half]
        done, axis = order[:phase], order[phase]
        ref = self.region(t, order, phase, half, p.a)
        src = self.blocks.at[t, pl.ds(half * (self.Rp // 2), self.Rp // 2), :] if phase == 0 else ref
        base = half * sum(self.size.values()) + sum(self.size[x] for x in done)
        made = []
        for i, (_, dev) in enumerate(peers_along(p, axis)):
            when = True
            if axis == "a" and i == 0:
                when = p.a != p.A - 1
            if axis == "a" and i == p.A - 2:
                when = p.a != 0
            made.append((when, remote(src, ref, self.ssem.at[t, base + i], self.rsem.at[t, base + i], dev)))
        return made

    def relays(self, t, mixed, phase, half):
        p = self.p
        order = self.ORDERS[mixed][half]
        if phase == 3 or order[phase] != "a":
            return []
        base = half * sum(self.size.values()) + sum(self.size[x] for x in order[:phase])
        ref = self.region(t, order, phase, half, p.a_peer(2))
        s = 2 * sum(self.size.values()) + 1 + half
        return [
            (p.a == near, remote(ref, ref, self.ssem.at[t, s], self.rsem.at[t, base + spot], p.dev(a=end)))
            for near, end, spot in ((2, 3, 2), (1, 0, 0))
        ]

    def start(self, t, mixed, phase, half=0):
        for when, copy in self.copies(t, mixed, phase, half):
            guard(when, copy.start)

    def landed(self, t, mixed, phase, half=0):
        copies = [copy for _, copy in self.copies(t, mixed, phase, half)]
        relays = self.relays(t, mixed, phase, half)
        if relays:
            copies[1].wait_recv()
            for when, copy in relays:
                guard(when, copy.start)
            copies = [copies[0]] + copies[2:]
        for copy in copies:
            copy.wait_recv()

    def first(self, t):
        def run(mixed):
            for half in (0, 1):
                self.start(t, mixed, 0, half)

        by_kind(self.kind(t), run)

    def slot(self, s, ahead):
        n = self.count

        def advance(t, phase):
            def run(mixed):
                for half in (0, 1):
                    self.landed(t, mixed, phase - 1, half)
                    if phase < 3:
                        self.start(t, mixed, phase, half)
                if phase == 3:
                    self.start(t, mixed, 3)

            guard(both(t >= 0, t < n), lambda: by_kind(self.kind(t), run))

        guard(s + ahead < n, lambda: self.first(s + ahead))
        for phase in (1, 2, 3):
            advance(s - phase + 1, phase)
        guard(both(s - 3 >= 0, s - 3 < n), lambda: self.landed(s - 3, False, 3))

    def drain(self):
        def one(t):
            def run(mixed):
                for phase in range(4):
                    for half in (0, 1) if phase < 3 else (0,):
                        for when, copy in self.copies(t, mixed, phase, half) + self.relays(t, mixed, phase, half):
                            guard(when, copy.wait_send)

            by_kind(self.kind(t), run)

        loop(self.count, one)


class Scatter:
    ORDERS = ("cba", "bca")

    def __init__(self, place, st, held, boxes, fin, out, ssem, rsem, fsem):
        self.p, self.st, self.held, self.boxes = place, st, held, boxes
        self.fin, self.out = fin, out
        self.ssem, self.rsem, self.fsem = ssem, rsem, fsem
        self.Rp, self.K = fin.shape[1], fin.shape[2]
        self.count = held.shape[0]
        self.size = {"a": place.A - 1, "b": place.B - 1, "c": place.C - 1}

    @staticmethod
    def sems(dims):
        A, B, C = dims
        return 1 + 2 * (A - 1 + B - 1 + C - 1)

    @classmethod
    def box_shapes(cls, dims, count, Rp, K):
        A, B, C = dims
        shapes = []
        for order in cls.ORDERS:
            for phase in range(3):
                left = order[phase + 1 :]
                lead = ((A,) if "a" in left else ()) + ((B,) if "b" in left else ())
                wide = C * K if "c" in left else K
                shapes.append((count, {"a": A, "b": B, "c": C}[order[phase]] - 1) + lead + (Rp // 2, wide))
        return shapes

    def box(self, r, half, phase):
        return self.boxes[3 * half + phase].at[r]

    def sibling(self, r, slot):
        p = self.p
        return remote(
            self.st[slot].at[:, :, 1 - p.k], self.held.at[r], self.ssem.at[r, 0], self.rsem.at[r, 0], p.dev(k=1 - p.k)
        )

    def sibling_part(self, r, slot, a):
        p = self.p
        return remote(
            self.st[slot].at[a, :, 1 - p.k],
            self.held.at[r, a],
            self.ssem.at[r, 0],
            self.rsem.at[r, 0],
            p.dev(k=1 - p.k),
        )

    def region(self, r, half, done, axis=None, peer=None):
        p = self.p
        every = slice(None)
        a = p.a if "a" in done else every
        b = p.b if "b" in done else every
        c = cols(p.c, self.K) if "c" in done else every
        if axis == "a":
            a = peer
        if axis == "b":
            b = peer
        if axis == "c":
            c = cols(peer, self.K)
        return r, a, b, pl.ds(half * (self.Rp // 2), self.Rp // 2), c

    def copies(self, r, half, phase):
        p = self.p
        order = self.ORDERS[half]
        done, axis = order[:phase], order[phase]
        base = 1 + half * sum(self.size.values()) + sum(self.size[x] for x in done)
        box = self.box(r, half, phase)
        return [
            remote(
                self.held.at[self.region(r, half, done, axis, peer)],
                box.at[i],
                self.ssem.at[r, base + i],
                self.rsem.at[r, base + i],
                dev,
            )
            for i, (peer, dev) in enumerate(peers_along(p, axis))
        ]

    def start(self, r, half, phase):
        for copy in self.copies(r, half, phase):
            copy.start()

    def add(self, r, half, phase):
        p = self.p
        order = self.ORDERS[half]
        for copy in self.copies(r, half, phase):
            copy.wait_recv()
        left = order[phase + 1 :]
        box = self.box(r, half, phase)
        _, a, b, rows, c = self.region(r, half, order[: phase + 1])
        count = self.size[order[phase]]

        def one(i):
            if "a" in left and "b" in left:
                lead = (i // p.B, lax.rem(i, p.B))
                spot = (r,) + lead + (rows, c)
            elif left[:1] == "a" or "a" in left:
                lead = (i,)
                spot = (r, i, b, rows, c)
            elif "b" in left:
                lead = (i,)
                spot = (r, a, i, rows, c)
            else:
                lead = ()
                spot = (r, a, b, rows, c)
            total = self.held[spot]
            for d in range(count):
                total = total + box[(d,) + lead]
            self.held[spot] = total

        trips = (p.A if "a" in left else 1) * (p.B if "b" in left else 1)
        if trips == 1:
            one(0)
        else:
            loop(trips, one)

    def flush(self, r, slot):
        p = self.p
        copy = self.sibling(r, slot)
        copy.wait_recv()

        def add(i):
            a, b = i // p.B, lax.rem(i, p.B)
            self.held[r, a, b] = self.held[r, a, b] + self.st[slot][a, b, p.k]

        loop(p.A * p.B, add)
        copy.wait_send()

    def begin(self, r):
        for half in (0, 1):
            self.start(r, half, 0)

    def step(self, r, phase):
        for half in (0, 1):
            self.add(r, half, phase)
            self.start(r, half, phase + 1)

    def mid(self, r):
        self.step(r, 0)

    def late(self, r):
        self.step(r, 1)

    def result(self, r):
        s = lax.rem(r, 2)
        return pltpu.make_async_copy(self.fin.at[s], self.out.at[r], self.fsem.at[s])

    def last(self, r):
        p = self.p
        guard(r >= 2, lambda: self.result(r - 2).wait())
        h = self.Rp // 2

        for half in (0, 1):
            for copy in self.copies(r, half, 2):
                copy.wait_recv()
            box = self.box(r, half, 2)
            total = self.held[self.region(r, half, "abc")].astype(f32)
            for d in range(self.size[self.ORDERS[half][2]]):
                total = total + box[d].astype(f32)
            self.fin[lax.rem(r, 2), half * h : (half + 1) * h] = total

        self.result(r).start()

    def tick(self, j):
        n = self.count
        guard(both(j >= 0, j < n), lambda: self.begin(j))
        guard(both(j >= 1, j - 1 < n), lambda: self.mid(j - 1))
        guard(both(j >= 2, j - 2 < n), lambda: self.late(j - 2))
        guard(both(j >= 3, j - 3 < n), lambda: self.last(j - 3))

    def drain(self):
        def one(r):
            for half in (0, 1):
                for phase in range(3):
                    for copy in self.copies(r, half, phase):
                        copy.wait_send()

        loop(self.count, one)
        for r in (self.count - 2, self.count - 1):
            self.result(r).wait()


class Spread:
    def __init__(self, place, block, full, axes, ssem, rsem, base):
        p = place
        self.p, self.block, self.full, self.axes = p, block, full, axes
        self.ssem, self.rsem, self.base = ssem, rsem, base

    def copies(self, phase):
        p = self.p
        with_c = "c" in self.axes
        tail = (p.c,) if with_c else ()
        axis = self.axes[phase]
        base = self.base
        for done in self.axes[:phase]:
            base += {"a": p.A - 1, "b": p.B - 1, "c": p.C - 1, "k": 1}[done]
        every = slice(None)
        done = self.axes[:phase]
        index = (
            every if "a" in done else p.a,
            every if "b" in done else p.b,
            every if "k" in done else p.k,
        )
        if with_c:
            index += (every if "c" in done else p.c,)
        dst = self.full.at[index]
        src = self.block if phase == 0 else dst
        made = []
        count = {"a": p.A, "b": p.B, "c": p.C, "k": 2}[axis]
        for d in range(1, count):
            dev = {
                "a": lambda: p.dev(a=p.a_peer(d)),
                "b": lambda: p.dev(b=p.b_peer(d)),
                "c": lambda: p.dev(c=p.c_peer(d)),
                "k": lambda: p.dev(k=1 - p.k),
            }[axis]()
            s = base + d - 1
            made.append(remote(src, dst, self.ssem.at[s], self.rsem.at[s], dev))
        return made

    def start(self, phase):
        for copy in self.copies(phase):
            copy.start()

    def landed(self, phase):
        for copy in self.copies(phase):
            copy.wait_recv()

    def drain(self):
        for phase in range(len(self.axes)):
            for copy in self.copies(phase):
                copy.wait_send()


LOOKAHEAD = 1
ROWS = 160
LOADED = (
    "blocks", "x", "dy", "cond", "ada", "uq", "uk_const", "ut", "selv", "table",
)
NAMES_IN = (
    "ids", "halves", "frames", "blocks_in", "x_in", "dy_in", "cond_in", "ada_in", "uq_in", "uk_const_in",
    "ut_in", "selv_in", "table_in",
)
NAMES_OUT = (
    "full", "mixed", "gx", "rout", "dmf", "tf",
)
NAMES_SCRATCH = (
    "blocks", "x", "dy", "cond", "ada", "uq", "uk_const", "ut", "selv", "table", "hid", "dff", "qkv", "heads",
    "mid", "ffn", "dh2", "wbuf", "mod", "dmod", "modx", "modf", "ms", "zacc", "tmat", "uk", "tb", "dmb", "st",
    "held", "box0", "box1", "box2", "box3", "box4", "box5",
    "fin", "in_sem", "w_sem", "own_sem", "o_sem", "g_s", "g_r", "r_s", "r_r", "f_sem", "m_s", "m_r", "s_s",
    "s_r",
)


def step_kernel(dims, wins, *refs):
    names = NAMES_IN + NAMES_OUT + NAMES_SCRATCH
    R = dict(zip(names, refs))
    p = Place(dims)
    A, B, C = dims
    T = wins * TOK
    D = 1024
    Rp = R["blocks"].shape[1]
    K = R["blocks"].shape[2]
    clips, ncol = R["cond"].shape[0], R["ada"].shape[1]
    x, dy, hid, dff, qkv, heads = (R[n] for n in ("x", "dy", "hid", "dff", "qkv", "heads"))
    mid, ffn, dh2, wbuf, mod, dmod = (R[n] for n in ("mid", "ffn", "dh2", "wbuf", "mod", "dmod"))
    full = R["full"]
    rows_per_win = TOK // ROWS

    loads = {
        name: pltpu.make_async_copy(R[name + "_in"], R[name], R["in_sem"].at[i]) for i, name in enumerate(LOADED)
    }
    for copy in loads.values():
        copy.start()
    p.barrier()
    gather = Gather(p, R["blocks"], full, R["g_s"], R["g_r"])
    scatter = Scatter(
        p, [R["st"].at[0], R["st"].at[1], wbuf.at[0]], R["held"], [R[f"box{i}"] for i in range(6)],
        R["fin"], R["rout"], R["r_s"], R["r_r"], R["f_sem"],
    )
    loads["blocks"].wait()
    gather.first(0)
    own = pltpu.make_async_copy(R["blocks"], full.at[:, p.a, p.b, p.k, :, cols(p.c, K)], R["own_sem"].at[0])
    own.start()

    def mod_c():
        return [
            remote(R["modx"].at[C - 1], R["modx"].at[d - 1], R["m_s"].at[d - 1], R["m_r"].at[d - 1], p.dev(c=p.c_peer(d)))
            for d in range(1, C)
        ]

    loads["cond"].wait()
    loads["ada"].wait()
    act_rows = jax.nn.silu(R["cond"][:, cols(p.c, R["ada"].shape[0])].astype(f32)).astype(bf16)
    R["modx"][C - 1] = nn(act_rows, R["ada"][...])
    for copy in mod_c():
        copy.start()
    spread = Spread(p, R["ms"], R["modf"], "abk", R["m_s"], R["m_r"], C - 1)

    for name in ("selv", "table", "uk_const", "uq", "ut", "x", "dy"):
        loads[name].wait()
    lanes = lax.broadcasted_iota(jnp.int32, (1, 128), 1)
    away = jnp.where(lanes == 21, -1e30, 0.0)
    for v in range(32):
        row = nt(R["table"][...], R["selv"][v]) if v < 21 else jnp.broadcast_to(away if v == 21 else away * 0.0, (HEADS, 128))
        R["zacc"][v * HEADS : (v + 1) * HEADS] = row
    for copy in mod_c():
        copy.wait_recv()
    total = R["modx"][C - 1]
    for d in range(C - 1):
        total = total + R["modx"][d]
    R["ms"][...] = total
    own_ms = pltpu.make_async_copy(R["ms"], R["modf"].at[p.a, p.b, p.k], R["own_sem"].at[1])
    own_ms.start()
    spread.start(0)
    own.wait()
    gather.slot(0, LOOKAHEAD)
    for h in range(HEADS):
        R["tmat"][h] = R["zacc"][pl.ds(h, 32, stride=HEADS), :].astype(bf16)
    own_ms.wait()
    spread.landed(0)
    spread.start(1)
    gather.slot(1, LOOKAHEAD)
    spread.landed(1)
    spread.start(2)
    frame = lax.broadcasted_iota(jnp.int32, (TOK, 128), 0) // (WIN_SIDE * WIN_SIDE)
    flag = lax.broadcasted_iota(jnp.int32, (TOK, 128), 1) == 21
    for win in range(wins):
        live = jnp.clip(R["frames"][R["ids"][win]] - WIN_FRAMES * R["halves"][win], 1, WIN_FRAMES)
        hide = jnp.logical_and(flag, frame >= live)
        R["uk"][win] = jnp.where(hide, 1.0, R["uk_const"][...].astype(f32)).astype(bf16)
    gather.slot(2, LOOKAHEAD)
    spread.landed(2)

    def weight(t, slot):
        return pltpu.make_async_copy(full.at[t], wbuf.at[slot], R["w_sem"].at[slot])

    gather.slot(3, LOOKAHEAD)
    weight(0, 0).start()
    piece = math.gcd(ncol, 128)
    clip_iota = lax.broadcasted_iota(jnp.int32, (clips, ncol), 0)
    for w in range(2 * A * B):
        blk = R["modf"][w // (2 * B), (w // 2) % B, w % 2]
        for win in range(wins):
            row = jnp.sum(jnp.where(clip_iota == R["ids"][win], blk, 0.0), 0, keepdims=True)
            for i in range(ncol // piece):
                col = w * ncol + i * piece
                mod[win * 6 + col // D, :, col % D : col % D + piece] = row[:, i * piece : (i + 1) * piece]
    gather.slot(4, LOOKAHEAD)
    weight(1, 1).start()

    def rows_loop(fn, also={}):
        def run(i):
            win = i // rows_per_win
            fn(pl.ds(pl.multiple_of(i * ROWS, ROWS), ROWS), win * 6)
            for at, extra in also.items():
                guard(i == at, extra)

        loop(T // ROWS, run)

    def make_hidden1():
        def run(rows, m):
            norm, _ = normalize(x[rows, :].astype(f32))
            hid[rows, :] = (norm * (1.0 + mod[m + 1]) + mod[m]).astype(bf16)

        rows_loop(run)

    make_hidden1()
    for i in range(wins * 6):
        dmod[i] = jnp.zeros((1, D), f32)
    R["zacc"][...] = jnp.zeros((HEADS * 32, 128), f32)

    gather.slot(5, LOOKAHEAD)
    weight(2, 2).start()
    for t in range(3):
        weight(t, t).wait()

    def qkv_rows(a, first):
        parts = []
        for b in range(B):
            for k in range(2):
                for t in range(3):
                    parts.append(wbuf[first + t, a, b, k])
        return jnp.concatenate(parts, 0)

    def qkv_cols(a):
        return pl.ds(pl.multiple_of(a * (3 * D // A), 128), 3 * D // A)

    def qkv_step(a):
        qkv[:, qkv_cols(a)] = nt(hid[...], qkv_rows(a, 0)).astype(bf16)

    loop(A, qkv_step)
    gather.slot(6, LOOKAHEAD)
    weight(3, 3).start()

    pairs = D // 128
    low_half = lax.broadcasted_iota(jnp.int32, (TOK, 128), 1) < 64

    def head_refs(i):
        win, pair = i // pairs, lax.rem(i, pairs)
        rows = pl.ds(pl.multiple_of(win * TOK, TOK), TOK)
        spots = [pl.ds(pl.multiple_of(j * D + pair * 128, 128), 128) for j in range(3)]
        return win, pair, rows, spots

    def two_heads(value):
        zero = jnp.zeros_like(value)
        return jnp.concatenate([jnp.where(low_half, value, zero), jnp.where(low_half, zero, value)], 0)

    def one_pair(value):
        return jnp.where(low_half, value[:TOK], value[TOK:])

    def attend(i):
        win, pair, rows, spots = head_refs(i)
        q = qkv[rows, spots[0]] * jnp.asarray(0.125, bf16)
        k, v = qkv[rows, spots[1]], qkv[rows, spots[2]]
        filler = jnp.zeros((96, 128), bf16)
        spread_rows = jnp.concatenate([R["tmat"][pair * 2], filler, R["tmat"][pair * 2 + 1], filler], 0)
        bias = nt(R["uq"][...], spread_rows).astype(bf16)
        bias = jnp.concatenate([bias[:, :128], bias[:, 128:]], 0)
        s = nt(jnp.concatenate([two_heads(q), bias], 1), jnp.concatenate([k, R["uk"][win]], 1))
        e = jnp.exp(s - jnp.max(s, -1, keepdims=True))
        probs = e * (1.0 / jnp.sum(e, -1, keepdims=True))
        heads[rows, spots[0]] = one_pair(nn(probs.astype(bf16), v)).astype(bf16)
        guard(i == 3, lambda: gather.slot(7, LOOKAHEAD))
        guard(i == 9, lambda: gather.slot(8, LOOKAHEAD))

    loop(wins * pairs, attend)
    weight(4, 0).start()
    weight(5, 1).start()
    weight(3, 3).wait()
    quarter = D // A

    def quarter_cols(a):
        return pl.ds(pl.multiple_of(a * quarter, 128), quarter)

    def out_step(a):
        got = nt(heads[...], wbuf[3, a].reshape(quarter, D))
        at = quarter_cols(a)
        for win in range(wins):
            rows = slice(win * TOK, (win + 1) * TOK)
            mid[rows, at] = x[rows, at].astype(f32) + mod[win * 6 + 2, :, at] * got[rows]

    gather.slot(9, LOOKAHEAD)
    loop(A, out_step)

    def second_norm(rows, m):
        norm, _ = normalize(mid[rows, :])
        hid[rows, :] = (norm * (1.0 + mod[m + 4]) + mod[m + 3]).astype(bf16)
        dff[rows, :] = (mod[m + 5] * dy[rows, :].astype(f32)).astype(bf16)
        ffn[rows, :] = jnp.zeros((ROWS, D), f32)
        dh2[rows, :] = jnp.zeros((ROWS, D), f32)

    rows_loop(second_norm)

    st = R["st"]
    F = 512

    def ffn_step(s):
        q, hf = s // 2, lax.rem(s, 2)
        su = 2 * lax.rem(q, 2)

        @pl.when(hf == 0)
        def _():
            weight(4 + 2 * q, su).wait()
            weight(5 + 2 * q, su + 1).wait()

        up = wbuf[su, pl.ds(hf * (A // 2), A // 2)].reshape(F, D)
        at = pl.ds(pl.multiple_of(hf * F, F), F)
        down = wbuf[su + 1, :, :, :, :, at].reshape(D, F)
        act, slope = gelu_parts(nt(hid[...], up))
        act = act.astype(bf16)
        ffn[...] += nt(act, down)
        d_pre = (nn(dff[...], down) * slope).astype(bf16)
        dh2[...] += nn(d_pre, up)

        @pl.when(jnp.logical_and(hf == 0, q > 0))
        def _():
            scatter.flush(2 * q - 2, 0)
            scatter.flush(2 * q - 1, 1)

        st[0, pl.ds(hf * (A // 2), A // 2)] = tn(d_pre, hid[...]).astype(bf16).reshape(A // 2, B, 2, Rp, D)
        st[1, :, :, :, :, at] = tn(dff[...], act).astype(bf16).reshape(A, B, 2, Rp, F)

        @pl.when(hf == 1)
        def _():
            scatter.sibling(2 * q, 0).start()
            scatter.sibling(2 * q + 1, 1).start()

        gather.slot(10 + s, LOOKAHEAD)
        guard(s == 4, lambda: scatter.tick(0))
        guard(s == 5, lambda: scatter.tick(1))
        guard(s == 7, lambda: scatter.tick(2))

        @pl.when(jnp.logical_and(hf == 0, q < 3))
        def _():
            weight(6 + 2 * q, 2 - su).start()
            weight(7 + 2 * q, 3 - su).start()

    loop(8, ffn_step)
    weight(3, 0).start()
    weight(0, 1).start()
    weight(1, 2).start()
    weight(2, 3).start()

    def second_back(rows, m):
        norm, inv = normalize(mid[rows, :])
        dyr = dy[rows, :].astype(f32)
        fo = ffn[rows, :]
        dh = dh2[rows, :]
        dmod[m + 5] += jnp.sum(dyr * fo, 0, keepdims=True)
        dmod[m + 3] += jnp.sum(dh, 0, keepdims=True)
        dmod[m + 4] += jnp.sum(dh * norm, 0, keepdims=True)
        dy[rows, :] = (mid[rows, :] + mod[m + 5] * fo).astype(bf16)
        ffn[rows, :] = jnp.zeros((ROWS, D), f32)
        d_mid = dyr + normalize_back(dh * (1.0 + mod[m + 4]), norm, inv)
        dh2[rows, :] = d_mid
        dff[rows, :] = (mod[m + 2] * d_mid).astype(bf16)

    rows_loop(second_back)
    mixed_out = pltpu.make_async_copy(dy, R["mixed"], R["o_sem"].at[0])
    mixed_out.start()
    scatter.flush(6, 0)
    scatter.flush(7, 1)
    scatter.tick(3)
    weight(3, 0).wait()

    def out_back(a):
        at = quarter_cols(a)
        wide = wbuf[0, a].reshape(quarter, D)
        attended = nt(heads[...], wide)
        for win in range(wins):
            rows = slice(win * TOK, (win + 1) * TOK)
            dmod[win * 6 + 2, :, at] = jnp.sum(dh2[rows, at] * attended[rows], 0, keepdims=True)
        st[0, a] = tn(dff[:, at], heads[...]).astype(bf16).reshape(B, 2, Rp, D)
        scatter.sibling_part(8, 0, a).start()
        hid[:, at] = nn(dff[...], wbuf[0, :, :, :, :, at].reshape(D, quarter)).astype(bf16)

    loop(A, out_back)
    scatter.tick(4)

    def attend_back(i):
        win, pair, rows, spots = head_refs(i)
        q = qkv[rows, spots[0]] * jnp.asarray(0.125, bf16)
        k, v = qkv[rows, spots[1]], qkv[rows, spots[2]]
        do = hid[rows, spots[0]]
        kk = two_heads(k)
        bias = nn(R["uk"][win][:, :32], jnp.concatenate([R["tmat"][pair * 2], R["tmat"][pair * 2 + 1]], 1)).astype(bf16)
        bias = jnp.concatenate([bias[:, :128], bias[:, 128:]], 0)
        query = jnp.concatenate([q, R["uq"][...]], 1)
        s = nt(jnp.concatenate([kk, bias], 1), query)
        dp = nt(two_heads(v), do)
        probs, ds = [], []
        for h in range(2):
            sh, dph = s[h * TOK : (h + 1) * TOK], dp[h * TOK : (h + 1) * TOK]
            e = jnp.exp(sh - jnp.max(sh, 0, keepdims=True))
            ph = e * (1.0 / jnp.sum(e, 0, keepdims=True))
            probs.append(ph.astype(bf16))
            ds.append((ph * (dph - jnp.sum(ph * dph, 0, keepdims=True))).astype(bf16))
        probs = jnp.concatenate(probs, 0)
        ds = jnp.concatenate(ds, 0)
        dk = nn(ds, query)
        qkv[rows, spots[0]] = (tn(ds, kk) * 0.125).astype(bf16)
        qkv[rows, spots[1]] = one_pair(dk[:, :128]).astype(bf16)
        qkv[rows, spots[2]] = one_pair(nn(probs, do)).astype(bf16)
        bias_part = jnp.concatenate([dk[:TOK, 128:], dk[TOK:, 128:]], 1)
        top = bias_part.astype(bf16)
        rest = (bias_part - top.astype(f32)).astype(bf16)
        z = nn(R["ut"][...], top) + nn(R["ut"][...], rest)
        for h in range(2):
            R["zacc"][pl.ds(pl.multiple_of((pair * 2 + h) * 32, 32), 32), :] += z[:, h * 128 : (h + 1) * 128]
        guard(i == 1, lambda: scatter.flush(8, 0))
        guard(i == 3, lambda: scatter.tick(5))
        guard(i == 7, lambda: scatter.tick(6))
        guard(i == 11, lambda: scatter.tick(7))
        guard(i == 15, lambda: scatter.tick(8))

    loop(wins * pairs, attend_back)
    make_hidden1()
    for t in range(3):
        weight(t, t + 1).wait()

    def qkv_grad(a):
        got = tn(qkv[:, qkv_cols(a)], hid[...]).astype(bf16)
        i = 0
        for b in range(B):
            for k in range(2):
                for t in range(3):
                    scatter.st[t][a, b, k] = got[i * Rp : (i + 1) * Rp]
                    i += 1
        for t in range(3):
            scatter.sibling_part(9 + t, t, a).start()

    loop(A, qkv_grad)
    scatter.flush(9, 0)
    scatter.tick(9)
    scatter.flush(10, 1)
    scatter.flush(11, 2)

    def qkv_back(a):
        ffn[...] += nn(qkv[:, qkv_cols(a)], qkv_rows(a, 1))

    loop(A, qkv_back)
    scatter.tick(10)

    def first_back(rows, m):
        norm, inv = normalize(x[rows, :].astype(f32))
        dh = ffn[rows, :]
        dmod[m] += jnp.sum(dh, 0, keepdims=True)
        dmod[m + 1] += jnp.sum(dh * norm, 0, keepdims=True)
        mid[rows, :] = dh2[rows, :] + normalize_back(dh * (1.0 + mod[m + 1]), norm, inv)

    rows_loop(first_back)
    scatter.tick(11)
    gx_out = pltpu.make_async_copy(mid, R["gx"], R["o_sem"].at[1])
    gx_out.start()
    filler = (-wins * 6) % 16
    stack = [dmod[i] for i in range(wins * 6)] + [jnp.zeros((1, D), f32)] * filler
    R["dmb"][...] = jnp.concatenate(stack, 0).astype(bf16)
    mods = Spread(p, R["dmb"], R["dmf"], "abck", R["s_s"].at[0], R["s_r"].at[0], 0)
    own_dm = pltpu.make_async_copy(R["dmb"], R["dmf"].at[p.a, p.b, p.k, p.c], R["own_sem"].at[2])
    own_dm.start()
    mods.start(0)

    lane = lax.broadcasted_iota(jnp.int32, (HEADS, 128), 1)
    table = jnp.zeros((HEADS, 128), f32)
    for win in range(wins):
        table = jnp.where(lane == 128 - wins + win, R["ids"][win].astype(f32), table)
    for v in range(21):
        zv = R["zacc"][pl.ds(v, HEADS, stride=32), :]
        top = zv.astype(bf16)
        rest = (zv - top.astype(f32)).astype(bf16)
        table = table + nn(top, R["selv"][v]) + nn(rest, R["selv"][v])
    R["tb"][...] = table
    tabs = Spread(p, R["tb"], R["tf"], "abck", R["s_s"].at[1], R["s_r"].at[1], 0)
    own_tb = pltpu.make_async_copy(R["tb"], R["tf"].at[p.a, p.b, p.k, p.c], R["own_sem"].at[3])
    own_tb.start()
    tabs.start(0)
    own_dm.wait()
    own_tb.wait()
    for phase in (1, 2, 3):
        for small in (mods, tabs):
            small.landed(phase - 1)
            small.start(phase)
        if phase == 2:
            scatter.tick(12)
    for small in (mods, tabs):
        small.landed(3)
    scatter.tick(13)
    scatter.tick(14)
    mixed_out.wait()
    gx_out.wait()
    gather.drain()
    scatter.drain()
    for copy in mod_c():
        copy.wait_send()
    for small in (spread, mods, tabs):
        small.drain()


def run_step(dims, wins, ins):
    A, B, C = dims
    n, Rp, K = ins[3].shape
    clips, ncol = ins[6].shape[0], ins[7].shape[1]
    T = wins * TOK
    D = 1024
    hbm = pl.BlockSpec(memory_space=pltpu.HBM)
    smem = pl.BlockSpec(memory_space=pltpu.SMEM)
    dm_rows = -(-wins * 6 // 16) * 16
    out_shape = [
        jax.ShapeDtypeStruct((n, A, B, 2, Rp, D), bf16),
        jax.ShapeDtypeStruct((T, D), bf16),
        jax.ShapeDtypeStruct((T, D), f32),
        jax.ShapeDtypeStruct((n, Rp, K), f32),
        jax.ShapeDtypeStruct((A, B, 2, C, dm_rows, D), bf16),
        jax.ShapeDtypeStruct((A, B, 2, C, HEADS, 128), f32),
    ]
    small = A - 1 + B - 1 + C - 1 + 1
    dma = pltpu.SemaphoreType.DMA
    scratch = [
        *[pltpu.VMEM(v.shape, v.dtype) for v in ins[3:]],
        pltpu.VMEM((T, D), bf16),
        pltpu.VMEM((T, D), bf16),
        pltpu.VMEM((T, 3 * D), bf16),
        pltpu.VMEM((T, D), bf16),
        pltpu.VMEM((T, D), f32),
        pltpu.VMEM((T, D), f32),
        pltpu.VMEM((T, D), f32),
        pltpu.VMEM((4, A, B, 2, Rp, D), bf16),
        pltpu.VMEM((wins * 6, 1, D), f32),
        pltpu.VMEM((wins * 6, 1, D), f32),
        pltpu.VMEM((C, clips, ncol), f32),
        pltpu.VMEM((A, B, 2, clips, ncol), f32),
        pltpu.VMEM((clips, ncol), f32),
        pltpu.VMEM((HEADS * 32, 128), f32),
        pltpu.VMEM((HEADS, 32, 128), bf16),
        pltpu.VMEM((wins, TOK, 128), bf16),
        pltpu.VMEM((HEADS, 128), f32),
        pltpu.VMEM((dm_rows, D), bf16),
        pltpu.VMEM((2, A, B, 2, Rp, D), bf16),
        pltpu.VMEM((n, A, B, Rp, D), bf16),
        *[pltpu.VMEM(shape, bf16) for shape in Scatter.box_shapes(dims, n, Rp, K)],
        pltpu.VMEM((2, Rp, K), f32),
        dma((len(LOADED),)),
        dma((4,)),
        dma((4,)),
        dma((2,)),
        dma((n, Gather.sems(dims))),
        dma((n, Gather.sems(dims))),
        dma((n, Scatter.sems(dims))),
        dma((n, Scatter.sems(dims))),
        dma((2,)),
        dma((C - 1 + small,)),
        dma((C - 1 + small,)),
        dma((2, small)),
        dma((2, small)),
    ]
    return pl.pallas_call(
        functools.partial(step_kernel, dims, wins),
        out_shape=out_shape,
        in_specs=[smem] * 3 + [hbm] * 10,
        out_specs=[hbm] * 6,
        scratch_shapes=scratch,
        compiler_params=pltpu.CompilerParams(
            collective_id=0, has_side_effects=True, vmem_limit_bytes=66 * 10**6 + 2**19
        ),
        name="block_step",
    )(*ins)


def body(dims, tokens, cotangent, cond, clip_frames, window_clip, window_half, ada, qkv_w, out_w, up_w, down_w, table):
    A, B, C = dims
    W = 2 * A * B
    devices = W * C
    micro, wl, toks, width = tokens.shape
    wins = micro * wl
    clips = cond.shape[0]
    n = lax.axis_index("narrow")
    w = lax.axis_index("wide")
    ids = window_clip.reshape(wins)
    half = window_half.reshape(wins)

    Rp = out_w.shape[1]
    K = out_w.shape[0]
    pieces = up_w.shape[1] // Rp
    up_t = up_w.T.reshape(pieces, Rp, K)
    down_t = down_w.reshape(-1, pieces, Rp, Rp).transpose(1, 3, 0, 2).reshape(pieces, Rp, K)
    ffn_t = jnp.stack([up_t, down_t], 1).reshape(2 * pieces, Rp, K)
    blocks = jnp.concatenate([qkv_w.T.reshape(3, Rp, K), out_w.T[None], ffn_t], 0)

    feats = position_features()
    uq_const = np.zeros((toks, 128), np.float32)
    uq_const[:, :21] = feats
    uq_const[:, 21] = 1
    uk_const = np.zeros((toks, 128), np.float32)
    uk_const[:, :21] = feats
    sel = offset_selector()
    entries = sel.shape[2]
    selv = np.zeros((21, 128, 128), np.float32)
    selv[:, :21, :entries] = sel.transpose(1, 0, 2)
    ins = (
        ids,
        half,
        clip_frames,
        blocks,
        tokens.reshape(wins * toks, width),
        cotangent.reshape(wins * toks, width),
        cond,
        ada,
        jnp.asarray(uq_const, bf16),
        jnp.asarray(uk_const, bf16),
        jnp.asarray(uk_const[:, :32].T, bf16),
        jnp.asarray(selv, bf16),
        jnp.pad(table, ((0, 0), (0, 128 - table.shape[1]))),
    )
    _, mixed, grad_x, rout, mod_grads, table_parts = run_step(dims, wins, ins)

    table_parts = table_parts.reshape(devices, HEADS, 128)
    grad_table = table_parts.sum(0)[:, : table.shape[1]]
    all_ids = table_parts[:, 0, 128 - wins :].reshape(devices, micro, wl).transpose(1, 0, 2).reshape(-1)
    ncol = ada.shape[1]
    dm = mod_grads.reshape(devices, -1, width)[:, : wins * 6].reshape(devices, micro, wl, 6 * width)
    dm = lax.dynamic_slice_in_dim(dm, w * ncol, ncol, 3)
    dm = dm.transpose(1, 0, 2, 3).reshape(-1, ncol)
    picked = (all_ids[:, None] == jnp.arange(clips, dtype=f32)[None, :]).astype(f32)
    cond_act = jax.nn.silu(cond.astype(f32)).astype(bf16)
    act_rows = lax.dynamic_slice_in_dim(cond_act, n * ada.shape[0], ada.shape[0], 1)
    by_clip = jnp.einsum("wc,we->ce", picked, dm.astype(f32), precision=highest)
    grad_ada = jnp.einsum("cr,ce->re", act_rows.astype(f32), by_clip, precision=highest)

    ffn_r = rout[: 2 * pieces].reshape(pieces, 2, Rp, K)
    g_up = ffn_r[:, 0].reshape(pieces * Rp, K).T
    g_down = ffn_r[:, 1].reshape(pieces, Rp, -1, Rp).transpose(2, 0, 3, 1).reshape(-1, Rp)
    g_out = rout[2 * pieces].T
    g_qkv = rout[2 * pieces + 1 :].reshape(3 * Rp, K).T
    return (
        mixed.reshape(tokens.shape),
        grad_x.reshape(tokens.shape),
        grad_ada,
        g_qkv,
        g_out,
        g_up,
        g_down,
        grad_table,
    )


def solution(mesh):
    W, C = mesh.shape["wide"], mesh.shape["narrow"]
    A = min(4, W // 2)
    dims = (A, W // 2 // A, C)
    sh = ("wide", "narrow")
    weight = P("narrow", "wide")
    return jax.shard_map(
        functools.partial(body, dims),
        mesh=mesh,
        in_specs=(P(None, sh), P(None, sh), P(), P(), P(None, sh), P(None, sh)) + (weight,) * 5 + (P(),),
        out_specs=(P(None, sh), P(None, sh)) + (weight,) * 5 + (P(),),
        check_vma=False,
    )
```

time: 339 us -> 283 us (0.83)
  Pallas kernels: 304 us -> 263 us
  other arithmetic: 11.3 us -> 1.64 us
  matrix products: 5.2 us -> 1.68 us
    pallas_call x1, Pallas kernels: 304 us -> 263 us  [run_step(): pl.pallas_call(functools.partial(step_kernel, dims, wins), out_shape=out_...]
where the time goes in v3:
time: 283 us; the launch traced here: 282 us
  Pallas kernels  263 us (93%)
  local copies, waits for them, and re-layouts  15.2 us (5%)
    pallas_call x1, Pallas kernels, run_step(): pl.pallas_call(functools.partial(step_kernel, dims, wins), out_shape=out_...  263 us
    unnamed x21, local copies, waits for them, and re-layouts  5.68 us

profile of v3, /device:TPU:0, one launch (start us, length us, event | category | flops | bytes accessed | tf_op | source)
XLA Modules:
  0.0 282.2 jit_solution(12394578490653229703)
XLA Ops:
  0.6 0.0 copy-start.3
  0.6 1.5 reshape.68
  2.2 0.1 copy.46
  2.2 0.0 copy-start.4
  2.2 0.0 copy-start.6
  2.3 0.3 stack_reshape.7
  2.6 0.0 copy-done.3
  2.6 0.1 copy.31
  2.7 0.1 pad_maximum_fusion.1
  2.8 0.0 copy-start.7
  2.9 0.3 copy-done.4
  3.2 0.0 copy-done.6
  3.2 0.9 pad_maximum_fusion.refs_3_
  4.1 0.0 copy-done.7
  4.1 0.6 pad.4.refs_12_
  4.7 262.9 %block_step.1 = (bf16[12,4,2,2,64,1024]{5,4,3,2,1,0:T(8,128)(2,1)}, bf16[640,1024]{1,0:T(8,128)(2,1)}, f32[640,1024]{1,0:T(8,128)}, f32[12,64,512]{2,1,0:T(8,128...) custom-call(s32[2]{0:T(128)} %bitcast.79, s32[2]{0:T(128)} %bitcast.80, s32[8]{0:T(128)} %refs_2_.1, ...), custom_call_target="tpu_custom_call" | custom-call | tf_op jit(solution)/shard_map/block_step/pallas_call | solution.py:1011
  267.6 0.0 copy-start.2
  267.6 0.0 copy-start.5
  267.6 0.0 copy-start.1
  267.6 2.7 reshape.76
  270.4 0.0 copy-done.2
  270.4 0.1 slice.32
  270.5 0.1 copy.41
  270.6 0.1 eq.15
  270.6 0.3 fusion
  270.9 0.0 copy-done.5
  270.9 1.4 fusion.2
  272.3 0.0 copy-done.1
  272.3 0.8 slice.26
  273.1 0.7 slice_bitcast_fusion
  273.8 0.1 slice.28
  273.9 0.1 fusion.6
  274.0 1.0 copy.40
  275.0 0.2 reshape_squeeze.11
  275.2 0.7 copy.45
  275.9 1.6 reshape.80
  277.5 0.0 copy-start
  277.5 0.6 reduce_sum.9
  278.1 2.6 copy.49
  280.7 0.0 copy-done
  280.7 1.5 copy.50
  (4 shorter events, 0.1 us)
Async XLA Ops:
  0.6 2.0 copy-start.3
  2.2 0.9 copy-start.4
  2.2 0.9 copy-start.6
  2.8 1.3 copy-start.7
  267.6 2.8 copy-start.2
  267.6 3.3 %copy-start.5 = (bf16[8,1024]{1,0:T(8,128)(2,1)S(1)}, bf16[8,1024]{1,0:T(8,128)(2,1)}, u32[]{:S(2)}) copy-start(bf16[8,1024]{1,0:T(8,128)(2,1)} %refs_6_.1) | copy-start | bytes 49156
  267.6 4.7 %copy-start.1 = (f32[12,64,512]{2,1,0:T(8,128)S(1)}, f32[12,64,512]{2,1,0:T(8,128)}, u32[]{:S(2)}) copy-start(f32[12,64,512]{2,1,0:T(8,128)} %get-tuple-element.17) | copy-start | bytes 4718596
  277.5 3.3 %copy-start = (f32[640,1024]{1,0:T(8,128)S(1)}, f32[640,1024]{1,0:T(8,128)}, u32[]{:S(2)}) copy-start(f32[640,1024]{1,0:T(8,128)} %get-tuple-element.14) | copy-start | bytes 7864324

commit v4 on v3

--- a/solution.py
+++ b/solution.py
@@ -454,23 +454,29 @@
 
         self.result(r).start()
 
-    def tick(self, j):
-        n = self.count
-        guard(both(j >= 0, j < n), lambda: self.begin(j))
-        guard(both(j >= 1, j - 1 < n), lambda: self.mid(j - 1))
-        guard(both(j >= 2, j - 2 < n), lambda: self.late(j - 2))
-        guard(both(j >= 3, j - 3 < n), lambda: self.last(j - 3))
-
-    def drain(self):
-        def one(r):
+    def step_of(self, kind, r):
+        if kind == 4:
+            self.flush(r, r % 2 if r < 8 else max(0, r - 9))
+        else:
+            (self.begin, self.mid, self.late, self.last)[kind](r)
+
+    def steps(self, *names):
+        for what in names:
+            self.step_of(*what)
+
+    def at(self, index, table):
+        for spot, names in table.items():
+            guard(index == spot, functools.partial(self.steps, *names))
+
+    def drain(self, first, count):
+        def one(i):
+            r = first + i
             for half in (0, 1):
                 for phase in range(3):
                     for copy in self.copies(r, half, phase):
                         copy.wait_send()
 
-        loop(self.count, one)
-        for r in (self.count - 2, self.count - 1):
-            self.result(r).wait()
+        loop(count, one)
 
 
 class Spread:
@@ -525,92 +531,186 @@
                 copy.wait_send()
 
 
+class Fold:
+    ORDER = "kbac"
+
+    def __init__(self, place, parts, boxes, total, ssem, rsem):
+        self.p, self.parts, self.boxes, self.total, self.ssem, self.rsem = place, parts, boxes, total, ssem, rsem
+
+    def peers(self, axis):
+        p = self.p
+        return [(1 - p.k, p.dev(k=1 - p.k))] if axis == "k" else peers_along(p, axis)
+
+    def region(self, phase, peer=None):
+        p = self.p
+        every = slice(None)
+        done = self.ORDER[: phase + 1]
+        mine = {"a": p.a, "b": p.b, "k": p.k}
+        if peer is not None and self.ORDER[phase] != "c":
+            mine[self.ORDER[phase]] = peer
+        return tuple(mine[x] if x in done else every for x in "abk")
+
+    def copies(self, phase):
+        base = sum(len(self.peers(x)) for x in self.ORDER[:phase])
+        return [
+            remote(
+                self.parts.at[self.region(phase, peer)],
+                self.boxes[phase].at[i],
+                self.ssem.at[base + i],
+                self.rsem.at[base + i],
+                dev,
+            )
+            for i, (peer, dev) in enumerate(self.peers(self.ORDER[phase]))
+        ]
+
+    def start(self, phase):
+        for copy in self.copies(phase):
+            copy.start()
+
+    def add(self, phase):
+        copies = self.copies(phase)
+        for copy in copies:
+            copy.wait_recv()
+        spot = self.region(phase)
+        got = self.parts[spot]
+        for i in range(len(copies)):
+            got = got + self.boxes[phase][i]
+        if self.ORDER[phase] == "c":
+            self.total[...] = got
+        else:
+            self.parts[spot] = got
+
+    def drain(self):
+        for phase in range(4):
+            for copy in self.copies(phase):
+                copy.wait_send()
+
+
 LOOKAHEAD = 1
-ROWS = 160
-LOADED = (
-    "blocks", "x", "dy", "cond", "ada", "uq", "uk_const", "ut", "selv", "table",
-)
-NAMES_IN = (
-    "ids", "halves", "frames", "blocks_in", "x_in", "dy_in", "cond_in", "ada_in", "uq_in", "uk_const_in",
-    "ut_in", "selv_in", "table_in",
-)
-NAMES_OUT = (
-    "full", "mixed", "gx", "rout", "dmf", "tf",
-)
-NAMES_SCRATCH = (
-    "blocks", "x", "dy", "cond", "ada", "uq", "uk_const", "ut", "selv", "table", "hid", "dff", "qkv", "heads",
-    "mid", "ffn", "dh2", "wbuf", "mod", "dmod", "modx", "modf", "ms", "zacc", "tmat", "uk", "tb", "dmb", "st",
-    "held", "box0", "box1", "box2", "box3", "box4", "box5",
-    "fin", "in_sem", "w_sem", "own_sem", "o_sem", "g_s", "g_r", "r_s", "r_r", "f_sem", "m_s", "m_r", "s_s",
-    "s_r",
-)
+ROWS = {True: 160, False: 64}
+def begin(r):
+    return 0, r
+
+
+def middle(r):
+    return 1, r
+
+
+def late(r):
+    return 2, r
+
+
+def end(r):
+    return 3, r
+
+
+def part(r):
+    return 4, r
+
+
+FFN_EARLY = {4: (begin(1),), 5: (begin(2), late(0)), 6: (begin(3), late(1)), 7: (begin(4), late(2))}
+FFN_LATE = {3: (begin(0),), 4: (middle(0),), 5: (middle(1),), 6: (middle(2), end(0)), 7: (middle(3), end(1))}
+SECOND_BACK = {0: (begin(5),), 1: (late(3),), 2: (middle(4),), 3: (end(2),)}
+OUT_BACK = {0: (begin(6),), 1: (late(4),), 2: (middle(5),), 3: (end(3),)}
+ATTEND_BACK = {
+    0: (part(8),), 1: (begin(7),), 3: (late(5),), 4: (middle(6),), 5: (end(4),), 7: (begin(8),), 9: (late(6),), 10: (middle(7),), 11: (end(5),), 13: (late(7),), 15: (middle(8),),
+}
+HIDDEN = {2: (end(6),)}
+QKV_GRAD = {1: (late(8),), 3: (end(7),)}
+QKV_BACK = {2: (begin(10),), 3: (end(8),)}
+AFTER_QKV = (middle(9),)
+FIRST_BACK = {0: (begin(11),), 1: (late(9),)}
+AFTER_FIRST = (middle(10),)
+HOPS = ((late(10), middle(11)), (end(9), late(11)), (end(10), end(11)))
+ENDING = ()
 
 
 def step_kernel(dims, wins, *refs):
-    names = NAMES_IN + NAMES_OUT + NAMES_SCRATCH
-    R = dict(zip(names, refs))
+    (
+        r_ids, r_halves, r_frames, r_blocks_in, r_x_in, r_dy_in, r_cond_in, r_ada_in, r_uq_in, r_uk_const_in, r_ut_in,
+        r_selv_in, r_table_in, r_full, r_mixed, r_gx, r_rout, r_by_clip, r_tf, r_blocks, r_x, r_dy, r_cond, r_ada, r_uq,
+        r_uk_const, r_ut, r_selv, r_table, r_hid, r_dff, r_qkv, r_heads, r_mid, r_ffn, r_dh2, r_wbuf, r_mod, r_dmod,
+        r_modx, r_modf, r_ms, r_zacc, r_tmat, r_uk, r_tb, r_fold0, r_fold1, r_fold2, r_fold3, r_cl, r_st, r_held,
+        r_box0, r_box1, r_box2, r_box3, r_box4, r_box5, r_fin, r_in_sem, r_w_sem, r_own_sem, r_o_sem, r_g_s, r_g_r,
+        r_r_s, r_r_r, r_f_sem, r_m_s, r_m_r, r_s_s, r_s_r,
+    ) = refs
     p = Place(dims)
     A, B, C = dims
     T = wins * TOK
     D = 1024
-    Rp = R["blocks"].shape[1]
-    K = R["blocks"].shape[2]
-    clips, ncol = R["cond"].shape[0], R["ada"].shape[1]
-    x, dy, hid, dff, qkv, heads = (R[n] for n in ("x", "dy", "hid", "dff", "qkv", "heads"))
-    mid, ffn, dh2, wbuf, mod, dmod = (R[n] for n in ("mid", "ffn", "dh2", "wbuf", "mod", "dmod"))
-    full = R["full"]
-    rows_per_win = TOK // ROWS
-
-    loads = {
-        name: pltpu.make_async_copy(R[name + "_in"], R[name], R["in_sem"].at[i]) for i, name in enumerate(LOADED)
-    }
-    for copy in loads.values():
+    Rp = r_blocks.shape[1]
+    K = r_blocks.shape[2]
+    clips, ncol = r_cond.shape[0], r_ada.shape[1]
+    x, dy, hid, dff, qkv, heads = r_x, r_dy, r_hid, r_dff, r_qkv, r_heads
+    mid, ffn, dh2, wbuf, mod, dmod = r_mid, r_ffn, r_dh2, r_wbuf, r_mod, r_dmod
+    full = r_full
+    at_once = ROWS[C <= 2]
+    rows_per_win = TOK // at_once
+
+    loads = [
+        pltpu.make_async_copy(src, dst, r_in_sem.at[i])
+        for i, (src, dst) in enumerate(
+            (
+                (r_blocks_in, r_blocks),
+                (r_x_in, r_x),
+                (r_dy_in, r_dy),
+                (r_cond_in, r_cond),
+                (r_ada_in, r_ada),
+                (r_uq_in, r_uq),
+                (r_uk_const_in, r_uk_const),
+                (r_ut_in, r_ut),
+                (r_selv_in, r_selv),
+                (r_table_in, r_table),
+            )
+        )
+    ]
+    for copy in loads:
         copy.start()
     p.barrier()
-    gather = Gather(p, R["blocks"], full, R["g_s"], R["g_r"])
+    gather = Gather(p, r_blocks, full, r_g_s, r_g_r)
     scatter = Scatter(
-        p, [R["st"].at[0], R["st"].at[1], wbuf.at[0]], R["held"], [R[f"box{i}"] for i in range(6)],
-        R["fin"], R["rout"], R["r_s"], R["r_r"], R["f_sem"],
+        p, [r_st.at[0], r_st.at[1], wbuf.at[0]], r_held, [r_box0, r_box1, r_box2, r_box3, r_box4, r_box5],
+        r_fin, r_rout, r_r_s, r_r_r, r_f_sem,
     )
-    loads["blocks"].wait()
+    loads[0].wait()
     gather.first(0)
-    own = pltpu.make_async_copy(R["blocks"], full.at[:, p.a, p.b, p.k, :, cols(p.c, K)], R["own_sem"].at[0])
+    own = pltpu.make_async_copy(r_blocks, full.at[:, p.a, p.b, p.k, :, cols(p.c, K)], r_own_sem.at[0])
     own.start()
 
     def mod_c():
         return [
-            remote(R["modx"].at[C - 1], R["modx"].at[d - 1], R["m_s"].at[d - 1], R["m_r"].at[d - 1], p.dev(c=p.c_peer(d)))
+            remote(r_modx.at[C - 1], r_modx.at[d - 1], r_m_s.at[d - 1], r_m_r.at[d - 1], p.dev(c=p.c_peer(d)))
             for d in range(1, C)
         ]
 
-    loads["cond"].wait()
-    loads["ada"].wait()
-    act_rows = jax.nn.silu(R["cond"][:, cols(p.c, R["ada"].shape[0])].astype(f32)).astype(bf16)
-    R["modx"][C - 1] = nn(act_rows, R["ada"][...])
+    loads[3].wait()
+    loads[4].wait()
+    act_rows = jax.nn.silu(r_cond[:, cols(p.c, r_ada.shape[0])].astype(f32)).astype(bf16)
+    r_modx[C - 1] = nn(act_rows, r_ada[...])
     for copy in mod_c():
         copy.start()
-    spread = Spread(p, R["ms"], R["modf"], "abk", R["m_s"], R["m_r"], C - 1)
-
-    for name in ("selv", "table", "uk_const", "uq", "ut", "x", "dy"):
-        loads[name].wait()
+    spread = Spread(p, r_ms, r_modf, "abk", r_m_s, r_m_r, C - 1)
+
+    for i in (8, 9, 6, 5, 7, 1, 2):
+        loads[i].wait()
     lanes = lax.broadcasted_iota(jnp.int32, (1, 128), 1)
     away = jnp.where(lanes == 21, -1e30, 0.0)
     for v in range(32):
-        row = nt(R["table"][...], R["selv"][v]) if v < 21 else jnp.broadcast_to(away if v == 21 else away * 0.0, (HEADS, 128))
-        R["zacc"][v * HEADS : (v + 1) * HEADS] = row
+        row = nt(r_table[...], r_selv[v]) if v < 21 else jnp.broadcast_to(away if v == 21 else away * 0.0, (HEADS, 128))
+        r_zacc[v * HEADS : (v + 1) * HEADS] = row
     for copy in mod_c():
         copy.wait_recv()
-    total = R["modx"][C - 1]
+    total = r_modx[C - 1]
     for d in range(C - 1):
-        total = total + R["modx"][d]
-    R["ms"][...] = total
-    own_ms = pltpu.make_async_copy(R["ms"], R["modf"].at[p.a, p.b, p.k], R["own_sem"].at[1])
+        total = total + r_modx[d]
+    r_ms[...] = total
+    own_ms = pltpu.make_async_copy(r_ms, r_modf.at[p.a, p.b, p.k], r_own_sem.at[1])
     own_ms.start()
     spread.start(0)
     own.wait()
     gather.slot(0, LOOKAHEAD)
     for h in range(HEADS):
-        R["tmat"][h] = R["zacc"][pl.ds(h, 32, stride=HEADS), :].astype(bf16)
+        r_tmat[h] = r_zacc[pl.ds(h, 32, stride=HEADS), :].astype(bf16)
     own_ms.wait()
     spread.landed(0)
     spread.start(1)
@@ -620,23 +720,23 @@
     frame = lax.broadcasted_iota(jnp.int32, (TOK, 128), 0) // (WIN_SIDE * WIN_SIDE)
     flag = lax.broadcasted_iota(jnp.int32, (TOK, 128), 1) == 21
     for win in range(wins):
-        live = jnp.clip(R["frames"][R["ids"][win]] - WIN_FRAMES * R["halves"][win], 1, WIN_FRAMES)
+        live = jnp.clip(r_frames[r_ids[win]] - WIN_FRAMES * r_halves[win], 1, WIN_FRAMES)
         hide = jnp.logical_and(flag, frame >= live)
-        R["uk"][win] = jnp.where(hide, 1.0, R["uk_const"][...].astype(f32)).astype(bf16)
+        r_uk[win] = jnp.where(hide, 1.0, r_uk_const[...].astype(f32)).astype(bf16)
     gather.slot(2, LOOKAHEAD)
     spread.landed(2)
 
     def weight(t, slot):
-        return pltpu.make_async_copy(full.at[t], wbuf.at[slot], R["w_sem"].at[slot])
+        return pltpu.make_async_copy(full.at[t], wbuf.at[slot], r_w_sem.at[slot])
 
     gather.slot(3, LOOKAHEAD)
     weight(0, 0).start()
     piece = math.gcd(ncol, 128)
     clip_iota = lax.broadcasted_iota(jnp.int32, (clips, ncol), 0)
     for w in range(2 * A * B):
-        blk = R["modf"][w // (2 * B), (w // 2) % B, w % 2]
+        blk = r_modf[w // (2 * B), (w // 2) % B, w % 2]
         for win in range(wins):
-            row = jnp.sum(jnp.where(clip_iota == R["ids"][win], blk, 0.0), 0, keepdims=True)
+            row = jnp.sum(jnp.where(clip_iota == r_ids[win], blk, 0.0), 0, keepdims=True)
             for i in range(ncol // piece):
                 col = w * ncol + i * piece
                 mod[win * 6 + col // D, :, col % D : col % D + piece] = row[:, i * piece : (i + 1) * piece]
@@ -646,23 +746,22 @@
     def rows_loop(fn, also={}):
         def run(i):
             win = i // rows_per_win
-            fn(pl.ds(pl.multiple_of(i * ROWS, ROWS), ROWS), win * 6)
-            for at, extra in also.items():
-                guard(i == at, extra)
-
-        loop(T // ROWS, run)
-
-    def make_hidden1():
+            fn(pl.ds(pl.multiple_of(i * at_once, at_once), at_once), win * 6)
+            scatter.at(i, also)
+
+        loop(T // at_once, run)
+
+    def make_hidden1(also={}):
         def run(rows, m):
             norm, _ = normalize(x[rows, :].astype(f32))
             hid[rows, :] = (norm * (1.0 + mod[m + 1]) + mod[m]).astype(bf16)
 
-        rows_loop(run)
+        rows_loop(run, also)
 
     make_hidden1()
     for i in range(wins * 6):
         dmod[i] = jnp.zeros((1, D), f32)
-    R["zacc"][...] = jnp.zeros((HEADS * 32, 128), f32)
+    r_zacc[...] = jnp.zeros((HEADS * 32, 128), f32)
 
     gather.slot(5, LOOKAHEAD)
     weight(2, 2).start()
@@ -708,10 +807,10 @@
         q = qkv[rows, spots[0]] * jnp.asarray(0.125, bf16)
         k, v = qkv[rows, spots[1]], qkv[rows, spots[2]]
         filler = jnp.zeros((96, 128), bf16)
-        spread_rows = jnp.concatenate([R["tmat"][pair * 2], filler, R["tmat"][pair * 2 + 1], filler], 0)
-        bias = nt(R["uq"][...], spread_rows).astype(bf16)
+        spread_rows = jnp.concatenate([r_tmat[pair * 2], filler, r_tmat[pair * 2 + 1], filler], 0)
+        bias = nt(r_uq[...], spread_rows).astype(bf16)
         bias = jnp.concatenate([bias[:, :128], bias[:, 128:]], 0)
-        s = nt(jnp.concatenate([two_heads(q), bias], 1), jnp.concatenate([k, R["uk"][win]], 1))
+        s = nt(jnp.concatenate([two_heads(q), bias], 1), jnp.concatenate([k, r_uk[win]], 1))
         e = jnp.exp(s - jnp.max(s, -1, keepdims=True))
         probs = e * (1.0 / jnp.sum(e, -1, keepdims=True))
         heads[rows, spots[0]] = one_pair(nn(probs.astype(bf16), v)).astype(bf16)
@@ -741,13 +840,14 @@
         norm, _ = normalize(mid[rows, :])
         hid[rows, :] = (norm * (1.0 + mod[m + 4]) + mod[m + 3]).astype(bf16)
         dff[rows, :] = (mod[m + 5] * dy[rows, :].astype(f32)).astype(bf16)
-        ffn[rows, :] = jnp.zeros((ROWS, D), f32)
-        dh2[rows, :] = jnp.zeros((ROWS, D), f32)
+        ffn[rows, :] = jnp.zeros((at_once, D), f32)
+        dh2[rows, :] = jnp.zeros((at_once, D), f32)
 
     rows_loop(second_norm)
 
-    st = R["st"]
-    F = 512
+    st = r_st
+    subs = 1 if C <= 2 else 2
+    per, F = A // 2 // subs, D // 2 // subs
 
     def ffn_step(s):
         q, hf = s // 2, lax.rem(s, 2)
@@ -758,34 +858,46 @@
             weight(4 + 2 * q, su).wait()
             weight(5 + 2 * q, su + 1).wait()
 
-        up = wbuf[su, pl.ds(hf * (A // 2), A // 2)].reshape(F, D)
-        at = pl.ds(pl.multiple_of(hf * F, F), F)
-        down = wbuf[su + 1, :, :, :, :, at].reshape(D, F)
-        act, slope = gelu_parts(nt(hid[...], up))
-        act = act.astype(bf16)
-        ffn[...] += nt(act, down)
-        d_pre = (nn(dff[...], down) * slope).astype(bf16)
-        dh2[...] += nn(d_pre, up)
-
-        @pl.when(jnp.logical_and(hf == 0, q > 0))
-        def _():
-            scatter.flush(2 * q - 2, 0)
-            scatter.flush(2 * q - 1, 1)
-
-        st[0, pl.ds(hf * (A // 2), A // 2)] = tn(d_pre, hid[...]).astype(bf16).reshape(A // 2, B, 2, Rp, D)
-        st[1, :, :, :, :, at] = tn(dff[...], act).astype(bf16).reshape(A, B, 2, Rp, F)
+        def between():
+            @pl.when(jnp.logical_and(hf == 0, q > 0))
+            def _():
+                scatter.flush(2 * q - 2, 0)
+                scatter.flush(2 * q - 1, 1)
+
+            guard(s == 4, lambda: gather.slot(13, LOOKAHEAD))
+
+            @pl.when(s == 5)
+            def _():
+                gather.slot(14, LOOKAHEAD)
+                weight(10, 2).start()
+                weight(11, 3).start()
+
+            scatter.at(s, FFN_EARLY)
+
+        for sub in range(subs):
+            first = hf * (A // 2) + sub * per
+            up = wbuf[su, pl.ds(first, per)].reshape(F, D)
+            at = pl.ds(pl.multiple_of((hf * subs + sub) * F, F), F)
+            down = wbuf[su + 1, :, :, :, :, at].reshape(D, F)
+            act, slope = gelu_parts(nt(hid[...], up))
+            act = act.astype(bf16)
+            ffn[...] += nt(act, down)
+            d_pre = (nn(dff[...], down) * slope).astype(bf16)
+            dh2[...] += nn(d_pre, up)
+            if sub == 0:
+                between()
+            st[0, pl.ds(first, per)] = tn(d_pre, hid[...]).astype(bf16).reshape(per, B, 2, Rp, D)
+            st[1, :, :, :, :, at] = tn(dff[...], act).astype(bf16).reshape(A, B, 2, Rp, F)
 
         @pl.when(hf == 1)
         def _():
             scatter.sibling(2 * q, 0).start()
             scatter.sibling(2 * q + 1, 1).start()
 
-        gather.slot(10 + s, LOOKAHEAD)
-        guard(s == 4, lambda: scatter.tick(0))
-        guard(s == 5, lambda: scatter.tick(1))
-        guard(s == 7, lambda: scatter.tick(2))
-
-        @pl.when(jnp.logical_and(hf == 0, q < 3))
+        guard(s < 3, lambda: gather.slot(10 + s, LOOKAHEAD))
+        scatter.at(s, FFN_LATE)
+
+        @pl.when(jnp.logical_and(hf == 0, q < 2))
         def _():
             weight(6 + 2 * q, 2 - su).start()
             weight(7 + 2 * q, 3 - su).start()
@@ -805,17 +917,16 @@
         dmod[m + 3] += jnp.sum(dh, 0, keepdims=True)
         dmod[m + 4] += jnp.sum(dh * norm, 0, keepdims=True)
         dy[rows, :] = (mid[rows, :] + mod[m + 5] * fo).astype(bf16)
-        ffn[rows, :] = jnp.zeros((ROWS, D), f32)
+        ffn[rows, :] = jnp.zeros((at_once, D), f32)
         d_mid = dyr + normalize_back(dh * (1.0 + mod[m + 4]), norm, inv)
         dh2[rows, :] = d_mid
         dff[rows, :] = (mod[m + 2] * d_mid).astype(bf16)
 
-    rows_loop(second_back)
-    mixed_out = pltpu.make_async_copy(dy, R["mixed"], R["o_sem"].at[0])
+    rows_loop(second_back, SECOND_BACK)
+    mixed_out = pltpu.make_async_copy(dy, r_mixed, r_o_sem.at[0])
     mixed_out.start()
     scatter.flush(6, 0)
     scatter.flush(7, 1)
-    scatter.tick(3)
     weight(3, 0).wait()
 
     def out_back(a):
@@ -828,19 +939,18 @@
         st[0, a] = tn(dff[:, at], heads[...]).astype(bf16).reshape(B, 2, Rp, D)
         scatter.sibling_part(8, 0, a).start()
         hid[:, at] = nn(dff[...], wbuf[0, :, :, :, :, at].reshape(D, quarter)).astype(bf16)
+        scatter.at(a, OUT_BACK)
 
     loop(A, out_back)
-    scatter.tick(4)
-
     def attend_back(i):
         win, pair, rows, spots = head_refs(i)
         q = qkv[rows, spots[0]] * jnp.asarray(0.125, bf16)
         k, v = qkv[rows, spots[1]], qkv[rows, spots[2]]
         do = hid[rows, spots[0]]
         kk = two_heads(k)
-        bias = nn(R["uk"][win][:, :32], jnp.concatenate([R["tmat"][pair * 2], R["tmat"][pair * 2 + 1]], 1)).astype(bf16)
+        bias = nn(r_uk[win][:, :32], jnp.concatenate([r_tmat[pair * 2], r_tmat[pair * 2 + 1]], 1)).astype(bf16)
         bias = jnp.concatenate([bias[:, :128], bias[:, 128:]], 0)
-        query = jnp.concatenate([q, R["uq"][...]], 1)
+        query = jnp.concatenate([q, r_uq[...]], 1)
         s = nt(jnp.concatenate([kk, bias], 1), query)
         dp = nt(two_heads(v), do)
         probs, ds = [], []
@@ -859,17 +969,29 @@
         bias_part = jnp.concatenate([dk[:TOK, 128:], dk[TOK:, 128:]], 1)
         top = bias_part.astype(bf16)
         rest = (bias_part - top.astype(f32)).astype(bf16)
-        z = nn(R["ut"][...], top) + nn(R["ut"][...], rest)
+        z = nn(r_ut[...], top) + nn(r_ut[...], rest)
         for h in range(2):
-            R["zacc"][pl.ds(pl.multiple_of((pair * 2 + h) * 32, 32), 32), :] += z[:, h * 128 : (h + 1) * 128]
-        guard(i == 1, lambda: scatter.flush(8, 0))
-        guard(i == 3, lambda: scatter.tick(5))
-        guard(i == 7, lambda: scatter.tick(6))
-        guard(i == 11, lambda: scatter.tick(7))
-        guard(i == 15, lambda: scatter.tick(8))
+            r_zacc[pl.ds(pl.multiple_of((pair * 2 + h) * 32, 32), 32), :] += z[:, h * 128 : (h + 1) * 128]
+        scatter.at(i, ATTEND_BACK)
 
     loop(wins * pairs, attend_back)
-    make_hidden1()
+    table = jnp.zeros((HEADS, 128), f32)
+    for v in range(21):
+        zv = r_zacc[pl.ds(v, HEADS, stride=32), :]
+        top = zv.astype(bf16)
+        rest = (zv - top.astype(f32)).astype(bf16)
+        table = table + nn(top, r_selv[v]) + nn(rest, r_selv[v])
+    r_tb[...] = table
+    tabs = Spread(p, r_tb, r_tf, "abck", r_s_s.at[1], r_s_r.at[1], 0)
+    own_tb = pltpu.make_async_copy(r_tb, r_tf.at[p.a, p.b, p.k, p.c], r_own_sem.at[3])
+    own_tb.start()
+    tabs.start(0)
+    spread.drain()
+    own_tb.wait()
+    gather.drain()
+    make_hidden1(HIDDEN)
+    tabs.landed(0)
+    tabs.start(1)
     for t in range(3):
         weight(t, t + 1).wait()
 
@@ -883,18 +1005,21 @@
                     i += 1
         for t in range(3):
             scatter.sibling_part(9 + t, t, a).start()
+        scatter.at(a, QKV_GRAD)
 
     loop(A, qkv_grad)
-    scatter.flush(9, 0)
-    scatter.tick(9)
-    scatter.flush(10, 1)
-    scatter.flush(11, 2)
+    scatter.steps(part(9), begin(9), part(10), part(11))
+    tabs.landed(1)
+    tabs.start(2)
 
     def qkv_back(a):
         ffn[...] += nn(qkv[:, qkv_cols(a)], qkv_rows(a, 1))
+        scatter.at(a, QKV_BACK)
 
     loop(A, qkv_back)
-    scatter.tick(10)
+    tabs.landed(2)
+    tabs.start(3)
+    scatter.steps(*AFTER_QKV)
 
     def first_back(rows, m):
         norm, inv = normalize(x[rows, :].astype(f32))
@@ -903,51 +1028,42 @@
         dmod[m + 1] += jnp.sum(dh * norm, 0, keepdims=True)
         mid[rows, :] = dh2[rows, :] + normalize_back(dh * (1.0 + mod[m + 1]), norm, inv)
 
-    rows_loop(first_back)
-    scatter.tick(11)
-    gx_out = pltpu.make_async_copy(mid, R["gx"], R["o_sem"].at[1])
+    rows_loop(first_back, FIRST_BACK)
+    gx_out = pltpu.make_async_copy(mid, r_gx, r_o_sem.at[1])
     gx_out.start()
-    filler = (-wins * 6) % 16
-    stack = [dmod[i] for i in range(wins * 6)] + [jnp.zeros((1, D), f32)] * filler
-    R["dmb"][...] = jnp.concatenate(stack, 0).astype(bf16)
-    mods = Spread(p, R["dmb"], R["dmf"], "abck", R["s_s"].at[0], R["s_r"].at[0], 0)
-    own_dm = pltpu.make_async_copy(R["dmb"], R["dmf"].at[p.a, p.b, p.k, p.c], R["own_sem"].at[2])
-    own_dm.start()
-    mods.start(0)
-
-    lane = lax.broadcasted_iota(jnp.int32, (HEADS, 128), 1)
-    table = jnp.zeros((HEADS, 128), f32)
-    for win in range(wins):
-        table = jnp.where(lane == 128 - wins + win, R["ids"][win].astype(f32), table)
-    for v in range(21):
-        zv = R["zacc"][pl.ds(v, HEADS, stride=32), :]
-        top = zv.astype(bf16)
-        rest = (zv - top.astype(f32)).astype(bf16)
-        table = table + nn(top, R["selv"][v]) + nn(rest, R["selv"][v])
-    R["tb"][...] = table
-    tabs = Spread(p, R["tb"], R["tf"], "abck", R["s_s"].at[1], R["s_r"].at[1], 0)
-    own_tb = pltpu.make_async_copy(R["tb"], R["tf"].at[p.a, p.b, p.k, p.c], R["own_sem"].at[3])
-    own_tb.start()
-    tabs.start(0)
-    own_dm.wait()
-    own_tb.wait()
+    own_clip = [
+        (lax.broadcasted_iota(jnp.int32, (clips, piece), 0) == r_ids[win]).astype(f32) for win in range(wins)
+    ]
+    for w in range(2 * A * B):
+        for i in range(ncol // piece):
+            col = w * ncol + i * piece
+            got = 0.0
+            for win in range(wins):
+                row = dmod[win * 6 + col // D, :, col % D : col % D + piece].astype(bf16).astype(f32)
+                got = got + own_clip[win] * row
+            r_modf[w // (2 * B), (w // 2) % B, w % 2, :, i * piece : (i + 1) * piece] = got
+    fold = Fold(p, r_modf, [r_fold0, r_fold1, r_fold2, r_fold3], r_cl, r_s_s.at[0], r_s_r.at[0])
+    fold.start(0)
+    scatter.steps(*AFTER_FIRST)
+    scatter.drain(0, 9)
     for phase in (1, 2, 3):
-        for small in (mods, tabs):
-            small.landed(phase - 1)
-            small.start(phase)
-        if phase == 2:
-            scatter.tick(12)
-    for small in (mods, tabs):
-        small.landed(3)
-    scatter.tick(13)
-    scatter.tick(14)
+        fold.add(phase - 1)
+        fold.start(phase)
+        scatter.steps(*HOPS[phase - 1])
+    fold.add(3)
+    clip_out = pltpu.make_async_copy(r_cl, r_by_clip, r_own_sem.at[2])
+    clip_out.start()
+    tabs.landed(3)
+    scatter.steps(*ENDING)
+    clip_out.wait()
     mixed_out.wait()
     gx_out.wait()
-    gather.drain()
-    scatter.drain()
+    for r in (scatter.count - 2, scatter.count - 1):
+        scatter.result(r).wait()
+    scatter.drain(9, 3)
     for copy in mod_c():
         copy.wait_send()
-    for small in (spread, mods, tabs):
+    for small in (fold, tabs):
         small.drain()
 
 
@@ -959,13 +1075,12 @@
     D = 1024
     hbm = pl.BlockSpec(memory_space=pltpu.HBM)
     smem = pl.BlockSpec(memory_space=pltpu.SMEM)
-    dm_rows = -(-wins * 6 // 16) * 16
     out_shape = [
         jax.ShapeDtypeStruct((n, A, B, 2, Rp, D), bf16),
         jax.ShapeDtypeStruct((T, D), bf16),
         jax.ShapeDtypeStruct((T, D), f32),
         jax.ShapeDtypeStruct((n, Rp, K), f32),
-        jax.ShapeDtypeStruct((A, B, 2, C, dm_rows, D), bf16),
+        jax.ShapeDtypeStruct((clips, ncol), f32),
         jax.ShapeDtypeStruct((A, B, 2, C, HEADS, 128), f32),
     ]
     small = A - 1 + B - 1 + C - 1 + 1
@@ -989,12 +1104,16 @@
         pltpu.VMEM((HEADS, 32, 128), bf16),
         pltpu.VMEM((wins, TOK, 128), bf16),
         pltpu.VMEM((HEADS, 128), f32),
-        pltpu.VMEM((dm_rows, D), bf16),
+        pltpu.VMEM((1, A, B, clips, ncol), f32),
+        pltpu.VMEM((B - 1, A, clips, ncol), f32),
+        pltpu.VMEM((A - 1, clips, ncol), f32),
+        pltpu.VMEM((C - 1, clips, ncol), f32),
+        pltpu.VMEM((clips, ncol), f32),
         pltpu.VMEM((2, A, B, 2, Rp, D), bf16),
         pltpu.VMEM((n, A, B, Rp, D), bf16),
         *[pltpu.VMEM(shape, bf16) for shape in Scatter.box_shapes(dims, n, Rp, K)],
         pltpu.VMEM((2, Rp, K), f32),
-        dma((len(LOADED),)),
+        dma((10,)),
         dma((4,)),
         dma((4,)),
         dma((2,)),
@@ -1029,7 +1148,6 @@
     wins = micro * wl
     clips = cond.shape[0]
     n = lax.axis_index("narrow")
-    w = lax.axis_index("wide")
     ids = window_clip.reshape(wins)
     half = window_half.reshape(wins)
 
@@ -1066,19 +1184,12 @@
         jnp.asarray(selv, bf16),
         jnp.pad(table, ((0, 0), (0, 128 - table.shape[1]))),
     )
-    _, mixed, grad_x, rout, mod_grads, table_parts = run_step(dims, wins, ins)
+    _, mixed, grad_x, rout, by_clip, table_parts = run_step(dims, wins, ins)
 
     table_parts = table_parts.reshape(devices, HEADS, 128)
     grad_table = table_parts.sum(0)[:, : table.shape[1]]
-    all_ids = table_parts[:, 0, 128 - wins :].reshape(devices, micro, wl).transpose(1, 0, 2).reshape(-1)
-    ncol = ada.shape[1]
-    dm = mod_grads.reshape(devices, -1, width)[:, : wins * 6].reshape(devices, micro, wl, 6 * width)
-    dm = lax.dynamic_slice_in_dim(dm, w * ncol, ncol, 3)
-    dm = dm.transpose(1, 0, 2, 3).reshape(-1, ncol)
-    picked = (all_ids[:, None] == jnp.arange(clips, dtype=f32)[None, :]).astype(f32)
     cond_act = jax.nn.silu(cond.astype(f32)).astype(bf16)
     act_rows = lax.dynamic_slice_in_dim(cond_act, n * ada.shape[0], ada.shape[0], 1)
-    by_clip = jnp.einsum("wc,we->ce", picked, dm.astype(f32), precision=highest)
     grad_ada = jnp.einsum("cr,ce->re", act_rows.astype(f32), by_clip, precision=highest)
 
     ffn_r = rout[: 2 * pieces].reshape(pieces, 2, Rp, K)

time: 283 us -> 271 us (0.958)
  Pallas kernels: 263 us -> 252 us
    pallas_call x1, Pallas kernels: 263 us -> 252 us  [run_step(): pl.pallas_call(functools.partial(step_kernel, dims, wins), out_shape=out_...]
    unnamed x21 -> x20, local copies, waits for them, and re-layouts: 5.68 us -> 5.6 us
where the time goes in v4:
time: 271 us; the launch traced here: 270 us
  Pallas kernels  252 us (93%)
  local copies, waits for them, and re-layouts  13.2 us (5%)
    pallas_call x1, Pallas kernels, run_step(): pl.pallas_call(functools.partial(step_kernel, dims, wins), out_shape=out_...  252 us
    unnamed x20, local copies, waits for them, and re-layouts  5.6 us

profile of v4, /device:TPU:0, one launch (start us, length us, event | category | flops | bytes accessed | tf_op | source)
XLA Modules:
  0.0 270.2 jit_solution(7526046093240371745)
XLA Ops:
  0.6 0.0 copy-start.2
  0.6 1.5 reshape.56
  2.2 0.1 copy.42
  2.2 0.0 copy-start.4
  2.2 0.0 copy-start.6
  2.3 0.3 stack_reshape.7
  2.6 0.0 copy-done.2
  2.6 0.1 copy.30
  2.7 0.1 pad_maximum_fusion.1
  2.8 0.0 copy-start.7
  2.9 0.3 copy-done.4
  3.2 0.0 copy-done.6
  3.2 0.9 pad_maximum_fusion.refs_3_
  4.1 0.0 copy-done.7
  4.1 0.6 pad.4.refs_12_
  4.7 0.0 copy-start.5
  4.7 252.4 %block_step.1 = (bf16[12,4,2,2,64,1024]{5,4,3,2,1,0:T(8,128)(2,1)}, bf16[640,1024]{1,0:T(8,128)(2,1)}, f32[640,1024]{1,0:T(8,128)}, f32[12,64,512]{2,1,0:T(8,128...) custom-call(s32[2]{0:T(128)} %bitcast.63, s32[2]{0:T(128)} %bitcast.64, s32[8]{0:T(128)} %refs_2_.1, ...), custom_call_target="tpu_custom_call" | custom-call | tf_op jit(solution)/shard_map/block_step/pallas_call | solution.py:1130
  257.1 0.0 copy-start.1
  257.1 0.0 copy-done.5
  257.1 2.2 fusion
  259.3 1.8 slice.18
  261.1 0.0 copy-done.1
  261.1 0.7 slice_bitcast_fusion
  261.8 0.1 slice.20
  261.9 0.1 fusion.4
  262.0 1.0 copy.37
  263.0 0.2 reshape_squeeze.7
  263.2 0.0 copy-start.3
  263.2 0.7 copy.41
  263.9 1.6 reshape.64
  265.5 0.0 copy-start
  265.5 0.0 copy-done.3
  265.5 0.6 reduce_sum.9
  266.1 2.6 copy.45
  268.7 0.0 copy-done
  268.7 1.5 copy.46
  (2 shorter events, 0.0 us)
Async XLA Ops:
  0.6 2.0 copy-start.2
  2.2 0.9 copy-start.4
  2.2 0.9 copy-start.6
  2.8 1.3 copy-start.7
  4.7 252.4 %copy-start.5 = (bf16[8,1024]{1,0:T(8,128)(2,1)S(1)}, bf16[8,1024]{1,0:T(8,128)(2,1)}, u32[]{:S(2)}) copy-start(bf16[8,1024]{1,0:T(8,128)(2,1)} %refs_6_.1) | copy-start | bytes 49156
  257.1 4.0 %copy-start.1 = (f32[12,64,512]{2,1,0:T(8,128)S(1)}, f32[12,64,512]{2,1,0:T(8,128)}, u32[]{:S(2)}) copy-start(f32[12,64,512]{2,1,0:T(8,128)} %get-tuple-element.16) | copy-start | bytes 4718596
  263.2 2.3 copy-start.3
  265.5 3.3 %copy-start = (f32[640,1024]{1,0:T(8,128)S(1)}, f32[640,1024]{1,0:T(8,128)}, u32[]{:S(2)}) copy-start(f32[640,1024]{1,0:T(8,128)} %get-tuple-element.14) | copy-start | bytes 7864324

commit v5 on v4

--- a/solution.py
+++ b/solution.py
@@ -814,8 +814,8 @@
         e = jnp.exp(s - jnp.max(s, -1, keepdims=True))
         probs = e * (1.0 / jnp.sum(e, -1, keepdims=True))
         heads[rows, spots[0]] = one_pair(nn(probs.astype(bf16), v)).astype(bf16)
-        guard(i == 3, lambda: gather.slot(7, LOOKAHEAD))
-        guard(i == 9, lambda: gather.slot(8, LOOKAHEAD))
+        guard(i == 5, lambda: gather.slot(7, LOOKAHEAD))
+        guard(i == 12, lambda: gather.slot(8, LOOKAHEAD))
 
     loop(wins * pairs, attend)
     weight(4, 0).start()
@@ -833,8 +833,8 @@
             rows = slice(win * TOK, (win + 1) * TOK)
             mid[rows, at] = x[rows, at].astype(f32) + mod[win * 6 + 2, :, at] * got[rows]
 
+    loop(A, out_step)
     gather.slot(9, LOOKAHEAD)
-    loop(A, out_step)
 
     def second_norm(rows, m):
         norm, _ = normalize(mid[rows, :])

time: 271 us -> 269 us (level)
  no operation moved by 1% of the time
where the time goes in v5:
time: 269 us
  Pallas kernels  251 us (93%)
  local copies, waits for them, and re-layouts  13.2 us (5%)
    pallas_call x1, Pallas kernels, run_step(): pl.pallas_call(functools.partial(step_kernel, dims, wins), out_shape=out_...  251 us
    unnamed x20, local copies, waits for them, and re-layouts  5.6 us

profile of v5, /device:TPU:0, one launch (start us, length us, event | category | flops | bytes accessed | tf_op | source)
XLA Modules:
  0.0 269.1 jit_solution(3703541521283000633)
XLA Ops:
  0.6 0.0 copy-start.2
  0.6 1.5 reshape.56
  2.2 0.1 copy.42
  2.2 0.0 copy-start.4
  2.2 0.0 copy-start.6
  2.3 0.3 stack_reshape.7
  2.6 0.0 copy-done.2
  2.6 0.1 copy.30
  2.7 0.1 pad_maximum_fusion.1
  2.8 0.0 copy-start.7
  2.9 0.3 copy-done.4
  3.2 0.0 copy-done.6
  3.2 0.9 pad_maximum_fusion.refs_3_
  4.1 0.0 copy-done.7
  4.1 0.6 pad.4.refs_12_
  4.7 0.0 copy-start.5
  4.7 251.2 %block_step.1 = (bf16[12,4,2,2,64,1024]{5,4,3,2,1,0:T(8,128)(2,1)}, bf16[640,1024]{1,0:T(8,128)(2,1)}, f32[640,1024]{1,0:T(8,128)}, f32[12,64,512]{2,1,0:T(8,128...) custom-call(s32[2]{0:T(128)} %bitcast.63, s32[2]{0:T(128)} %bitcast.64, s32[8]{0:T(128)} %refs_2_.1, ...), custom_call_target="tpu_custom_call" | custom-call | tf_op jit(solution)/shard_map/block_step/pallas_call | solution.py:1130
  256.0 0.0 copy-start.1
  256.0 0.0 copy-done.5
  256.0 2.2 fusion
  258.2 1.8 slice.18
  260.0 0.0 copy-done.1
  260.0 0.7 slice_bitcast_fusion
  260.7 0.1 slice.20
  260.8 0.1 fusion.4
  260.9 1.0 copy.37
  261.9 0.2 reshape_squeeze.7
  262.1 0.0 copy-start.3
  262.1 0.7 copy.41
  262.8 1.6 reshape.64
  264.4 0.0 copy-start
  264.4 0.0 copy-done.3
  264.4 0.6 reduce_sum.9
  265.0 2.6 copy.45
  267.6 0.0 copy-done
  267.6 1.5 copy.46
  (2 shorter events, 0.0 us)
Async XLA Ops:
  0.6 2.0 copy-start.2
  2.2 0.9 copy-start.4
  2.2 0.9 copy-start.6
  2.8 1.3 copy-start.7
  4.7 251.2 %copy-start.5 = (bf16[8,1024]{1,0:T(8,128)(2,1)S(1)}, bf16[8,1024]{1,0:T(8,128)(2,1)}, u32[]{:S(2)}) copy-start(bf16[8,1024]{1,0:T(8,128)(2,1)} %refs_6_.1) | copy-start | bytes 49156
  256.0 4.0 %copy-start.1 = (f32[12,64,512]{2,1,0:T(8,128)S(1)}, f32[12,64,512]{2,1,0:T(8,128)}, u32[]{:S(2)}) copy-start(f32[12,64,512]{2,1,0:T(8,128)} %get-tuple-element.16) | copy-start | bytes 4718596
  262.1 2.3 copy-start.3
  264.4 3.3 %copy-start = (f32[640,1024]{1,0:T(8,128)S(1)}, f32[640,1024]{1,0:T(8,128)}, u32[]{:S(2)}) copy-start(f32[640,1024]{1,0:T(8,128)} %get-tuple-element.14) | copy-start | bytes 7864324
